TPU v7x, 512 devices: a whole 4x4x16 slice. The times are simulated.
512 devices in a mesh: ep: 64 (over y_lo, z, core), dp: 8 (over y_hi, x).
Axes of the slice: x: 4, y: 4 (y_hi: 2, y_lo: 2; y = y_hi * 2 + y_lo), z: 16, core: 2. Of those that a mesh axis runs over, the one named last changes fastest.
Arguments:
- out_grad: bfloat16 [65536, 3584], P(('ep', 'dp')), may hold values from -6 to 6
- expert_ids: int32 [65536, 2], P(('ep', 'dp')), may hold values from 0 to 63, all different within a row; in each aligned block of 128 rows (0 to 127, 128 to 255, ...) at most 6 rows name the same one
- combine: float32 [65536, 2], P(('ep', 'dp')), may hold values from 0.1 to 1
- router_logits: bfloat16 [65536, 384], P(('ep', 'dp')), may hold values from -16 to 250
- saved_hidden: bfloat16 [64, 3072, 1024], P('ep', 'dp'), may hold values from -6 to 6
- weight: bfloat16 [64, 1024, 3584], P('ep', 'dp'), may hold values from -0.1875 to 0.1875
- moment_one: bfloat16 [64, 1024, 3584], P('ep', 'dp'), may hold values from -6 to 6
- moment_two: bfloat16 [64, 1024, 3584], P('ep', 'dp'), may hold values from 2 to 40
- next_hidden: bfloat16 [64, 256, 1024], P('ep', 'dp'), may hold values from -6 to 6
Outputs:
- refreshed: bfloat16 [64, 256, 3584], P('ep', 'dp')
- router_grad: bfloat16 [65536, 384], P(('ep', 'dp'))
Inputs may be any that keep to these rules, and one draw needn't show every extreme that they name: `expert_ids`: each row names 2 different experts; among the 128 rows of one device no expert is named more than 6 times, a bound that some block reaches.
All inputs are finite; a program needn't handle non-finite values.
Results may differ from a plain program's by a relative error of at most 0.014.
Values may be sent and summed in bfloat16 or wider, within the bound.
No kernel may reach another device: no remote copies, remote signals or barrier semaphores. Data moves between devices by JAX's collectives and lax.ppermute only.
A program may use at most 64 MiB of HBM per device.

v0:
```python
import jax
import jax.numpy as jnp
from jax import lax
from jax.sharding import PartitionSpec as P

beta_one = 0.9
beta_two = 0.95
learn_rate = 0.2
decay_rate = 0.1
step_count = 100.0
adam_eps = 1e-08
zloss_coef = 0.25


def adamw(weight, first, second, gradient):
    first_new = beta_one * first.astype(jnp.float32) + (1.0 - beta_one) * gradient
    second_new = beta_two * second.astype(jnp.float32) + (1.0 - beta_two) * gradient * gradient
    first_hat = first_new / (1.0 - beta_one**step_count)
    second_hat = second_new / (1.0 - beta_two**step_count)
    current = weight.astype(jnp.float32)
    change = first_hat / (jnp.sqrt(second_hat) + adam_eps) + decay_rate * current
    return (current - learn_rate * change).astype(jnp.bfloat16)


def zloss_grad(logits):
    values = logits.astype(jnp.float32)
    row_max = jnp.max(values, axis=-1, keepdims=True)
    log_total = row_max + jnp.log(jnp.sum(jnp.exp(values - row_max), axis=-1, keepdims=True))
    probs = jnp.exp(values - log_total)
    return (zloss_coef * 2.0 * log_total * probs).astype(jnp.bfloat16)


def per_device(
    out_grad,
    expert_ids,
    combine,
    router_logits,
    saved_hidden,
    weight,
    moment_one,
    moment_two,
    next_hidden,
):
    experts_count = lax.axis_size("ep")
    replicas = lax.axis_size("dp")
    rows_total = saved_hidden.shape[1]
    capacity = rows_total // experts_count
    model_width = out_grad.shape[1]
    slab_rows = weight.shape[1]
    flat_ids = expert_ids.reshape(-1)
    onehot = (flat_ids[:, None] == jnp.arange(experts_count, dtype=jnp.int32)[None, :]).astype(
        jnp.int32
    )
    before = jnp.cumsum(onehot, axis=0) - onehot
    slot_index = jnp.sum(before * onehot, axis=1)
    target = flat_ids * capacity + slot_index
    scaled = (combine[:, :, None] * out_grad[:, None, :].astype(jnp.float32)).astype(jnp.bfloat16)
    scaled = scaled.reshape(-1, model_width)
    send_rows = jnp.zeros((rows_total, model_width), jnp.bfloat16).at[target].set(scaled)
    received = lax.all_to_all(
        send_rows.reshape(experts_count, capacity, model_width),
        "ep",
        split_axis=0,
        concat_axis=0,
        tiled=True,
    )
    received = received.reshape(rows_total, model_width)
    router_grad = zloss_grad(router_logits)
    partial_value = lax.dot_general(
        saved_hidden[0], received, (((0,), (0,)), ((), ())), preferred_element_type=jnp.float32
    )
    slabs = partial_value.astype(jnp.bfloat16).reshape(replicas, slab_rows, model_width)
    collected = lax.all_to_all(slabs, "dp", split_axis=0, concat_axis=0, tiled=True)
    gradient = jnp.sum(collected.astype(jnp.float32), axis=0)
    updated = adamw(weight[0], moment_one[0], moment_two[0], gradient)
    hidden_rows = next_hidden[0]
    refreshed = jnp.dot(
        hidden_rows,
        lax.all_gather(updated, "dp", axis=0, tiled=True),
        preferred_element_type=jnp.float32,
    )
    return (refreshed.astype(jnp.bfloat16)[None], router_grad)


def solution(mesh):
    in_specs = (
        P(("ep", "dp"), None),
        P(("ep", "dp"), None),
        P(("ep", "dp"), None),
        P(("ep", "dp"), None),
        P("ep", "dp", None),
        P("ep", "dp", None),
        P("ep", "dp", None),
        P("ep", "dp", None),
        P("ep", "dp", None),
    )
    out_specs = (P("ep", "dp", None), P(("ep", "dp"), None))
    return jax.shard_map(
        per_device, mesh=mesh, in_specs=in_specs, out_specs=out_specs, check_vma=False
    )
```

profile of v0, /device:TPU:1, one launch (start us, length us, event | category | flops | bytes accessed | tf_op | source)
XLA Modules:
  0.0 433.3 jit_solution(5571850612483556148)
XLA Ops:
  7.2 0.0 copy-start
  7.2 0.0 all-gather.2.cloned.1.call-start
  7.2 0.7 broadcast_multiply_fusion
  8.0 0.8 copy.12
  8.8 0.1 eq.25
  8.9 0.1 eq.29
  9.0 0.1 copy.11
  9.2 0.1 mul.100
  9.3 0.6 reduce-window.6
  9.9 0.2 slice_reduce_fusion
  10.2 3.9 mul.104
  14.1 0.0 copy-start.6
  14.1 5.7 %mul.105 = f32[256,3584]{1,0:T(8,128)} reshape(f32[128,2,3584]{2,1,0:T(2,128)} %mul.104) | data formatting | bytes 7340032 | tf_op jit(solution)/shard_map/mul | solution.py:57
  19.8 0.0 copy-done.6
  19.8 0.1 copy.15
  19.9 0.1 mul.102
  20.0 0.1 fusion.21
  20.1 5.5 %scatter_custom_fusion = bf16[384,3584]{1,0:T(8,128)(2,1)S(1)} fusion(s32[256]{0:T(256)S(1)} %bitcast.49, f32[256,3584]{1,0:T(8,128)} %mul.105, f32[256]{0:T(256)S(1)} %mul.102, bf16[]{:T(256)} %constant.16.clone.1), kind=kCustom, calls=%fused_computation.17 | custom fusion | flops 1835008 | bytes 6423554 | tf_op jit(solution)/shard_map/scatter | solution.py:59
  25.7 2.7 reshape.92
  28.4 179.6 %all_to_all.10 = bf16[64,6,3584]{2,1,0:T(8,128)(2,1)} all-to-all(bf16[64,6,3584]{2,1,0:T(8,128)(2,1)} %reshape.92), channel_id=1, replica_groups=mesh['ep'=64,'dp'=8] {'ep'}, dimensions={0} | all-to-all | bytes 5505024 | tf_op jit(solution)/shard_map/all_to_all | solution.py:60
  208.0 4.0 reshape.93
  212.0 0.0 copy-done
  212.0 4.3 convolution_convert_fusion
  216.2 87.3 %all_to_all.11 = bf16[8,128,3584]{2,1,0:T(8,128)(2,1)S(1)} all-to-all(bf16[8,128,3584]{2,1,0:T(8,128)(2,1)S(1)} %bitcast.47), channel_id=1, replica_groups=mesh['ep'=64,'dp'=8] {'dp'}, dimensions={0} | all-to-all | bytes 14680064 | tf_op jit(solution)/shard_map/all_to_all | solution.py:73
  303.6 0.0 copy-start.1
  303.6 0.0 copy-start.2
  303.6 0.0 copy-start.3
  303.6 1.1 convert_reduce_fusion
  304.6 0.1 copy-done.1
  304.7 0.3 copy-done.2
  305.0 0.3 copy-done.3
  305.3 0.0 copy-start.4
  305.3 0.0 copy-start.5
  305.3 2.5 fusion.3
  307.8 0.0 all-gather.2.cloned.1.call-update
  307.8 0.0 copy-done.4
  307.8 0.1 reduce_max.14
  307.9 0.2 fusion.15
  308.2 0.8 fusion.18
  308.9 112.4 %all-gather.2.cloned.1.call-done = bf16[1024,3584]{1,0:T(8,128)(2,1)} async-done(((bf16[128,3584]{1,0:T(8,128)(2,1)}), bf16[1024,3584]{1,0:T(8,128)(2,1)}) %all-gather.2.cloned.1.call-update) | async-done | bytes 7340048 | tf_op jit(solution)/shard_map/all_gather | solution.py:79
  421.3 0.0 copy-done.5
  421.3 5.1 %fusion = bf16[1,32,3584]{2,1,0:T(8,128)(2,1)} fusion(bf16[1024,3584]{1,0:T(8,128)(2,1)} %all-gather.2.cloned.1.call-done, bf16[1,32,1024]{2,1,0:T(8,128)(2,1)S(1)} %copy-done.5), kind=kOutput, calls=%fused_computation.4 | convolution fusion | flops 234995712 | bytes 7634944 | tf_op jit(solution)/shard_map/dot_general | solution.py:77
  (6 shorter events, 0.1 us)
Async XLA Ops:
  7.2 204.8 %copy-start = (bf16[1,384,1024]{2,1,0:T(8,128)(2,1)S(1)}, bf16[1,384,1024]{2,1,0:T(8,128)(2,1)}, u32[]{:S(2)}) copy-start(bf16[1,384,1024]{2,1,0:T(8,128)(2,1)} %param.13) | copy-start | bytes 2359300
  7.2 414.2 %all-gather.2.cloned.1.call-start = ((), (), s32[]{:S(2)}) async-start(), calls=%async_computation.2 | async-start | bytes 8257536 | tf_op jit(solution)/shard_map/all_gather | solution.py:79
  14.1 5.7 %copy-start.6 = (f32[128,2]{0,1:T(2,128)S(1)}, f32[128,2]{0,1:T(2,128)}, u32[]{:S(2)}) copy-start(f32[128,2]{0,1:T(2,128)} %param.11) | copy-start | bytes 3076
  303.6 1.2 copy-start.1
  303.6 1.5 copy-start.2
  303.6 1.7 copy-start.3
  305.3 2.5 copy-start.4
  305.3 116.0 %copy-start.5 = (bf16[1,32,1024]{2,1,0:T(8,128)(2,1)S(1)}, bf16[1,32,1024]{2,1,0:T(8,128)(2,1)}, u32[]{:S(2)}) copy-start(bf16[1,32,1024]{2,1,0:T(8,128)(2,1)} %param.17) | copy-start | bytes 196612
Sparse Core Ops, SparseCore 0:
  307.9 113.3 all-gather.1
where the time goes:
time: 434 us; the launch traced here: 433 us
  blocking collectives  267 us (62%)
  waiting for transfers between devices  112 us (26%)
  local copies, waits for them, and re-layouts  18.7 us (4%)
  between operations  14.1 us (3%)
  other arithmetic  11.7 us (3%)
  matrix products  9.39 us (2%)
    all_to_all x1, blocking collectives, per_device(): lax.all_to_all(send_rows.reshape(experts_count, capacity, model_width), '...  180 us
    all_gather x1, waiting for transfers between devices, per_device(): lax.all_gather(updated, 'dp', axis=0, tiled=True)  112 us
    all_to_all x1, blocking collectives, per_device(): lax.all_to_all(slabs, 'dp', split_axis=0, concat_axis=0, tiled=True)  87.3 us
    mul x3, local copies, waits for them, and re-layouts, per_device(): combine[:, :, None] * out_grad[:, None, :].astype(jnp.float32)  9.76 us
  transfers between devices with their start and end apart: 1, of which 1 were waited for; matrix products, arithmetic and copies ran while one was open for 0% of the time, Pallas kernels for 0%

commit v1 on v0

v1 whole, which is shorter than its diff:
```python
import jax
import jax.numpy as jnp
from jax import lax
from jax.experimental import pallas as pl
from jax.experimental.pallas import tpu as pltpu
from jax.sharding import PartitionSpec as P

beta_one = 0.9
beta_two = 0.95
learn_rate = 0.2
decay_rate = 0.1
step_count = 100.0
adam_eps = 1e-08
zloss_coef = 0.25

LANE = 128
HALF = 64
META = 8
WIDE = 3
SPAN = WIDE * LANE


def adamw(weight, first, second, gradient):
    first_new = beta_one * first.astype(jnp.float32) + (1.0 - beta_one) * gradient
    second_new = beta_two * second.astype(jnp.float32) + (1.0 - beta_two) * gradient * gradient
    first_hat = first_new / (1.0 - beta_one**step_count)
    second_hat = second_new / (1.0 - beta_two**step_count)
    current = weight.astype(jnp.float32)
    change = first_hat / (jnp.sqrt(second_hat) + adam_eps) + decay_rate * current
    return (current - learn_rate * change).astype(jnp.bfloat16)


def zloss_grad(logits):
    values = logits.astype(jnp.float32)
    row_max = jnp.max(values, axis=-1, keepdims=True)
    log_total = row_max + jnp.log(jnp.sum(jnp.exp(values - row_max), axis=-1, keepdims=True))
    probs = jnp.exp(values - log_total)
    return (zloss_coef * 2.0 * log_total * probs).astype(jnp.bfloat16)


def iota(shape, dim):
    return lax.broadcasted_iota(jnp.int32, shape, dim)


def digits(value, *bases):
    found = []
    for base in reversed(bases):
        above = jnp.floor((value.astype(jnp.float32) + 0.5) * (1.0 / base)).astype(jnp.int32)
        found.append(value - above * base)
        value = above
    return found[::-1]


def slots_of(ids):
    tokens = ids[0].shape[1]
    wide = [jnp.broadcast_to(row, (tokens, tokens)) for row in ids]
    tall = [jnp.transpose(mat) for mat in wide]
    earlier = iota((tokens, tokens), 0) < iota((tokens, tokens), 1)
    counts = []
    for mat in wide:
        hits = jnp.where(earlier & (tall[0] == mat), 1.0, 0.0)
        hits = hits + jnp.where(earlier & (tall[1] == mat), 1.0, 0.0)
        counts.append(jnp.sum(hits, axis=0, keepdims=True))
    return counts


def own_block(replicas):
    def body(own_ref, ids_ref, combine_ref, grad_ref, *message_refs):
        ids = ids_ref[...].astype(jnp.float32)
        combine = combine_ref[...]
        tokens = ids.shape[1]
        pieces = [ids[0:1], ids[1:2]]
        for k in range(2):
            rest = combine[k : k + 1]
            for _ in range(3):
                part = rest.astype(jnp.bfloat16).astype(jnp.float32)
                pieces.append(part)
                rest = rest - part
        meta = jnp.concatenate(pieces, axis=0).astype(jnp.bfloat16)
        meta = jnp.concatenate([meta] * WIDE, axis=1)
        for r in range(replicas):
            start = pl.multiple_of((own_ref[0] ^ r) * SPAN, LANE)
            message_refs[r][0:tokens, :] = grad_ref[:, pl.ds(start, SPAN)]
            message_refs[r][tokens : tokens + META, :] = meta

    return body


def own_tail(experts, capacity, replicas):
    tiles = replicas * HALF // LANE
    half = capacity // 2
    rows = half * replicas

    def body(ids_ref, combine_ref, grad_ref, tail_ref):
        ids = ids_ref[...].astype(jnp.float32)
        combine = combine_ref[...]
        tokens = ids.shape[1]
        id_rows = [ids[0:1], ids[1:2]]
        slots = slots_of(id_rows)
        target = [
            (id_rows[k] * capacity + slots[k]).astype(jnp.int32)[:, None, :] for k in range(2)
        ]
        shape = (experts, rows, tokens)
        place = iota(shape, 1)
        group = jnp.zeros(shape, jnp.int32)
        for c in range(1, half):
            group = group + jnp.where(place >= c * replicas, 1, 0)
        owner = (place - group * replicas)[:, :, 0:LANE]
        outs = []
        for side in range(2):
            key = iota(shape, 0) * capacity + group + side * half
            spread = jnp.where(key == target[0], combine[0:1][:, None, :], 0.0) + jnp.where(
                key == target[1], combine[1:2][:, None, :], 0.0
            )
            scale = jnp.sum(spread, axis=2, keepdims=True)
            chosen = jnp.where(spread > 0.0, 1.0, 0.0).reshape(experts * rows, tokens)
            picked = jnp.dot(
                chosen.astype(jnp.bfloat16), grad_ref[...], preferred_element_type=jnp.float32
            ).reshape(experts, rows, tiles * LANE)
            out = picked[:, :, 0:LANE]
            for t in range(1, tiles):
                out = jnp.where(owner >= 2 * t, picked[:, :, t * LANE : (t + 1) * LANE], out)
            outs.append((out * scale).reshape(experts * rows, LANE))
        odd = (owner & 1).reshape(experts * rows, LANE) == 1
        left = iota((experts * rows, LANE), 1) < HALF
        low = jnp.where(odd, pltpu.roll(outs[0], HALF, 1), outs[0])
        high = jnp.where(odd, outs[1], pltpu.roll(outs[1], HALF, 1))
        tail_ref[...] = jnp.where(left, low, high).astype(jnp.bfloat16)

    return body


def own_columns(experts, capacity, replicas, tokens, group):
    def body(*refs):
        message_refs, (send_ref, tokens_ref, target_ref, weight_ref) = (
            refs[:replicas],
            refs[replicas:],
        )
        for r in range(replicas):
            tokens_ref[r * tokens : (r + 1) * tokens, :] = message_refs[r][0:tokens, :]
            meta = message_refs[r][tokens : tokens + META, 0:tokens].astype(jnp.float32)
            id_rows = [meta[0:1], meta[1:2]]
            slots = slots_of(id_rows)
            for k in range(2):
                where = id_rows[k] * (replicas * capacity) + slots[k] + float(r * capacity)
                target_ref[k : k + 1, r * tokens : (r + 1) * tokens] = where.astype(jnp.int32)
                first = 2 + 3 * k
                weight_ref[k : k + 1, r * tokens : (r + 1) * tokens] = (
                    meta[first : first + 1] + meta[first + 1 : first + 2]
                ) + meta[first + 2 : first + 3]
        height = replicas * capacity
        rows = group * height

        def step(i, carry):
            key = iota((rows, replicas * tokens), 0) + i * rows
            spread = jnp.where(
                key == target_ref[0:1, :],
                weight_ref[0:1, :],
                jnp.where(key == target_ref[1:2, :], weight_ref[1:2, :], 0.0),
            )
            scale = jnp.sum(spread, axis=1, keepdims=True)
            chosen = jnp.where(spread > 0.0, 1.0, 0.0).astype(jnp.bfloat16)
            picked = jnp.dot(chosen, tokens_ref[...], preferred_element_type=jnp.float32)
            sent = (picked * scale).astype(jnp.bfloat16)
            for g in range(group):
                for t in range(WIDE):
                    start = pl.multiple_of((i * group + g) * (WIDE * height) + t * height, 16)
                    send_ref[pl.ds(start, height), :] = sent[
                        g * height : (g + 1) * height, t * LANE : (t + 1) * LANE
                    ]
            return carry

        lax.fori_loop(0, experts // group, step, 0)

    return body


def split_state(replicas):
    def body(own_ref, *refs):
        inputs, outputs = refs[:3], refs[3:]
        for a in range(3):
            rows = inputs[a].shape[0]
            height = WIDE * rows + rows // 2
            for r in range(replicas):
                owner = own_ref[0] ^ r
                for t in range(WIDE):
                    start = pl.multiple_of(owner * SPAN + t * LANE, LANE)
                    outputs[r][a * height + t * rows : a * height + (t + 1) * rows, :] = inputs[a][
                        :, pl.ds(start, LANE)
                    ]
                start = pl.multiple_of(replicas * SPAN + (owner >> 1) * LANE, LANE)
                tile = inputs[a][:, pl.ds(start, LANE)].astype(jnp.float32)
                turned = pltpu.roll(tile, HALF, 1)
                odd = jnp.broadcast_to(owner & 1, (rows // 2, LANE)) == 1
                low = jnp.where(odd, turned[: rows // 2], tile[: rows // 2])
                high = jnp.where(odd, tile[rows // 2 :], turned[rows // 2 :])
                left = iota((rows // 2, LANE), 1) < HALF
                outputs[r][a * height + WIDE * rows : (a + 1) * height, :] = jnp.where(
                    left, low, high
                ).astype(jnp.bfloat16)

    return body


def split_tail(replicas):
    def body(own_ref, tail_ref, *refs):
        outputs, buffer_ref = refs[:replicas], refs[replicas]
        buffer_ref[...] = tail_ref[...].astype(jnp.float32)
        count = outputs[0].shape[0]
        for r in range(replicas):
            owner = own_ref[0] ^ r
            outputs[r][...] = buffer_ref[pl.ds(owner, count, stride=replicas), :].astype(
                jnp.bfloat16
            )

    return body


def order_hidden(experts, capacity, replicas, group):
    rows = group * capacity
    total = replicas * rows

    def body(*refs):
        pieces, out_ref = refs[:replicas], refs[replicas]
        source, replica, slot = digits(iota((total, total), 0), group, replicas, capacity)
        wanted = replica * rows + source * capacity + slot
        move = jnp.where(iota((total, total), 1) == wanted, 1.0, 0.0).astype(jnp.bfloat16)

        def step(i, carry):
            start = pl.multiple_of(i * rows, 16)
            stacked = jnp.concatenate([ref[pl.ds(start, rows), :] for ref in pieces], axis=0)
            moved = jnp.dot(move, stacked, preferred_element_type=jnp.float32)
            place = pl.multiple_of(i * total, LANE)
            out_ref[:, pl.ds(place, total)] = jnp.transpose(moved).astype(jnp.bfloat16)
            return carry

        lax.fori_loop(0, experts // group, step, 0)

    return body


def tail_gradient(capacity, replicas):
    half = capacity // 2

    def body(*refs):
        hidden_refs, tail_refs, out_ref = refs[:replicas], refs[replicas : 2 * replicas], refs[-1]
        folded = tail_refs[0].shape[0]
        rows = 2 * folded
        source, side, slot = digits(iota((rows, folded), 0), rows // capacity, 2, half)
        move = jnp.where(iota((rows, folded), 1) == source * half + slot, 1.0, 0.0)
        move = move.astype(jnp.bfloat16)
        side = digits(iota((rows, LANE), 0), rows // capacity, 2, half)[1]
        for r in range(replicas):
            moved = jnp.dot(move, tail_refs[r][...], preferred_element_type=jnp.float32)
            moved = jnp.where(side == 1, pltpu.roll(moved, HALF, 1), moved).astype(jnp.bfloat16)
            part = lax.dot_general(
                hidden_refs[r][0:rows, :],
                moved,
                (((0,), (0,)), ((), ())),
                preferred_element_type=jnp.float32,
            )
            if r == 0:
                out_ref[...] = part
            else:
                out_ref[...] += part

    return body


def finish(experts, capacity, replicas):
    height = replicas * capacity

    def body(own_ref, wide_ref, hidden_ref, tail_ref, *refs):
        state_refs, next_refs = refs[:replicas], refs[replicas : 2 * replicas]
        out_refs = refs[2 * replicas : 3 * replicas]
        gradient_ref, updated_ref = refs[3 * replicas :]
        rows = experts * height
        received = wide_ref[...].reshape(experts, WIDE * height, LANE)
        tiles = [
            received[:, t * height : (t + 1) * height, :].reshape(rows, LANE) for t in range(WIDE)
        ]
        gradient_ref[...] = jnp.dot(
            hidden_ref[...], jnp.concatenate(tiles, axis=1), preferred_element_type=jnp.float32
        )
        slab = state_refs[0].shape[0] * 2 // (3 * (2 * WIDE + 1))
        part = WIDE * slab + slab // 2
        for r in range(replicas):
            start = pl.multiple_of((own_ref[0] ^ r) * slab, slab)
            for t in range(WIDE):
                state = [
                    state_refs[r][a * part + t * slab : a * part + (t + 1) * slab, :]
                    for a in range(3)
                ]
                gradient = gradient_ref[pl.ds(start, slab), t * LANE : (t + 1) * LANE]
                updated_ref[pl.ds(start, slab), t * LANE : (t + 1) * LANE] = adamw(
                    *state, gradient
                )
            state = []
            for a in range(3):
                folded = state_refs[r][a * part + WIDE * slab : (a + 1) * part, :]
                folded = folded.astype(jnp.float32)
                state.append(jnp.concatenate([folded, pltpu.roll(folded, HALF, 1)], axis=0))
            updated_ref[pl.ds(start, slab), SPAN : SPAN + LANE] = adamw(
                *state, tail_ref[pl.ds(start, slab), :]
            )
        for r in range(replicas):
            out_refs[r][...] = jnp.dot(
                next_refs[r][...], updated_ref[...], preferred_element_type=jnp.float32
            ).astype(jnp.bfloat16)

    return body


def join_columns(replicas):
    def body(own_ref, *refs):
        pieces, out_ref = refs[:replicas], refs[replicas]
        rows = pieces[0].shape[0]
        left = iota((rows, LANE), 1) < HALF
        for r in range(replicas):
            owner = own_ref[0] ^ r
            start = pl.multiple_of(owner * SPAN, LANE)
            out_ref[:, pl.ds(start, SPAN)] = pieces[r][:, 0:SPAN]
            if r % 2 == 0:
                pair = [pieces[r + s][:, SPAN : SPAN + LANE].astype(jnp.float32) for s in (0, 1)]
                odd = jnp.broadcast_to(owner & 1, (rows, LANE)) == 1
                low = jnp.where(odd, pair[1], pair[0])
                high = pltpu.roll(jnp.where(odd, pair[0], pair[1]), HALF, 1)
                start = pl.multiple_of(replicas * SPAN + (owner >> 1) * LANE, LANE)
                out_ref[:, pl.ds(start, LANE)] = jnp.where(left, low, high).astype(jnp.bfloat16)

    return body


def per_device(
    out_grad,
    expert_ids,
    combine,
    router_logits,
    saved_hidden,
    weight,
    moment_one,
    moment_two,
    next_hidden,
    interpret=False,
):
    experts = lax.axis_size("ep")
    replicas = lax.axis_size("dp")
    rows_total = saved_hidden.shape[1]
    capacity = rows_total // experts
    tokens = out_grad.shape[0]
    slab_rows = weight.shape[1]
    ff_width = saved_hidden.shape[2]
    next_rows = next_hidden.shape[1]
    main = replicas * SPAN
    tail_rows = replicas * capacity // 2
    state_rows = 3 * (WIDE * slab_rows + slab_rows // 2)
    vmem = pl.BlockSpec(memory_space=pltpu.VMEM)
    smem = pl.BlockSpec(memory_space=pltpu.SMEM)
    own = lax.axis_index("dp").astype(jnp.int32).reshape(1)

    def call(body, ins, outs, scratch=(), scalar=False):
        shapes = [jax.ShapeDtypeStruct(shape, dtype) for shape, dtype in outs]
        single = len(shapes) == 1
        specs = [vmem] * len(ins)
        if scalar:
            specs, ins = [smem] + specs, [own] + list(ins)
        return pl.pallas_call(
            body,
            out_shape=shapes[0] if single else tuple(shapes),
            in_specs=specs,
            out_specs=vmem if single else (vmem,) * len(shapes),
            scratch_shapes=list(scratch),
            interpret=interpret,
        )(*ins)

    def exchange(pieces):
        return [pieces[0]] + [
            lax.ppermute(pieces[r], "dp", [(i, i ^ r) for i in range(replicas)])
            for r in range(1, replicas)
        ]

    def swap(value, parts):
        value = value.reshape(parts, value.shape[0] // parts, value.shape[1])
        value = lax.all_to_all(value, "ep", split_axis=0, concat_axis=0, tiled=True)
        return value.reshape(-1, value.shape[2])

    half16 = jnp.bfloat16
    ids_wide, combine_wide = expert_ids.T, combine.T
    message = call(
        own_block(replicas),
        [ids_wide, combine_wide, out_grad],
        [((tokens + META, SPAN), half16)] * replicas,
        scalar=True,
    )
    message = exchange(message)
    tail = call(
        own_tail(experts, capacity, replicas),
        [ids_wide, combine_wide, out_grad[:, main:]],
        [((experts * tail_rows, LANE), half16)],
    )
    tail = swap(tail, experts)
    send = call(
        own_columns(experts, capacity, replicas, tokens, 8),
        message,
        [((experts * WIDE * replicas * capacity, LANE), half16)],
        [
            pltpu.VMEM((replicas * tokens, SPAN), jnp.bfloat16),
            pltpu.VMEM((2, replicas * tokens), jnp.int32),
            pltpu.VMEM((2, replicas * tokens), jnp.float32),
        ],
    )
    wide = swap(send, experts)

    tail = call(
        split_tail(replicas),
        [tail],
        [((experts * capacity // 2, LANE), half16)] * replicas,
        [pltpu.VMEM((experts * tail_rows, LANE), jnp.float32)],
        scalar=True,
    )
    tail = exchange(tail)
    state = call(
        split_state(replicas),
        [weight[0], moment_one[0], moment_two[0]],
        [((state_rows, LANE), half16)] * replicas,
        scalar=True,
    )
    state = exchange(state)
    hidden = exchange([saved_hidden[0]] * replicas)
    following = exchange([next_hidden[0]] * replicas)

    gradient_tail = call(
        tail_gradient(capacity, replicas),
        hidden + tail,
        [((ff_width, LANE), jnp.float32)],
    )
    ordered = call(
        order_hidden(experts, capacity, replicas, 8),
        hidden,
        [((ff_width, replicas * rows_total), half16)],
    )
    result = call(
        finish(experts, capacity, replicas),
        [wide, ordered, gradient_tail] + state + following,
        [((next_rows, SPAN + LANE), half16)] * replicas,
        [
            pltpu.VMEM((ff_width, SPAN), jnp.float32),
            pltpu.VMEM((ff_width, SPAN + LANE), jnp.bfloat16),
        ],
        scalar=True,
    )
    result = exchange(result)
    refreshed = call(
        join_columns(replicas),
        result,
        [((next_rows, out_grad.shape[1]), half16)],
        scalar=True,
    )
    return (refreshed[None], zloss_grad(router_logits))


def solution(mesh):
    in_specs = (
        P(("ep", "dp"), None),
        P(("ep", "dp"), None),
        P(("ep", "dp"), None),
        P(("ep", "dp"), None),
        P("ep", "dp", None),
        P("ep", "dp", None),
        P("ep", "dp", None),
        P("ep", "dp", None),
        P("ep", "dp", None),
    )
    out_specs = (P("ep", "dp", None), P(("ep", "dp"), None))
    return jax.shard_map(
        per_device, mesh=mesh, in_specs=in_specs, out_specs=out_specs, check_vma=False
    )
```

time: 434 us -> 339 us (0.78)
  the two profiles are of different devices: /device:TPU:1 before, /device:TPU:96 now
where the time goes in v1:
time: 339 us; the launch traced here: 337 us
  starting transfers between devices  186 us (55%)
  waiting for transfers between devices  90.8 us (27%)
  Pallas kernels  51.4 us (15%)
  local copies, waits for them, and re-layouts  5.82 us (2%)
    ppermute x42, starting transfers between devices, exchange(): lax.ppermute(pieces[r], 'dp', [(i, i ^ r) for i in range(replicas)])  158 us
    ppermute x42, waiting for transfers between devices, exchange(): lax.ppermute(pieces[r], 'dp', [(i, i ^ r) for i in range(replicas)])  90.8 us
    pallas_call x9, Pallas kernels, call(): pl.pallas_call(body, out_shape=shapes[0] if single else tuple(shapes), in...  51.4 us
    all_to_all x2, starting transfers between devices, swap(): value = lax.all_to_all(value, 'ep', split_axis=0, concat_axis=0, tiled=True)  28.9 us
  transfers between devices with their start and end apart: 44, of which 12 were waited for; matrix products, arithmetic and copies ran while one was open for 0% of the time, Pallas kernels for 10%

profile of v1, /device:TPU:96, one launch (start us, length us, event | category | flops | bytes accessed | tf_op | source)
XLA Modules:
  0.0 337.2 jit_solution(4993519121505151971)
XLA Ops:
  2.2 2.9 shard_map.107
  5.1 15.9 %all-to-all-start.1 = ((bf16[64,24,128]{2,1,0:T(8,128)(2,1)}), bf16[64,24,128]{2,1,0:T(8,128)(2,1)S(1)}, u32[]{:S(2)}, u32[]{:S(2)}) async-start(bf16[64,24,128]{2,1,0:T(8,128)(2,1)} %bitcast.25), calls=%async_computation.1 | async-start | bytes 786432 | tf_op jit(solution)/shard_map/all_to_all | solution.py:384
  21.0 2.2 shard_map.104
  23.2 3.4 %collective-permute-start = (bf16[136,384]{1,0:T(8,128)(2,1)}, bf16[136,384]{1,0:T(8,128)(2,1)S(1)}, u32[]{:S(2)}, u32[]{:S(2)}) collective-permute-start(bf16[136,384]{1,0:T(8,128)(2,1)} %get-tuple-element.35), channel_id=1, source_target_pairs={{0,1},{1,0},{2,3},{3,2},{4,5},{5,4},{6,7},{7,6},{8,9},{9,8},{10,11... | collective-permute-start | bytes 313352 | tf_op jit(solution)/shard_map/ppermute | solution.py:378
  26.6 4.6 %collective-permute-start.1 = (bf16[136,384]{1,0:T(8,128)(2,1)}, bf16[136,384]{1,0:T(8,128)(2,1)S(1)}, u32[]{:S(2)}, u32[]{:S(2)}) collective-permute-start(bf16[136,384]{1,0:T(8,128)(2,1)} %get-tuple-element.36), channel_id=1, source_target_pairs={{0,2},{1,3},{2,0},{3,1},{4,6},{5,7},{6,4},{7,5},{8,10},{9,11},{10,... | collective-permute-start | bytes 313352 | tf_op jit(solution)/shard_map/ppermute | solution.py:378
  31.2 2.4 collective-permute-start.2
  33.6 4.8 %collective-permute-start.3 = (bf16[136,384]{1,0:T(8,128)(2,1)}, bf16[136,384]{1,0:T(8,128)(2,1)S(1)}, u32[]{:S(2)}, u32[]{:S(2)}) collective-permute-start(bf16[136,384]{1,0:T(8,128)(2,1)} %get-tuple-element.38), channel_id=1, source_target_pairs={{0,4},{1,5},{2,6},{3,7},{4,0},{5,1},{6,2},{7,3},{8,12},{9,13},{10,... | collective-permute-start | bytes 313352 | tf_op jit(solution)/shard_map/ppermute | solution.py:378
  38.4 2.3 collective-permute-start.4
  40.7 8.2 %collective-permute-start.5 = (bf16[136,384]{1,0:T(8,128)(2,1)}, bf16[136,384]{1,0:T(8,128)(2,1)S(1)}, u32[]{:S(2)}, u32[]{:S(2)}) collective-permute-start(bf16[136,384]{1,0:T(8,128)(2,1)} %get-tuple-element.40), channel_id=1, source_target_pairs={{0,6},{1,7},{2,4},{3,5},{4,2},{5,3},{6,0},{7,1},{8,14},{9,15},{10,... | collective-permute-start | bytes 313352 | tf_op jit(solution)/shard_map/ppermute | solution.py:378
  48.9 2.5 collective-permute-start.6
  52.0 7.3 %collective-permute-done.6.refs_7_ = bf16[136,384]{1,0:T(8,128)(2,1)S(1)} collective-permute-done((bf16[136,384]{1,0:T(8,128)(2,1)}, bf16[136,384]{1,0:T(8,128)(2,1)S(1)}, u32[]{:S(2)}, u32[]{:S(2)}) %collective-permute-start.6) | collective-permute-done | bytes 104480 | tf_op jit(solution)/shard_map/ppermute | solution.py:378
  59.9 8.1 %shard_map.105 = bf16[9216,128]{1,0:T(8,128)(2,1)} custom-call(bf16[136,384]{1,0:T(8,128)(2,1)} %get-tuple-element.34.refs_0_, bf16[136,384]{1,0:T(8,128)(2,1)} %copy-done.8, bf16[136,384]{1,0:T(8,128)(2,1)} %copy-done.9, bf16[136,384]{1,0:T(8,128)(2,1)} %copy-done.10, bf16[136,384]{1,0:T(8,128)(2,1)} %copy-done.11, bf16[136,384]{1,0:T(8,128)(2,1)} %copy-done.12, ...), custom_call_target="tpu_custom_call" | custom-call | tf_op jit(solution)/shard_map/pallas_call | solution.py:367
  68.8 13.1 %all-to-all-start = ((bf16[64,144,128]{2,1,0:T(8,128)(2,1)}), bf16[64,144,128]{2,1,0:T(8,128)(2,1)S(1)}, u32[]{:S(2)}, u32[]{:S(2)}) async-start(bf16[64,144,128]{2,1,0:T(8,128)(2,1)} %bitcast.13), calls=%async_computation | async-start | bytes 4718592 | tf_op jit(solution)/shard_map/all_to_all | solution.py:384
  81.9 3.8 %collective-permute-start.13 = (bf16[384,1024]{1,0:T(8,128)(2,1)S(1)}, bf16[384,1024]{1,0:T(8,128)(2,1)}, u32[]{:S(2)}, u32[]{:S(2)}) collective-permute-start(bf16[384,1024]{1,0:T(8,128)(2,1)S(1)} %bitcast.17), channel_id=1, source_target_pairs={{0,7},{1,6},{2,5},{3,4},{4,3},{5,2},{6,1},{7,0},{8,15},{9,14},{10,... | collective-permute-start | bytes 2359304 | tf_op jit(solution)/shard_map/ppermute | solution.py:378
  85.7 2.4 collective-permute-start.12
  88.1 5.3 %collective-permute-start.34 = (bf16[32,1024]{1,0:T(8,128)(2,1)}, bf16[32,1024]{1,0:T(8,128)(2,1)S(1)}, u32[]{:S(2)}, u32[]{:S(2)}) collective-permute-start(bf16[32,1024]{1,0:T(8,128)(2,1)} %bitcast.30), channel_id=1, source_target_pairs={{0,7},{1,6},{2,5},{3,4},{4,3},{5,2},{6,1},{7,0},{8,15},{9,14},{10,... | collective-permute-start | bytes 196616 | tf_op jit(solution)/shard_map/ppermute | solution.py:378
  93.4 7.2 %collective-permute-start.33 = (bf16[32,1024]{1,0:T(8,128)(2,1)}, bf16[32,1024]{1,0:T(8,128)(2,1)S(1)}, u32[]{:S(2)}, u32[]{:S(2)}) collective-permute-start(bf16[32,1024]{1,0:T(8,128)(2,1)} %bitcast.31), channel_id=1, source_target_pairs={{0,6},{1,7},{2,4},{3,5},{4,2},{5,3},{6,0},{7,1},{8,14},{9,15},{10,... | collective-permute-start | bytes 196616 | tf_op jit(solution)/shard_map/ppermute | solution.py:378
  100.7 3.9 %shard_map.110 = (bf16[1344,128]{1,0:T(8,128)(2,1)}, bf16[1344,128]{1,0:T(8,128)(2,1)}, bf16[1344,128]{1,0:T(8,128)(2,1)}, bf16[1344,128]{1,0:T(8,128)(2,1)}, bf...) custom-call(s32[1]{0:T(128)} %bitcast.own_ref, ...), custom_call_target="tpu_custom_call" | custom-call | tf_op jit(solution)/shard_map/pallas_call | solution.py:367
  104.5 1.9 collective-permute-start.21
  106.4 34.8 %collective-permute-done.34.refs_15_ = bf16[32,1024]{1,0:T(8,128)(2,1)S(1)} collective-permute-done((bf16[32,1024]{1,0:T(8,128)(2,1)}, bf16[32,1024]{1,0:T(8,128)(2,1)S(1)}, u32[]{:S(2)}, u32[]{:S(2)}) %collective-permute-start.34) | collective-permute-done | bytes 65568 | tf_op jit(solution)/shard_map/ppermute | solution.py:378
  141.3 1.9 collective-permute-start.32
  143.2 5.1 %collective-permute-start.22 = (bf16[1344,128]{1,0:T(8,128)(2,1)}, bf16[1344,128]{1,0:T(8,128)(2,1)S(1)}, u32[]{:S(2)}, u32[]{:S(2)}) collective-permute-start(bf16[1344,128]{1,0:T(8,128)(2,1)} %get-tuple-element.52), channel_id=1, source_target_pairs={{0,2},{1,3},{2,0},{3,1},{4,6},{5,7},{6,4},{7,5},{8,10},{9,11},{10,... | collective-permute-start | bytes 1032200 | tf_op jit(solution)/shard_map/ppermute | solution.py:378
  148.4 2.1 collective-permute-done.32.refs_13_
  150.4 3.8 %collective-permute-start.31 = (bf16[32,1024]{1,0:T(8,128)(2,1)S(1)}, bf16[32,1024]{1,0:T(8,128)(2,1)S(1)}, u32[]{:S(2)}, u32[]{:S(2)}) collective-permute-start(bf16[32,1024]{1,0:T(8,128)(2,1)S(1)} %bitcast.34), channel_id=1, source_target_pairs={{0,4},{1,5},{2,6},{3,7},{4,0},{5,1},{6,2},{7,3},{8,12},{9,13},{10,... | collective-permute-start | bytes 196616 | tf_op jit(solution)/shard_map/ppermute | solution.py:378
  154.2 4.2 %collective-permute-done.31.refs_12_ = bf16[32,1024]{1,0:T(8,128)(2,1)S(1)} collective-permute-done((bf16[32,1024]{1,0:T(8,128)(2,1)S(1)}, bf16[32,1024]{1,0:T(8,128)(2,1)S(1)}, u32[]{:S(2)}, u32[]{:S(2)}) %collective-permute-start.31) | collective-permute-done | bytes 65568 | tf_op jit(solution)/shard_map/ppermute | solution.py:378
  158.5 2.5 collective-permute-start.30
  161.0 4.8 %collective-permute-done.30.refs_11_ = bf16[32,1024]{1,0:T(8,128)(2,1)S(1)} collective-permute-done((bf16[32,1024]{1,0:T(8,128)(2,1)S(1)}, bf16[32,1024]{1,0:T(8,128)(2,1)S(1)}, u32[]{:S(2)}, u32[]{:S(2)}) %collective-permute-start.30) | collective-permute-done | bytes 65568 | tf_op jit(solution)/shard_map/ppermute | solution.py:378
  165.8 1.9 collective-permute-start.29
  167.8 5.7 %collective-permute-done.29.refs_10_ = bf16[32,1024]{1,0:T(8,128)(2,1)S(1)} collective-permute-done((bf16[32,1024]{1,0:T(8,128)(2,1)S(1)}, bf16[32,1024]{1,0:T(8,128)(2,1)S(1)}, u32[]{:S(2)}, u32[]{:S(2)}) %collective-permute-start.29) | collective-permute-done | bytes 65568 | tf_op jit(solution)/shard_map/ppermute | solution.py:378
  173.5 1.9 collective-permute-start.28
  175.4 4.6 %collective-permute-done.28.refs_9_ = bf16[32,1024]{1,0:T(8,128)(2,1)S(1)} collective-permute-done((bf16[32,1024]{1,0:T(8,128)(2,1)S(1)}, bf16[32,1024]{1,0:T(8,128)(2,1)S(1)}, u32[]{:S(2)}, u32[]{:S(2)}) %collective-permute-start.28) | collective-permute-done | bytes 65568 | tf_op jit(solution)/shard_map/ppermute | solution.py:378
  180.0 3.6 %collective-permute-start.11 = (bf16[384,1024]{1,0:T(8,128)(2,1)S(1)}, bf16[384,1024]{1,0:T(8,128)(2,1)}, u32[]{:S(2)}, u32[]{:S(2)}) collective-permute-start(bf16[384,1024]{1,0:T(8,128)(2,1)S(1)} %bitcast.19), channel_id=1, source_target_pairs={{0,5},{1,4},{2,7},{3,6},{4,1},{5,0},{6,3},{7,2},{8,13},{9,12},{10,... | collective-permute-start | bytes 2359304 | tf_op jit(solution)/shard_map/ppermute | solution.py:378
  183.6 3.0 collective-permute-start.10
  186.7 2.4 collective-permute-start.9
  189.0 5.8 %collective-permute-start.8 = (bf16[384,1024]{1,0:T(8,128)(2,1)S(1)}, bf16[384,1024]{1,0:T(8,128)(2,1)}, u32[]{:S(2)}, u32[]{:S(2)}) collective-permute-start(bf16[384,1024]{1,0:T(8,128)(2,1)S(1)} %bitcast.22), channel_id=1, source_target_pairs={{0,2},{1,3},{2,0},{3,1},{4,6},{5,7},{6,4},{7,5},{8,10},{9,11},{10,... | collective-permute-start | bytes 2359304 | tf_op jit(solution)/shard_map/ppermute | solution.py:378
  194.8 1.9 collective-permute-start.7
  196.8 2.0 shard_map.108
  198.8 6.6 %collective-permute-done.11.refs_5_ = bf16[384,1024]{1,0:T(8,128)(2,1)} collective-permute-done((bf16[384,1024]{1,0:T(8,128)(2,1)S(1)}, bf16[384,1024]{1,0:T(8,128)(2,1)}, u32[]{:S(2)}, u32[]{:S(2)}) %collective-permute-start.11) | collective-permute-done | bytes 786464 | tf_op jit(solution)/shard_map/ppermute | solution.py:378
  205.4 1.9 collective-permute-start.14
  207.3 8.2 %collective-permute-done.10.refs_4_ = bf16[384,1024]{1,0:T(8,128)(2,1)} collective-permute-done((bf16[384,1024]{1,0:T(8,128)(2,1)S(1)}, bf16[384,1024]{1,0:T(8,128)(2,1)}, u32[]{:S(2)}, u32[]{:S(2)}) %collective-permute-start.10) | collective-permute-done | bytes 786464 | tf_op jit(solution)/shard_map/ppermute | solution.py:378
  215.4 2.6 collective-permute-start.15
  218.1 4.1 %collective-permute-start.16 = (bf16[192,128]{1,0:T(8,128)(2,1)}, bf16[192,128]{1,0:T(8,128)(2,1)S(1)}, u32[]{:S(2)}, u32[]{:S(2)}) collective-permute-start(bf16[192,128]{1,0:T(8,128)(2,1)} %get-tuple-element.45), channel_id=1, source_target_pairs={{0,3},{1,2},{2,1},{3,0},{4,7},{5,6},{6,5},{7,4},{8,11},{9,10},{10,... | collective-permute-start | bytes 147464 | tf_op jit(solution)/shard_map/ppermute | solution.py:378
  222.1 3.5 %collective-permute-start.17 = (bf16[192,128]{1,0:T(8,128)(2,1)}, bf16[192,128]{1,0:T(8,128)(2,1)S(1)}, u32[]{:S(2)}, u32[]{:S(2)}) collective-permute-start(bf16[192,128]{1,0:T(8,128)(2,1)} %get-tuple-element.46), channel_id=1, source_target_pairs={{0,4},{1,5},{2,6},{3,7},{4,0},{5,1},{6,2},{7,3},{8,12},{9,13},{10,... | collective-permute-start | bytes 147464 | tf_op jit(solution)/shard_map/ppermute | solution.py:378
  225.6 7.1 %collective-permute-done.7.refs_1_ = bf16[384,1024]{1,0:T(8,128)(2,1)} collective-permute-done((bf16[384,1024]{1,0:T(8,128)(2,1)S(1)}, bf16[384,1024]{1,0:T(8,128)(2,1)}, u32[]{:S(2)}, u32[]{:S(2)}) %collective-permute-start.7) | collective-permute-done | bytes 786464 | tf_op jit(solution)/shard_map/ppermute | solution.py:378
  232.8 3.3 collective-permute-start.18
  236.1 5.5 %collective-permute-start.19 = (bf16[192,128]{1,0:T(8,128)(2,1)}, bf16[192,128]{1,0:T(8,128)(2,1)S(1)}, u32[]{:S(2)}, u32[]{:S(2)}) collective-permute-start(bf16[192,128]{1,0:T(8,128)(2,1)} %get-tuple-element.48), channel_id=1, source_target_pairs={{0,6},{1,7},{2,4},{3,5},{4,2},{5,3},{6,0},{7,1},{8,14},{9,15},{10,... | collective-permute-start | bytes 147464 | tf_op jit(solution)/shard_map/ppermute | solution.py:378
  241.6 5.2 %collective-permute-start.20 = (bf16[192,128]{1,0:T(8,128)(2,1)}, bf16[192,128]{1,0:T(8,128)(2,1)}, u32[]{:S(2)}, u32[]{:S(2)}) collective-permute-start(bf16[192,128]{1,0:T(8,128)(2,1)} %get-tuple-element.49), channel_id=1, source_target_pairs={{0,7},{1,6},{2,5},{3,4},{4,3},{5,2},{6,1},{7,0},{8,15},{9,14},{10,... | collective-permute-start | bytes 147464 | tf_op jit(solution)/shard_map/ppermute | solution.py:378
  246.8 3.1 collective-permute-start.23
  250.5 3.6 %collective-permute-start.24 = (bf16[1344,128]{1,0:T(8,128)(2,1)}, bf16[1344,128]{1,0:T(8,128)(2,1)S(1)}, u32[]{:S(2)}, u32[]{:S(2)}) collective-permute-start(bf16[1344,128]{1,0:T(8,128)(2,1)} %get-tuple-element.54), channel_id=1, source_target_pairs={{0,4},{1,5},{2,6},{3,7},{4,0},{5,1},{6,2},{7,3},{8,12},{9,13},{10,... | collective-permute-start | bytes 1032200 | tf_op jit(solution)/shard_map/ppermute | solution.py:378
  254.2 1.9 collective-permute-start.25
  256.1 7.9 %collective-permute-start.26 = (bf16[1344,128]{1,0:T(8,128)(2,1)}, bf16[1344,128]{1,0:T(8,128)(2,1)}, u32[]{:S(2)}, u32[]{:S(2)}) collective-permute-start(bf16[1344,128]{1,0:T(8,128)(2,1)} %get-tuple-element.56), channel_id=1, source_target_pairs={{0,6},{1,7},{2,4},{3,5},{4,2},{5,3},{6,0},{7,1},{8,14},{9,15},{10,... | collective-permute-start | bytes 1032200 | tf_op jit(solution)/shard_map/ppermute | solution.py:378
  264.1 4.4 %collective-permute-start.27 = (bf16[1344,128]{1,0:T(8,128)(2,1)}, bf16[1344,128]{1,0:T(8,128)(2,1)}, u32[]{:S(2)}, u32[]{:S(2)}) collective-permute-start(bf16[1344,128]{1,0:T(8,128)(2,1)} %get-tuple-element.57), channel_id=1, source_target_pairs={{0,7},{1,6},{2,5},{3,4},{4,3},{5,2},{6,1},{7,0},{8,15},{9,14},{10,... | collective-permute-start | bytes 1032200 | tf_op jit(solution)/shard_map/ppermute | solution.py:378
  268.8 11.0 %shard_map.106.hidden_ref = bf16[1024,3072]{1,0:T(8,128)(2,1)} custom-call(bf16[384,1024]{1,0:T(8,128)(2,1)} %bitcast.15, bf16[384,1024]{1,0:T(8,128)(2,1)} %collective-permute-done.7.refs_1_, bf16[384,1024]{1,0:T(8,128)(2,1)} %collective-permute-done.8.refs_2_, bf16[384,1024]{1,0:T(8,128)(2,1)} %collective-permute-done.9.refs_3_, ...), custom_call_target="tpu_custom_call" | custom-call | tf_op jit(solution)/shard_map/pallas_call | solution.py:367
  279.8 7.5 %shard_map.109.tail_ref = f32[1024,128]{1,0:T(8,128)} custom-call(bf16[384,1024]{1,0:T(8,128)(2,1)} %bitcast.16, bf16[384,1024]{1,0:T(8,128)(2,1)} %collective-permute-done.7.refs_1_, bf16[384,1024]{1,0:T(8,128)(2,1)} %collective-permute-done.8.refs_2_, bf16[384,1024]{1,0:T(8,128)(2,1)} %collective-permute-done.9.refs_3_, ...), custom_call_target="tpu_custom_call" | custom-call | tf_op jit(solution)/shard_map/pallas_call | solution.py:367
  289.0 12.3 %shard_map.111 = (bf16[32,512]{1,0:T(8,128)(2,1)}, bf16[32,512]{1,0:T(8,128)(2,1)}, bf16[32,512]{1,0:T(8,128)(2,1)}, bf16[32,512]{1,0:T(8,128)(2,1)}, bf16[32,51...) custom-call(s32[1]{0:T(128)} %bitcast.own_ref, ...), custom_call_target="tpu_custom_call" | custom-call | tf_op jit(solution)/shard_map/pallas_call | solution.py:367
  301.3 1.9 collective-permute-start.35
  303.2 5.4 %collective-permute-start.36 = (bf16[32,512]{1,0:T(8,128)(2,1)}, bf16[32,512]{1,0:T(8,128)(2,1)S(1)}, u32[]{:S(2)}, u32[]{:S(2)}) collective-permute-start(bf16[32,512]{1,0:T(8,128)(2,1)} %get-tuple-element.60), channel_id=1, source_target_pairs={{0,2},{1,3},{2,0},{3,1},{4,6},{5,7},{6,4},{7,5},{8,10},{9,11},{10,... | collective-permute-start | bytes 98312 | tf_op jit(solution)/shard_map/ppermute | solution.py:378
  308.6 3.1 collective-permute-start.37
  311.7 3.7 %collective-permute-start.38 = (bf16[32,512]{1,0:T(8,128)(2,1)}, bf16[32,512]{1,0:T(8,128)(2,1)S(1)}, u32[]{:S(2)}, u32[]{:S(2)}) collective-permute-start(bf16[32,512]{1,0:T(8,128)(2,1)} %get-tuple-element.62), channel_id=1, source_target_pairs={{0,4},{1,5},{2,6},{3,7},{4,0},{5,1},{6,2},{7,3},{8,12},{9,13},{10,... | collective-permute-start | bytes 98312 | tf_op jit(solution)/shard_map/ppermute | solution.py:378
  315.4 1.9 collective-permute-start.39
  317.3 7.9 %collective-permute-start.40 = (bf16[32,512]{1,0:T(8,128)(2,1)}, bf16[32,512]{1,0:T(8,128)(2,1)S(1)}, u32[]{:S(2)}, u32[]{:S(2)}) collective-permute-start(bf16[32,512]{1,0:T(8,128)(2,1)} %get-tuple-element.64), channel_id=1, source_target_pairs={{0,6},{1,7},{2,4},{3,5},{4,2},{5,3},{6,0},{7,1},{8,14},{9,15},{10,... | collective-permute-start | bytes 98312 | tf_op jit(solution)/shard_map/ppermute | solution.py:378
  325.3 4.2 %collective-permute-start.41 = (bf16[32,512]{1,0:T(8,128)(2,1)}, bf16[32,512]{1,0:T(8,128)(2,1)S(1)}, u32[]{:S(2)}, u32[]{:S(2)}) collective-permute-start(bf16[32,512]{1,0:T(8,128)(2,1)} %get-tuple-element.65), channel_id=1, source_target_pairs={{0,7},{1,6},{2,5},{3,4},{4,3},{5,2},{6,1},{7,0},{8,15},{9,14},{10,... | collective-permute-start | bytes 98312 | tf_op jit(solution)/shard_map/ppermute | solution.py:378
  330.3 4.6 %collective-permute-done.41.refs_7_ = bf16[32,512]{1,0:T(8,128)(2,1)S(1)} collective-permute-done((bf16[32,512]{1,0:T(8,128)(2,1)}, bf16[32,512]{1,0:T(8,128)(2,1)S(1)}, u32[]{:S(2)}, u32[]{:S(2)}) %collective-permute-start.41) | collective-permute-done | bytes 32800 | tf_op jit(solution)/shard_map/ppermute | solution.py:378
  335.5 1.7 shard_map.112
  (111 shorter events, 7.6 us)
Async XLA Ops:
  5.1 62.9 %all-to-all-start.1 = ((bf16[64,24,128]{2,1,0:T(8,128)(2,1)}), bf16[64,24,128]{2,1,0:T(8,128)(2,1)S(1)}, u32[]{:S(2)}, u32[]{:S(2)}) async-start(bf16[64,24,128]{2,1,0:T(8,128)(2,1)} %bitcast.25), calls=%async_computation.1 | async-start | bytes 786432 | tf_op jit(solution)/shard_map/all_to_all | solution.py:384
  23.2 17.5 %collective-permute-start = (bf16[136,384]{1,0:T(8,128)(2,1)}, bf16[136,384]{1,0:T(8,128)(2,1)S(1)}, u32[]{:S(2)}, u32[]{:S(2)}) collective-permute-start(bf16[136,384]{1,0:T(8,128)(2,1)} %get-tuple-element.35), channel_id=1, source_target_pairs={{0,1},{1,0},{2,3},{3,2},{4,5},{5,4},{6,7},{7,6},{8,9},{9,8},{10,11... | collective-permute-start | bytes 313352 | tf_op jit(solution)/shard_map/ppermute | solution.py:378
  26.6 22.3 %collective-permute-start.1 = (bf16[136,384]{1,0:T(8,128)(2,1)}, bf16[136,384]{1,0:T(8,128)(2,1)S(1)}, u32[]{:S(2)}, u32[]{:S(2)}) collective-permute-start(bf16[136,384]{1,0:T(8,128)(2,1)} %get-tuple-element.36), channel_id=1, source_target_pairs={{0,2},{1,3},{2,0},{3,1},{4,6},{5,7},{6,4},{7,5},{8,10},{9,11},{10,... | collective-permute-start | bytes 313352 | tf_op jit(solution)/shard_map/ppermute | solution.py:378
  31.2 20.2 %collective-permute-start.2 = (bf16[136,384]{1,0:T(8,128)(2,1)}, bf16[136,384]{1,0:T(8,128)(2,1)S(1)}, u32[]{:S(2)}, u32[]{:S(2)}) collective-permute-start(bf16[136,384]{1,0:T(8,128)(2,1)} %get-tuple-element.37), channel_id=1, source_target_pairs={{0,3},{1,2},{2,1},{3,0},{4,7},{5,6},{6,5},{7,4},{8,11},{9,10},{10,... | collective-permute-start | bytes 313352 | tf_op jit(solution)/shard_map/ppermute | solution.py:378
  33.6 17.8 %collective-permute-start.3 = (bf16[136,384]{1,0:T(8,128)(2,1)}, bf16[136,384]{1,0:T(8,128)(2,1)S(1)}, u32[]{:S(2)}, u32[]{:S(2)}) collective-permute-start(bf16[136,384]{1,0:T(8,128)(2,1)} %get-tuple-element.38), channel_id=1, source_target_pairs={{0,4},{1,5},{2,6},{3,7},{4,0},{5,1},{6,2},{7,3},{8,12},{9,13},{10,... | collective-permute-start | bytes 313352 | tf_op jit(solution)/shard_map/ppermute | solution.py:378
  38.4 13.0 %collective-permute-start.4 = (bf16[136,384]{1,0:T(8,128)(2,1)}, bf16[136,384]{1,0:T(8,128)(2,1)S(1)}, u32[]{:S(2)}, u32[]{:S(2)}) collective-permute-start(bf16[136,384]{1,0:T(8,128)(2,1)} %get-tuple-element.39), channel_id=1, source_target_pairs={{0,5},{1,4},{2,7},{3,6},{4,1},{5,0},{6,3},{7,2},{8,13},{9,12},{10,... | collective-permute-start | bytes 313352 | tf_op jit(solution)/shard_map/ppermute | solution.py:378
  40.7 18.6 %copy-start.8 = (bf16[136,384]{1,0:T(8,128)(2,1)}, bf16[136,384]{1,0:T(8,128)(2,1)S(1)}, u32[]{:S(2)}) copy-start(bf16[136,384]{1,0:T(8,128)(2,1)S(1)} %collective-permute-done.refs_1_) | copy-start | bytes 313348
  40.7 11.3 %collective-permute-start.5 = (bf16[136,384]{1,0:T(8,128)(2,1)}, bf16[136,384]{1,0:T(8,128)(2,1)S(1)}, u32[]{:S(2)}, u32[]{:S(2)}) collective-permute-start(bf16[136,384]{1,0:T(8,128)(2,1)} %get-tuple-element.40), channel_id=1, source_target_pairs={{0,6},{1,7},{2,4},{3,5},{4,2},{5,3},{6,0},{7,1},{8,14},{9,15},{10,... | collective-permute-start | bytes 313352 | tf_op jit(solution)/shard_map/ppermute | solution.py:378
  48.9 10.4 %copy-start.9 = (bf16[136,384]{1,0:T(8,128)(2,1)}, bf16[136,384]{1,0:T(8,128)(2,1)S(1)}, u32[]{:S(2)}) copy-start(bf16[136,384]{1,0:T(8,128)(2,1)S(1)} %collective-permute-done.1.refs_2_) | copy-start | bytes 313348
  48.9 10.4 %collective-permute-start.6 = (bf16[136,384]{1,0:T(8,128)(2,1)}, bf16[136,384]{1,0:T(8,128)(2,1)S(1)}, u32[]{:S(2)}, u32[]{:S(2)}) collective-permute-start(bf16[136,384]{1,0:T(8,128)(2,1)} %get-tuple-element.41), channel_id=1, source_target_pairs={{0,7},{1,6},{2,5},{3,4},{4,3},{5,2},{6,1},{7,0},{8,15},{9,14},{10,... | collective-permute-start | bytes 313352 | tf_op jit(solution)/shard_map/ppermute | solution.py:378
  68.0 13.9 %copy-start.1 = (bf16[1,384,1024]{2,1,0:T(8,128)(2,1)S(1)}, bf16[1,384,1024]{2,1,0:T(8,128)(2,1)}, u32[]{:S(2)}) copy-start(bf16[1,384,1024]{2,1,0:T(8,128)(2,1)} %param.13) | copy-start | bytes 2359300
  68.8 218.6 %all-to-all-start = ((bf16[64,144,128]{2,1,0:T(8,128)(2,1)}), bf16[64,144,128]{2,1,0:T(8,128)(2,1)S(1)}, u32[]{:S(2)}, u32[]{:S(2)}) async-start(bf16[64,144,128]{2,1,0:T(8,128)(2,1)} %bitcast.13), calls=%async_computation | async-start | bytes 4718592 | tf_op jit(solution)/shard_map/all_to_all | solution.py:384
  81.9 59.4 %copy-start.15 = (bf16[1,32,1024]{2,1,0:T(8,128)(2,1)S(1)}, bf16[1,32,1024]{2,1,0:T(8,128)(2,1)}, u32[]{:S(2)}) copy-start(bf16[1,32,1024]{2,1,0:T(8,128)(2,1)} %param.17) | copy-start | bytes 196612
  81.9 186.6 %copy-start.3 = (bf16[128,384]{1,0:T(8,128)(2,1)S(1)}, bf16[128,384]{1,0:T(8,128)(2,1)}, u32[]{:S(2)}) copy-start(bf16[128,384]{1,0:T(8,128)(2,1)} %param.12) | copy-start | bytes 294916
  81.9 107.1 %collective-permute-start.13 = (bf16[384,1024]{1,0:T(8,128)(2,1)S(1)}, bf16[384,1024]{1,0:T(8,128)(2,1)}, u32[]{:S(2)}, u32[]{:S(2)}) collective-permute-start(bf16[384,1024]{1,0:T(8,128)(2,1)S(1)} %bitcast.17), channel_id=1, source_target_pairs={{0,7},{1,6},{2,5},{3,4},{4,3},{5,2},{6,1},{7,0},{8,15},{9,14},{10,... | collective-permute-start | bytes 2359304 | tf_op jit(solution)/shard_map/ppermute | solution.py:378
  85.7 109.1 %collective-permute-start.12 = (bf16[384,1024]{1,0:T(8,128)(2,1)S(1)}, bf16[384,1024]{1,0:T(8,128)(2,1)}, u32[]{:S(2)}, u32[]{:S(2)}) collective-permute-start(bf16[384,1024]{1,0:T(8,128)(2,1)S(1)} %bitcast.18), channel_id=1, source_target_pairs={{0,6},{1,7},{2,4},{3,5},{4,2},{5,3},{6,0},{7,1},{8,14},{9,15},{10,... | collective-permute-start | bytes 2359304 | tf_op jit(solution)/shard_map/ppermute | solution.py:378
  88.1 53.1 %collective-permute-start.34 = (bf16[32,1024]{1,0:T(8,128)(2,1)}, bf16[32,1024]{1,0:T(8,128)(2,1)S(1)}, u32[]{:S(2)}, u32[]{:S(2)}) collective-permute-start(bf16[32,1024]{1,0:T(8,128)(2,1)} %bitcast.30), channel_id=1, source_target_pairs={{0,7},{1,6},{2,5},{3,4},{4,3},{5,2},{6,1},{7,0},{8,15},{9,14},{10,... | collective-permute-start | bytes 196616 | tf_op jit(solution)/shard_map/ppermute | solution.py:378
  93.4 49.8 %collective-permute-start.33 = (bf16[32,1024]{1,0:T(8,128)(2,1)}, bf16[32,1024]{1,0:T(8,128)(2,1)S(1)}, u32[]{:S(2)}, u32[]{:S(2)}) collective-permute-start(bf16[32,1024]{1,0:T(8,128)(2,1)} %bitcast.31), channel_id=1, source_target_pairs={{0,6},{1,7},{2,4},{3,5},{4,2},{5,3},{6,0},{7,1},{8,14},{9,15},{10,... | collective-permute-start | bytes 196616 | tf_op jit(solution)/shard_map/ppermute | solution.py:378
  104.5 79.1 %collective-permute-start.21 = (bf16[1344,128]{1,0:T(8,128)(2,1)}, bf16[1344,128]{1,0:T(8,128)(2,1)S(1)}, u32[]{:S(2)}, u32[]{:S(2)}) collective-permute-start(bf16[1344,128]{1,0:T(8,128)(2,1)} %get-tuple-element.51), channel_id=1, source_target_pairs={{0,1},{1,0},{2,3},{3,2},{4,5},{5,4},{6,7},{7,6},{8,9},{9,8},{10,11... | collective-permute-start | bytes 1032200 | tf_op jit(solution)/shard_map/ppermute | solution.py:378
  141.3 146.0 %copy-start.16 = (bf16[32,1024]{1,0:T(8,128)(2,1)}, bf16[32,1024]{1,0:T(8,128)(2,1)S(1)}, u32[]{:S(2)}) copy-start(bf16[32,1024]{1,0:T(8,128)(2,1)S(1)} %collective-permute-done.34.refs_15_) | copy-start | bytes 196612
  141.3 9.2 %collective-permute-start.32 = (bf16[32,1024]{1,0:T(8,128)(2,1)S(1)}, bf16[32,1024]{1,0:T(8,128)(2,1)S(1)}, u32[]{:S(2)}, u32[]{:S(2)}) collective-permute-start(bf16[32,1024]{1,0:T(8,128)(2,1)S(1)} %bitcast.33), channel_id=1, source_target_pairs={{0,5},{1,4},{2,7},{3,6},{4,1},{5,0},{6,3},{7,2},{8,13},{9,12},{10,... | collective-permute-start | bytes 196616 | tf_op jit(solution)/shard_map/ppermute | solution.py:378
  143.2 144.1 %copy-start.17 = (bf16[32,1024]{1,0:T(8,128)(2,1)}, bf16[32,1024]{1,0:T(8,128)(2,1)S(1)}, u32[]{:S(2)}) copy-start(bf16[32,1024]{1,0:T(8,128)(2,1)S(1)} %collective-permute-done.33.refs_14_) | copy-start | bytes 196612
  143.2 43.4 %collective-permute-start.22 = (bf16[1344,128]{1,0:T(8,128)(2,1)}, bf16[1344,128]{1,0:T(8,128)(2,1)S(1)}, u32[]{:S(2)}, u32[]{:S(2)}) collective-permute-start(bf16[1344,128]{1,0:T(8,128)(2,1)} %get-tuple-element.52), channel_id=1, source_target_pairs={{0,2},{1,3},{2,0},{3,1},{4,6},{5,7},{6,4},{7,5},{8,10},{9,11},{10,... | collective-permute-start | bytes 1032200 | tf_op jit(solution)/shard_map/ppermute | solution.py:378
  150.4 136.8 %copy-start.18 = (bf16[32,1024]{1,0:T(8,128)(2,1)}, bf16[32,1024]{1,0:T(8,128)(2,1)S(1)}, u32[]{:S(2)}) copy-start(bf16[32,1024]{1,0:T(8,128)(2,1)S(1)} %collective-permute-done.32.refs_13_) | copy-start | bytes 196612
  150.4 8.0 %collective-permute-start.31 = (bf16[32,1024]{1,0:T(8,128)(2,1)S(1)}, bf16[32,1024]{1,0:T(8,128)(2,1)S(1)}, u32[]{:S(2)}, u32[]{:S(2)}) collective-permute-start(bf16[32,1024]{1,0:T(8,128)(2,1)S(1)} %bitcast.34), channel_id=1, source_target_pairs={{0,4},{1,5},{2,6},{3,7},{4,0},{5,1},{6,2},{7,3},{8,12},{9,13},{10,... | collective-permute-start | bytes 196616 | tf_op jit(solution)/shard_map/ppermute | solution.py:378
  158.5 38.3 %copy-start.19 = (bf16[32,1024]{1,0:T(8,128)(2,1)}, bf16[32,1024]{1,0:T(8,128)(2,1)S(1)}, u32[]{:S(2)}) copy-start(bf16[32,1024]{1,0:T(8,128)(2,1)S(1)} %collective-permute-done.31.refs_12_) | copy-start | bytes 196612
  158.5 7.4 %collective-permute-start.30 = (bf16[32,1024]{1,0:T(8,128)(2,1)S(1)}, bf16[32,1024]{1,0:T(8,128)(2,1)S(1)}, u32[]{:S(2)}, u32[]{:S(2)}) collective-permute-start(bf16[32,1024]{1,0:T(8,128)(2,1)S(1)} %bitcast.35), channel_id=1, source_target_pairs={{0,3},{1,2},{2,1},{3,0},{4,7},{5,6},{6,5},{7,4},{8,11},{9,10},{10,... | collective-permute-start | bytes 196616 | tf_op jit(solution)/shard_map/ppermute | solution.py:378
  165.8 30.9 %copy-start.20 = (bf16[32,1024]{1,0:T(8,128)(2,1)}, bf16[32,1024]{1,0:T(8,128)(2,1)S(1)}, u32[]{:S(2)}) copy-start(bf16[32,1024]{1,0:T(8,128)(2,1)S(1)} %collective-permute-done.30.refs_11_) | copy-start | bytes 196612
  165.8 7.7 %collective-permute-start.29 = (bf16[32,1024]{1,0:T(8,128)(2,1)S(1)}, bf16[32,1024]{1,0:T(8,128)(2,1)S(1)}, u32[]{:S(2)}, u32[]{:S(2)}) collective-permute-start(bf16[32,1024]{1,0:T(8,128)(2,1)S(1)} %bitcast.36), channel_id=1, source_target_pairs={{0,2},{1,3},{2,0},{3,1},{4,6},{5,7},{6,4},{7,5},{8,10},{9,11},{10,... | collective-permute-start | bytes 196616 | tf_op jit(solution)/shard_map/ppermute | solution.py:378
  173.5 23.3 %copy-start.21 = (bf16[32,1024]{1,0:T(8,128)(2,1)}, bf16[32,1024]{1,0:T(8,128)(2,1)S(1)}, u32[]{:S(2)}) copy-start(bf16[32,1024]{1,0:T(8,128)(2,1)S(1)} %collective-permute-done.29.refs_10_) | copy-start | bytes 196612
  173.5 6.5 %collective-permute-start.28 = (bf16[32,1024]{1,0:T(8,128)(2,1)S(1)}, bf16[32,1024]{1,0:T(8,128)(2,1)S(1)}, u32[]{:S(2)}, u32[]{:S(2)}) collective-permute-start(bf16[32,1024]{1,0:T(8,128)(2,1)S(1)} %bitcast.37), channel_id=1, source_target_pairs={{0,1},{1,0},{2,3},{3,2},{4,5},{5,4},{6,7},{7,6},{8,9},{9,8},{10,11... | collective-permute-start | bytes 196616 | tf_op jit(solution)/shard_map/ppermute | solution.py:378
  180.0 16.7 %copy-start.22 = (bf16[32,1024]{1,0:T(8,128)(2,1)}, bf16[32,1024]{1,0:T(8,128)(2,1)S(1)}, u32[]{:S(2)}) copy-start(bf16[32,1024]{1,0:T(8,128)(2,1)S(1)} %collective-permute-done.28.refs_9_) | copy-start | bytes 196612
  180.0 25.3 %collective-permute-start.11 = (bf16[384,1024]{1,0:T(8,128)(2,1)S(1)}, bf16[384,1024]{1,0:T(8,128)(2,1)}, u32[]{:S(2)}, u32[]{:S(2)}) collective-permute-start(bf16[384,1024]{1,0:T(8,128)(2,1)S(1)} %bitcast.19), channel_id=1, source_target_pairs={{0,5},{1,4},{2,7},{3,6},{4,1},{5,0},{6,3},{7,2},{8,13},{9,12},{10,... | collective-permute-start | bytes 2359304 | tf_op jit(solution)/shard_map/ppermute | solution.py:378
  183.6 13.2 %copy-start.4 = (bf16[1344,128]{1,0:T(8,128)(2,1)}, bf16[1344,128]{1,0:T(8,128)(2,1)S(1)}, u32[]{:S(2)}) copy-start(bf16[1344,128]{1,0:T(8,128)(2,1)S(1)} %collective-permute-done.21.refs_1_) | copy-start | bytes 1032196
  183.6 31.8 %collective-permute-start.10 = (bf16[384,1024]{1,0:T(8,128)(2,1)S(1)}, bf16[384,1024]{1,0:T(8,128)(2,1)}, u32[]{:S(2)}, u32[]{:S(2)}) collective-permute-start(bf16[384,1024]{1,0:T(8,128)(2,1)S(1)} %bitcast.20), channel_id=1, source_target_pairs={{0,4},{1,5},{2,6},{3,7},{4,0},{5,1},{6,2},{7,3},{8,12},{9,13},{10,... | collective-permute-start | bytes 2359304 | tf_op jit(solution)/shard_map/ppermute | solution.py:378
  186.6 10.1 %copy-start.5 = (bf16[1344,128]{1,0:T(8,128)(2,1)}, bf16[1344,128]{1,0:T(8,128)(2,1)S(1)}, u32[]{:S(2)}) copy-start(bf16[1344,128]{1,0:T(8,128)(2,1)S(1)} %collective-permute-done.22.refs_2_) | copy-start | bytes 1032196
  186.7 31.4 %collective-permute-start.9 = (bf16[384,1024]{1,0:T(8,128)(2,1)S(1)}, bf16[384,1024]{1,0:T(8,128)(2,1)}, u32[]{:S(2)}, u32[]{:S(2)}) collective-permute-start(bf16[384,1024]{1,0:T(8,128)(2,1)S(1)} %bitcast.21), channel_id=1, source_target_pairs={{0,3},{1,2},{2,1},{3,0},{4,7},{5,6},{6,5},{7,4},{8,11},{9,10},{10,... | collective-permute-start | bytes 2359304 | tf_op jit(solution)/shard_map/ppermute | solution.py:378
  189.0 33.1 %collective-permute-start.8 = (bf16[384,1024]{1,0:T(8,128)(2,1)S(1)}, bf16[384,1024]{1,0:T(8,128)(2,1)}, u32[]{:S(2)}, u32[]{:S(2)}) collective-permute-start(bf16[384,1024]{1,0:T(8,128)(2,1)S(1)} %bitcast.22), channel_id=1, source_target_pairs={{0,2},{1,3},{2,0},{3,1},{4,6},{5,7},{6,4},{7,5},{8,10},{9,11},{10,... | collective-permute-start | bytes 2359304 | tf_op jit(solution)/shard_map/ppermute | solution.py:378
  194.8 38.0 %collective-permute-start.7 = (bf16[384,1024]{1,0:T(8,128)(2,1)S(1)}, bf16[384,1024]{1,0:T(8,128)(2,1)}, u32[]{:S(2)}, u32[]{:S(2)}) collective-permute-start(bf16[384,1024]{1,0:T(8,128)(2,1)S(1)} %bitcast.23), channel_id=1, source_target_pairs={{0,1},{1,0},{2,3},{3,2},{4,5},{5,4},{6,7},{7,6},{8,9},{9,8},{10,11... | collective-permute-start | bytes 2359304 | tf_op jit(solution)/shard_map/ppermute | solution.py:378
  205.4 30.7 %collective-permute-start.14 = (bf16[192,128]{1,0:T(8,128)(2,1)}, bf16[192,128]{1,0:T(8,128)(2,1)S(1)}, u32[]{:S(2)}, u32[]{:S(2)}) collective-permute-start(bf16[192,128]{1,0:T(8,128)(2,1)} %get-tuple-element.43), channel_id=1, source_target_pairs={{0,1},{1,0},{2,3},{3,2},{4,5},{5,4},{6,7},{7,6},{8,9},{9,8},{10,11... | collective-permute-start | bytes 147464 | tf_op jit(solution)/shard_map/ppermute | solution.py:378
  215.4 26.1 %collective-permute-start.15 = (bf16[192,128]{1,0:T(8,128)(2,1)}, bf16[192,128]{1,0:T(8,128)(2,1)S(1)}, u32[]{:S(2)}, u32[]{:S(2)}) collective-permute-start(bf16[192,128]{1,0:T(8,128)(2,1)} %get-tuple-element.44), channel_id=1, source_target_pairs={{0,2},{1,3},{2,0},{3,1},{4,6},{5,7},{6,4},{7,5},{8,10},{9,11},{10,... | collective-permute-start | bytes 147464 | tf_op jit(solution)/shard_map/ppermute | solution.py:378
  218.1 28.7 %collective-permute-start.16 = (bf16[192,128]{1,0:T(8,128)(2,1)}, bf16[192,128]{1,0:T(8,128)(2,1)S(1)}, u32[]{:S(2)}, u32[]{:S(2)}) collective-permute-start(bf16[192,128]{1,0:T(8,128)(2,1)} %get-tuple-element.45), channel_id=1, source_target_pairs={{0,3},{1,2},{2,1},{3,0},{4,7},{5,6},{6,5},{7,4},{8,11},{9,10},{10,... | collective-permute-start | bytes 147464 | tf_op jit(solution)/shard_map/ppermute | solution.py:378
  222.1 27.7 %collective-permute-start.17 = (bf16[192,128]{1,0:T(8,128)(2,1)}, bf16[192,128]{1,0:T(8,128)(2,1)S(1)}, u32[]{:S(2)}, u32[]{:S(2)}) collective-permute-start(bf16[192,128]{1,0:T(8,128)(2,1)} %get-tuple-element.46), channel_id=1, source_target_pairs={{0,4},{1,5},{2,6},{3,7},{4,0},{5,1},{6,2},{7,3},{8,12},{9,13},{10,... | collective-permute-start | bytes 147464 | tf_op jit(solution)/shard_map/ppermute | solution.py:378
  232.8 21.4 %collective-permute-start.18 = (bf16[192,128]{1,0:T(8,128)(2,1)}, bf16[192,128]{1,0:T(8,128)(2,1)S(1)}, u32[]{:S(2)}, u32[]{:S(2)}) collective-permute-start(bf16[192,128]{1,0:T(8,128)(2,1)} %get-tuple-element.47), channel_id=1, source_target_pairs={{0,5},{1,4},{2,7},{3,6},{4,1},{5,0},{6,3},{7,2},{8,13},{9,12},{10,... | collective-permute-start | bytes 147464 | tf_op jit(solution)/shard_map/ppermute | solution.py:378
  236.1 43.7 %copy-start.23 = (bf16[192,128]{1,0:T(8,128)(2,1)}, bf16[192,128]{1,0:T(8,128)(2,1)S(1)}, u32[]{:S(2)}) copy-start(bf16[192,128]{1,0:T(8,128)(2,1)S(1)} %collective-permute-done.14.refs_9_) | copy-start | bytes 147460
  236.1 20.0 %collective-permute-start.19 = (bf16[192,128]{1,0:T(8,128)(2,1)}, bf16[192,128]{1,0:T(8,128)(2,1)S(1)}, u32[]{:S(2)}, u32[]{:S(2)}) collective-permute-start(bf16[192,128]{1,0:T(8,128)(2,1)} %get-tuple-element.48), channel_id=1, source_target_pairs={{0,6},{1,7},{2,4},{3,5},{4,2},{5,3},{6,0},{7,1},{8,14},{9,15},{10,... | collective-permute-start | bytes 147464 | tf_op jit(solution)/shard_map/ppermute | solution.py:378
  241.6 38.2 %copy-start.24 = (bf16[192,128]{1,0:T(8,128)(2,1)}, bf16[192,128]{1,0:T(8,128)(2,1)S(1)}, u32[]{:S(2)}) copy-start(bf16[192,128]{1,0:T(8,128)(2,1)S(1)} %collective-permute-done.15.refs_10_) | copy-start | bytes 147460
  241.6 22.5 %collective-permute-start.20 = (bf16[192,128]{1,0:T(8,128)(2,1)}, bf16[192,128]{1,0:T(8,128)(2,1)}, u32[]{:S(2)}, u32[]{:S(2)}) collective-permute-start(bf16[192,128]{1,0:T(8,128)(2,1)} %get-tuple-element.49), channel_id=1, source_target_pairs={{0,7},{1,6},{2,5},{3,4},{4,3},{5,2},{6,1},{7,0},{8,15},{9,14},{10,... | collective-permute-start | bytes 147464 | tf_op jit(solution)/shard_map/ppermute | solution.py:378
  246.8 40.5 %collective-permute-start.23 = (bf16[1344,128]{1,0:T(8,128)(2,1)}, bf16[1344,128]{1,0:T(8,128)(2,1)S(1)}, u32[]{:S(2)}, u32[]{:S(2)}) collective-permute-start(bf16[1344,128]{1,0:T(8,128)(2,1)} %get-tuple-element.53), channel_id=1, source_target_pairs={{0,3},{1,2},{2,1},{3,0},{4,7},{5,6},{6,5},{7,4},{8,11},{9,10},{10,... | collective-permute-start | bytes 1032200 | tf_op jit(solution)/shard_map/ppermute | solution.py:378
  250.5 36.8 %collective-permute-start.24 = (bf16[1344,128]{1,0:T(8,128)(2,1)}, bf16[1344,128]{1,0:T(8,128)(2,1)S(1)}, u32[]{:S(2)}, u32[]{:S(2)}) collective-permute-start(bf16[1344,128]{1,0:T(8,128)(2,1)} %get-tuple-element.54), channel_id=1, source_target_pairs={{0,4},{1,5},{2,6},{3,7},{4,0},{5,1},{6,2},{7,3},{8,12},{9,13},{10,... | collective-permute-start | bytes 1032200 | tf_op jit(solution)/shard_map/ppermute | solution.py:378
  254.2 25.6 %copy-start.27 = (bf16[192,128]{1,0:T(8,128)(2,1)}, bf16[192,128]{1,0:T(8,128)(2,1)S(1)}, u32[]{:S(2)}) copy-start(bf16[192,128]{1,0:T(8,128)(2,1)S(1)} %collective-permute-done.18.refs_13_) | copy-start | bytes 147460
  254.2 33.2 %collective-permute-start.25 = (bf16[1344,128]{1,0:T(8,128)(2,1)}, bf16[1344,128]{1,0:T(8,128)(2,1)}, u32[]{:S(2)}, u32[]{:S(2)}) collective-permute-start(bf16[1344,128]{1,0:T(8,128)(2,1)} %get-tuple-element.55), channel_id=1, source_target_pairs={{0,5},{1,4},{2,7},{3,6},{4,1},{5,0},{6,3},{7,2},{8,13},{9,12},{10,... | collective-permute-start | bytes 1032200 | tf_op jit(solution)/shard_map/ppermute | solution.py:378
  256.1 23.7 %copy-start.28 = (bf16[192,128]{1,0:T(8,128)(2,1)}, bf16[192,128]{1,0:T(8,128)(2,1)S(1)}, u32[]{:S(2)}) copy-start(bf16[192,128]{1,0:T(8,128)(2,1)S(1)} %collective-permute-done.19.refs_14_) | copy-start | bytes 147460
  256.1 31.2 %collective-permute-start.26 = (bf16[1344,128]{1,0:T(8,128)(2,1)}, bf16[1344,128]{1,0:T(8,128)(2,1)}, u32[]{:S(2)}, u32[]{:S(2)}) collective-permute-start(bf16[1344,128]{1,0:T(8,128)(2,1)} %get-tuple-element.56), channel_id=1, source_target_pairs={{0,6},{1,7},{2,4},{3,5},{4,2},{5,3},{6,0},{7,1},{8,14},{9,15},{10,... | collective-permute-start | bytes 1032200 | tf_op jit(solution)/shard_map/ppermute | solution.py:378
  264.1 23.3 %collective-permute-start.27 = (bf16[1344,128]{1,0:T(8,128)(2,1)}, bf16[1344,128]{1,0:T(8,128)(2,1)}, u32[]{:S(2)}, u32[]{:S(2)}) collective-permute-start(bf16[1344,128]{1,0:T(8,128)(2,1)} %get-tuple-element.57), channel_id=1, source_target_pairs={{0,7},{1,6},{2,5},{3,4},{4,3},{5,2},{6,1},{7,0},{8,15},{9,14},{10,... | collective-permute-start | bytes 1032200 | tf_op jit(solution)/shard_map/ppermute | solution.py:378
  301.3 16.1 %collective-permute-start.35 = (bf16[32,512]{1,0:T(8,128)(2,1)}, bf16[32,512]{1,0:T(8,128)(2,1)S(1)}, u32[]{:S(2)}, u32[]{:S(2)}) collective-permute-start(bf16[32,512]{1,0:T(8,128)(2,1)} %get-tuple-element.59), channel_id=1, source_target_pairs={{0,1},{1,0},{2,3},{3,2},{4,5},{5,4},{6,7},{7,6},{8,9},{9,8},{10,11... | collective-permute-start | bytes 98312 | tf_op jit(solution)/shard_map/ppermute | solution.py:378
  303.2 22.1 %collective-permute-start.36 = (bf16[32,512]{1,0:T(8,128)(2,1)}, bf16[32,512]{1,0:T(8,128)(2,1)S(1)}, u32[]{:S(2)}, u32[]{:S(2)}) collective-permute-start(bf16[32,512]{1,0:T(8,128)(2,1)} %get-tuple-element.60), channel_id=1, source_target_pairs={{0,2},{1,3},{2,0},{3,1},{4,6},{5,7},{6,4},{7,5},{8,10},{9,11},{10,... | collective-permute-start | bytes 98312 | tf_op jit(solution)/shard_map/ppermute | solution.py:378
  308.6 21.6 %collective-permute-start.37 = (bf16[32,512]{1,0:T(8,128)(2,1)}, bf16[32,512]{1,0:T(8,128)(2,1)S(1)}, u32[]{:S(2)}, u32[]{:S(2)}) collective-permute-start(bf16[32,512]{1,0:T(8,128)(2,1)} %get-tuple-element.61), channel_id=1, source_target_pairs={{0,3},{1,2},{2,1},{3,0},{4,7},{5,6},{6,5},{7,4},{8,11},{9,10},{10,... | collective-permute-start | bytes 98312 | tf_op jit(solution)/shard_map/ppermute | solution.py:378
  311.7 18.5 %collective-permute-start.38 = (bf16[32,512]{1,0:T(8,128)(2,1)}, bf16[32,512]{1,0:T(8,128)(2,1)S(1)}, u32[]{:S(2)}, u32[]{:S(2)}) collective-permute-start(bf16[32,512]{1,0:T(8,128)(2,1)} %get-tuple-element.62), channel_id=1, source_target_pairs={{0,4},{1,5},{2,6},{3,7},{4,0},{5,1},{6,2},{7,3},{8,12},{9,13},{10,... | collective-permute-start | bytes 98312 | tf_op jit(solution)/shard_map/ppermute | solution.py:378
  315.4 14.9 %collective-permute-start.39 = (bf16[32,512]{1,0:T(8,128)(2,1)}, bf16[32,512]{1,0:T(8,128)(2,1)S(1)}, u32[]{:S(2)}, u32[]{:S(2)}) collective-permute-start(bf16[32,512]{1,0:T(8,128)(2,1)} %get-tuple-element.63), channel_id=1, source_target_pairs={{0,5},{1,4},{2,7},{3,6},{4,1},{5,0},{6,3},{7,2},{8,13},{9,12},{10,... | collective-permute-start | bytes 98312 | tf_op jit(solution)/shard_map/ppermute | solution.py:378
  317.3 17.6 %copy-start.29 = (bf16[32,512]{1,0:T(8,128)(2,1)}, bf16[32,512]{1,0:T(8,128)(2,1)S(1)}, u32[]{:S(2)}) copy-start(bf16[32,512]{1,0:T(8,128)(2,1)S(1)} %collective-permute-done.35.refs_1_) | copy-start | bytes 98308
  317.3 12.9 %collective-permute-start.40 = (bf16[32,512]{1,0:T(8,128)(2,1)}, bf16[32,512]{1,0:T(8,128)(2,1)S(1)}, u32[]{:S(2)}, u32[]{:S(2)}) collective-permute-start(bf16[32,512]{1,0:T(8,128)(2,1)} %get-tuple-element.64), channel_id=1, source_target_pairs={{0,6},{1,7},{2,4},{3,5},{4,2},{5,3},{6,0},{7,1},{8,14},{9,15},{10,... | collective-permute-start | bytes 98312 | tf_op jit(solution)/shard_map/ppermute | solution.py:378
  325.3 9.6 %copy-start.30 = (bf16[32,512]{1,0:T(8,128)(2,1)}, bf16[32,512]{1,0:T(8,128)(2,1)S(1)}, u32[]{:S(2)}) copy-start(bf16[32,512]{1,0:T(8,128)(2,1)S(1)} %collective-permute-done.36.refs_2_) | copy-start | bytes 98308
  325.3 9.6 %collective-permute-start.41 = (bf16[32,512]{1,0:T(8,128)(2,1)}, bf16[32,512]{1,0:T(8,128)(2,1)S(1)}, u32[]{:S(2)}, u32[]{:S(2)}) collective-permute-start(bf16[32,512]{1,0:T(8,128)(2,1)} %get-tuple-element.65), channel_id=1, source_target_pairs={{0,7},{1,6},{2,5},{3,4},{4,3},{5,2},{6,1},{7,0},{8,15},{9,14},{10,... | collective-permute-start | bytes 98312 | tf_op jit(solution)/shard_map/ppermute | solution.py:378
  (16 other events, 58.8 us)

commit v2 on v0

v2 whole, which is shorter than its diff:
```python
import jax
import jax.numpy as jnp
from jax import lax
from jax.experimental import pallas as pl
from jax.experimental.pallas import tpu as pltpu
from jax.sharding import PartitionSpec as P

beta_one = 0.9
beta_two = 0.95
learn_rate = 0.2
decay_rate = 0.1
step_count = 100.0
adam_eps = 1e-08
zloss_coef = 0.25

LANE = 128
HALF = 64
META = 8
WIDE = 3
SPAN = WIDE * LANE
SCOPED = 56 << 20


def adamw(weight, first, second, gradient):
    first_new = beta_one * first.astype(jnp.float32) + (1.0 - beta_one) * gradient
    second_new = beta_two * second.astype(jnp.float32) + (1.0 - beta_two) * gradient * gradient
    first_hat = first_new * (1.0 / (1.0 - beta_one**step_count))
    second_hat = second_new * (1.0 / (1.0 - beta_two**step_count))
    current = weight.astype(jnp.float32)
    change = first_hat / (jnp.sqrt(second_hat) + adam_eps) + decay_rate * current
    return (current - learn_rate * change).astype(jnp.bfloat16)


def zloss_grad(logits):
    values = logits.astype(jnp.float32)
    row_max = jnp.max(values, axis=-1, keepdims=True)
    log_total = row_max + jnp.log(jnp.sum(jnp.exp(values - row_max), axis=-1, keepdims=True))
    probs = jnp.exp(values - log_total)
    return (zloss_coef * 2.0 * log_total * probs).astype(jnp.bfloat16)


def iota(shape, dim):
    return lax.broadcasted_iota(jnp.int32, shape, dim)


def digits(value, *bases):
    found = []
    for base in reversed(bases):
        above = jnp.floor((value.astype(jnp.float32) + 0.5) * (1.0 / base)).astype(jnp.int32)
        found.append(value - above * base)
        value = above
    return found[::-1]


def slots_of(ids):
    tokens = ids[0].shape[1]
    wide = [jnp.broadcast_to(row, (tokens, tokens)) for row in ids]
    tall = [jnp.transpose(mat) for mat in wide]
    earlier = iota((tokens, tokens), 0) < iota((tokens, tokens), 1)
    counts = []
    for mat in wide:
        hits = jnp.where(earlier & (tall[0] == mat), 1.0, 0.0)
        hits = hits + jnp.where(earlier & (tall[1] == mat), 1.0, 0.0)
        counts.append(jnp.sum(hits, axis=0, keepdims=True))
    return counts


def own_block(replicas):
    def body(ids_ref, combine_ref, grad_ref, message_ref):
        ids = ids_ref[...].astype(jnp.float32)
        combine = combine_ref[...]
        tokens = ids.shape[1]
        fold = tokens // 2
        pieces = [ids[0:1], ids[1:2]]
        for k in range(2):
            rest = combine[k : k + 1]
            for _ in range(3):
                part = rest.astype(jnp.bfloat16).astype(jnp.float32)
                pieces.append(part)
                rest = rest - part
        meta = jnp.concatenate(pieces, axis=0).astype(jnp.bfloat16)
        left = iota((fold, LANE), 1) < HALF
        size = WIDE * tokens + fold + META
        for j in range(replicas):
            base = j * size
            for t in range(WIDE):
                column = j * SPAN + t * LANE
                message_ref[base + t * tokens : base + (t + 1) * tokens, :] = grad_ref[
                    :, column : column + LANE
                ]
            column = replicas * SPAN + (j // 2) * LANE
            tile = grad_ref[:, column : column + LANE].astype(jnp.float32)
            turned = pltpu.roll(tile, HALF, 1)
            if j % 2 == 0:
                folded = jnp.where(left, tile[:fold], turned[fold:])
            else:
                folded = jnp.where(left, turned[:fold], tile[fold:])
            base += WIDE * tokens
            message_ref[base : base + fold, :] = folded.astype(jnp.bfloat16)
            message_ref[base + fold : base + fold + META, :] = meta

    return body


def own_columns(experts, capacity, replicas, tokens, group):
    part = replicas // 2
    height = part * capacity
    fold = tokens // 2

    def body(message_ref, send_ref, tokens_ref, target_ref, weight_ref):
        size = WIDE * tokens + fold + META
        for j in range(replicas):
            base, row = j * size, j * tokens
            for t in range(WIDE):
                tokens_ref[row : row + tokens, t * LANE : (t + 1) * LANE] = message_ref[
                    base + t * tokens : base + (t + 1) * tokens, :
                ]
            base += WIDE * tokens
            folded = message_ref[base : base + fold, :]
            turned = pltpu.roll(folded.astype(jnp.float32), HALF, 1).astype(jnp.bfloat16)
            tokens_ref[row : row + fold, SPAN : SPAN + LANE] = folded
            tokens_ref[row + fold : row + tokens, SPAN : SPAN + LANE] = turned
            meta = message_ref[base + fold : base + fold + META, 0:tokens].astype(jnp.float32)
            id_rows = [meta[0:1], meta[1:2]]
            slots = slots_of(id_rows)
            for k in range(2):
                where = id_rows[k] * height + slots[k] + float((j % part) * capacity)
                target_ref[k : k + 1, row : row + tokens] = where.astype(jnp.int32)
                first = 2 + 3 * k
                weight_ref[k : k + 1, row : row + tokens] = (
                    meta[first : first + 1] + meta[first + 1 : first + 2]
                ) + meta[first + 2 : first + 3]
        rows = group * height
        block = part * tokens
        total = 2 * WIDE * height + height
        left = iota((height, LANE), 1) < HALF

        def step(i, carry):
            key = iota((rows, block), 0) + i * rows
            lasts = []
            for h in range(2):
                columns = slice(h * block, (h + 1) * block)
                spread = jnp.where(
                    key == target_ref[0:1, columns],
                    weight_ref[0:1, columns],
                    jnp.where(key == target_ref[1:2, columns], weight_ref[1:2, columns], 0.0),
                )
                scale = jnp.sum(spread, axis=1, keepdims=True)
                chosen = jnp.where(spread > 0.0, 1.0, 0.0).astype(jnp.bfloat16)
                picked = jnp.dot(
                    chosen, tokens_ref[columns, :], preferred_element_type=jnp.float32
                )
                sent = picked * scale
                for g in range(group):
                    for t in range(WIDE):
                        start = (i * group + g) * total + (h * WIDE + t) * height
                        send_ref[pl.ds(pl.multiple_of(start, 8), height), :] = sent[
                            g * height : (g + 1) * height, t * LANE : (t + 1) * LANE
                        ].astype(jnp.bfloat16)
                lasts.append(sent[:, SPAN : SPAN + LANE])
            turned = pltpu.roll(lasts[1], HALF, 1)
            for g in range(group):
                place = slice(g * height, (g + 1) * height)
                start = (i * group + g) * total + 2 * WIDE * height
                send_ref[pl.ds(pl.multiple_of(start, 8), height), :] = jnp.where(
                    left, lasts[0][place], turned[place]
                ).astype(jnp.bfloat16)
            return carry

        lax.fori_loop(0, experts // group, step, 0)

    return body


def split_state(replicas):
    def body(own_ref, *refs):
        inputs, outputs = refs[:3], refs[3:]
        for a in range(3):
            rows = inputs[a].shape[0]
            height = WIDE * rows + rows // 2
            for r in range(replicas):
                owner = own_ref[0] ^ r
                for t in range(WIDE):
                    start = pl.multiple_of(owner * SPAN + t * LANE, LANE)
                    outputs[r][a * height + t * rows : a * height + (t + 1) * rows, :] = inputs[a][
                        :, pl.ds(start, LANE)
                    ]
                start = pl.multiple_of(replicas * SPAN + (owner >> 1) * LANE, LANE)
                tile = inputs[a][:, pl.ds(start, LANE)].astype(jnp.float32)
                turned = pltpu.roll(tile, HALF, 1)
                odd = jnp.broadcast_to(owner & 1, (rows // 2, LANE)) == 1
                low = jnp.where(odd, turned[: rows // 2], tile[: rows // 2])
                high = jnp.where(odd, tile[rows // 2 :], turned[rows // 2 :])
                left = iota((rows // 2, LANE), 1) < HALF
                outputs[r][a * height + WIDE * rows : (a + 1) * height, :] = jnp.where(
                    left, low, high
                ).astype(jnp.bfloat16)

    return body


def order_hidden(experts, capacity, replicas, group):
    rows = group * capacity
    part = replicas // 2
    total = part * rows
    runs = 2

    def body(own_ref, *refs):
        pieces, out_ref = refs[:replicas], refs[replicas]
        units = out_ref.shape[1]
        half, source, replica, slot = digits(iota((2 * total, 2 * total), 0), 2, group, part, capacity)
        origin = (half * part + replica) ^ own_ref[0]
        wanted = origin * rows + source * capacity + slot
        move = jnp.where(iota((2 * total, 2 * total), 1) == wanted, 1.0, 0.0)
        move = move.astype(jnp.bfloat16)
        steps = experts // group
        for i in range(steps):
            stacked = jnp.concatenate(
                [ref[i * rows : (i + 1) * rows, :] for ref in pieces], axis=0
            )
            moved = jnp.dot(move, stacked, preferred_element_type=jnp.float32)
            moved = jnp.transpose(moved).astype(jnp.bfloat16)
            run, place = i // (steps // runs), i % (steps // runs)
            for h in range(2):
                out_ref[2 * run + h, :, place * total : (place + 1) * total] = moved[
                    :, h * total : (h + 1) * total
                ]

    return body


def finish(experts, capacity, replicas, far):
    part = replicas // 2
    height = part * capacity
    runs = 2

    def body(own_ref, wide_ref, hidden_ref, *refs):
        state_hbm, next_hbm = refs[:replicas], refs[replicas : 2 * replicas]
        out_ref, units_ref, state_ref, next_ref, gradient_ref, updated_ref, sems = refs[
            2 * replicas :
        ]
        total = wide_ref.shape[0] // experts
        run_rows = experts // runs * total
        state_rows = state_hbm[0].shape[0]
        rows = next_hbm[0].shape[0] - far
        count = experts // runs * height
        copies = [
            pltpu.make_async_copy(hidden_ref.at[i], units_ref.at[i], sems.at[i])
            for i in range(2 * runs)
        ]
        for r in range(replicas):
            place = pl.ds(r * state_rows, state_rows)
            copies.append(
                pltpu.make_async_copy(
                    state_hbm[r], state_ref.at[place], sems.at[2 * runs + r]
                )
            )
        for r in range(replicas):
            copies.append(
                pltpu.make_async_copy(
                    next_hbm[r].at[pl.ds(far, rows)],
                    next_ref.at[pl.ds(r * rows, rows)],
                    sems.at[2 * runs + replicas + r],
                )
            )
        for copy in copies:
            copy.start()
        for run in range(runs):
            received = wide_ref[run * run_rows : (run + 1) * run_rows, :]
            received = received.reshape(experts // runs, total, LANE)
            last = received[:, 2 * WIDE * height : total, :].reshape(count, LANE)
            for h in range(2):
                tiles = [
                    received[:, (h * WIDE + t) * height : (h * WIDE + t + 1) * height, :].reshape(
                        count, LANE
                    )
                    for t in range(WIDE)
                ]
                copies[2 * run + h].wait()
                product = jnp.dot(
                    units_ref[2 * run + h],
                    jnp.concatenate(tiles + [last], axis=1),
                    preferred_element_type=jnp.float32,
                )
                if h == 1:
                    turned = pltpu.roll(product[:, SPAN : SPAN + LANE], HALF, 1)
                    product = jnp.concatenate([product[:, :SPAN], turned], axis=1)
                if run == 0 and h == 0:
                    gradient_ref[...] = product
                else:
                    gradient_ref[...] += product
        slab = state_rows * 2 // (3 * (2 * WIDE + 1))
        piece = WIDE * slab + slab // 2
        for r in range(replicas):
            copies[2 * runs + r].wait()
            start = pl.multiple_of((own_ref[0] ^ r) * slab, slab)
            for t in range(WIDE + 1):
                state = []
                for a in range(3):
                    base = r * state_rows + a * piece + t * slab
                    if t < WIDE:
                        state.append(state_ref[base : base + slab, :])
                    else:
                        folded = state_ref[base : base + slab // 2, :].astype(jnp.float32)
                        state.append(
                            jnp.concatenate([folded, pltpu.roll(folded, HALF, 1)], axis=0)
                        )
                gradient = gradient_ref[pl.ds(start, slab), t * LANE : (t + 1) * LANE]
                updated_ref[pl.ds(start, slab), t * LANE : (t + 1) * LANE] = adamw(
                    *state, gradient
                )
        for copy in copies[2 * runs + replicas :]:
            copy.wait()
        result = jnp.dot(next_ref[...], updated_ref[...], preferred_element_type=jnp.float32)
        for r in range(replicas):
            start = pl.multiple_of((own_ref[0] ^ r) * rows, 16)
            out_ref[pl.ds(start, rows), :] = result[r * rows : (r + 1) * rows, :].astype(
                jnp.bfloat16
            )

    return body


def join_columns(replicas):
    def body(pieces_ref, out_ref):
        rows = out_ref.shape[0]
        left = iota((rows, LANE), 1) < HALF
        for j in range(replicas):
            out_ref[:, j * SPAN : (j + 1) * SPAN] = pieces_ref[j * rows : (j + 1) * rows, 0:SPAN]
            if j % 2 == 0:
                low, high = [
                    pieces_ref[(j + s) * rows : (j + s + 1) * rows, SPAN : SPAN + LANE].astype(
                        jnp.float32
                    )
                    for s in (0, 1)
                ]
                start = replicas * SPAN + (j // 2) * LANE
                out_ref[:, start : start + LANE] = jnp.where(
                    left, low, pltpu.roll(high, HALF, 1)
                ).astype(jnp.bfloat16)

    return body


def per_device(
    out_grad,
    expert_ids,
    combine,
    router_logits,
    saved_hidden,
    weight,
    moment_one,
    moment_two,
    next_hidden,
    interpret=False,
):
    experts = lax.axis_size("ep")
    replicas = lax.axis_size("dp")
    rows_total = saved_hidden.shape[1]
    capacity = rows_total // experts
    tokens = out_grad.shape[0]
    slab_rows = weight.shape[1]
    ff_width = saved_hidden.shape[2]
    next_rows = next_hidden.shape[1]
    part = replicas // 2
    message_rows = WIDE * tokens + tokens // 2 + META
    expert_rows = (2 * WIDE + 1) * part * capacity
    state_rows = 3 * (WIDE * slab_rows + slab_rows // 2)
    vmem = pl.BlockSpec(memory_space=pltpu.VMEM)
    smem = pl.BlockSpec(memory_space=pltpu.SMEM)
    hbm = pl.BlockSpec(memory_space=pl.ANY)
    own = lax.axis_index("dp").astype(jnp.int32).reshape(1)

    def near(value):
        return value if interpret else pltpu.with_memory_space_constraint(value, pltpu.VMEM)

    def call(body, ins, outs, scratch=(), scalar=False, local=False, last=False, specs=None):
        kind = pltpu.VMEM if local and not interpret and not last else jax.ShapeDtypeStruct
        shapes = [kind(shape, dtype) for shape, dtype in outs]
        single = len(shapes) == 1
        specs = specs or [vmem] * len(ins)
        if scalar:
            specs, ins = [smem] + specs, [own] + list(ins)
        return pl.pallas_call(
            body,
            out_shape=shapes[0] if single else tuple(shapes),
            in_specs=specs,
            out_specs=vmem if single else (vmem,) * len(shapes),
            scratch_shapes=list(scratch),
            compiler_params=pltpu.CompilerParams(vmem_limit_bytes=SCOPED if local else None),
            interpret=interpret,
        )(*ins)

    def send(value, r):
        return lax.ppermute(value, "dp", [(i, i ^ r) for i in range(replicas)])

    def tie(*values):
        return lax.optimization_barrier(values)

    def spread(value, pieces):
        if part != 4:
            return (
                [value] + [send(value, r) for r in range(1, replicas)],
                pieces[:1] + [send(pieces[r], r) for r in range(1, replicas)],
            )
        moved = {r: send(pieces[r], r) for r in (1, 3)}
        first = (send(value, 1), send(value, 3), send(value, part), moved[1], moved[3])
        near1, near3, far0, moved[1], moved[3], *pieces = tie(*first, *pieces)
        moved[4] = send(pieces[4], 4)
        far1, far3, near3, moved[4], *pieces = tie(
            send(far0, 1), send(far0, 3), near3, moved[4], *pieces
        )
        moved[2] = send(pieces[2], 2)
        near2, far2, moved[2], *pieces = tie(send(near3, 1), send(far1, 3), moved[2], *pieces)
        moved.update({r: send(pieces[r], r) for r in (6, 5, 7)})
        gathered = [value, near1, near2, near3, far0, far1, far2, far3]
        return gathered, pieces[:1] + [moved[r] for r in range(1, replicas)]

    def swap(value, axis):
        parts = lax.axis_size(axis)
        value = value.reshape(parts, value.shape[0] // parts, value.shape[1])
        value = lax.all_to_all(value, axis, split_axis=0, concat_axis=0, tiled=True)
        return value.reshape(-1, value.shape[2])

    half16 = jnp.bfloat16
    message = call(
        own_block(replicas),
        [expert_ids.T, combine.T, out_grad],
        [((replicas * message_rows, LANE), half16)],
        local=True,
    )
    message = swap(message, "dp")
    hidden = jnp.concatenate([saved_hidden[0], next_hidden[0]], axis=0)
    state = call(
        split_state(replicas),
        [weight[0], moment_one[0], moment_two[0]],
        [((state_rows, LANE), half16)] * replicas,
        scalar=True,
    )
    message, hidden, *state = tie(message, hidden, *state)
    wide = call(
        own_columns(experts, capacity, replicas, tokens, 8),
        [near(message)],
        [((experts * expert_rows, LANE), half16)],
        [
            pltpu.VMEM((replicas * tokens, SPAN + LANE), half16),
            pltpu.VMEM((2, replicas * tokens), jnp.int32),
            pltpu.VMEM((2, replicas * tokens), jnp.float32),
        ],
        local=True,
    )
    wide = swap(wide, "ep")
    hidden, state = spread(hidden, state)

    runs = 2
    ordered = call(
        order_hidden(experts, capacity, replicas, 8),
        hidden,
        [((2 * runs, ff_width, part * rows_total // runs), half16)],
        scalar=True,
    )
    result = call(
        finish(experts, capacity, replicas, rows_total),
        [near(wide), ordered] + state + hidden,
        [((replicas * next_rows, SPAN + LANE), half16)],
        [
            pltpu.VMEM((2 * runs, ff_width, part * rows_total // runs), half16),
            pltpu.VMEM((replicas * state_rows, LANE), half16),
            pltpu.VMEM((replicas * next_rows, ff_width), half16),
            pltpu.VMEM((ff_width, SPAN + LANE), jnp.float32),
            pltpu.VMEM((ff_width, SPAN + LANE), half16),
            pltpu.SemaphoreType.DMA((2 * runs + 2 * replicas,)),
        ],
        scalar=True,
        local=True,
        specs=[vmem] + [hbm] * (1 + 2 * replicas),
    )
    result = swap(result, "dp")
    refreshed = call(
        join_columns(replicas),
        [near(result)],
        [((next_rows, out_grad.shape[1]), half16)],
        local=True,
        last=True,
    )
    return (refreshed[None], zloss_grad(router_logits))


def solution(mesh):
    in_specs = (
        P(("ep", "dp"), None),
        P(("ep", "dp"), None),
        P(("ep", "dp"), None),
        P(("ep", "dp"), None),
        P("ep", "dp", None),
        P("ep", "dp", None),
        P("ep", "dp", None),
        P("ep", "dp", None),
        P("ep", "dp", None),
    )
    out_specs = (P("ep", "dp", None), P(("ep", "dp"), None))
    return jax.shard_map(
        per_device, mesh=mesh, in_specs=in_specs, out_specs=out_specs, check_vma=False
    )
```

time: 434 us -> 199 us (0.46)
  the two profiles are of different devices: /device:TPU:1 before, /device:TPU:8 now
where the time goes in v2:
time: 199 us; the launch traced here: 198 us
  waiting for transfers between devices  89.8 us (45%)
  starting transfers between devices  73.5 us (37%)
  Pallas kernels  32.1 us (16%)
  other arithmetic  2 us (1%)
    ppermute x14, waiting for transfers between devices, send(): return lax.ppermute(value, 'dp', [(i, i ^ r) for i in range(replicas)])  67.2 us
    ppermute x14, starting transfers between devices, send(): return lax.ppermute(value, 'dp', [(i, i ^ r) for i in range(replicas)])  46.5 us
    pallas_call x6, Pallas kernels, call(): pl.pallas_call(body, out_shape=shapes[0] if single else tuple(shapes), in...  32.1 us
    all_to_all x3, starting transfers between devices, swap(): value = lax.all_to_all(value, axis, split_axis=0, concat_axis=0, tiled=True)  26.9 us
    all_to_all x3, waiting for transfers between devices, swap(): value = lax.all_to_all(value, axis, split_axis=0, concat_axis=0, tiled=True)  22.5 us
  transfers between devices with their start and end apart: 17, of which 13 were waited for; matrix products, arithmetic and copies ran while one was open for 1% of the time, Pallas kernels for 7%

profile of v2, /device:TPU:8, one launch (start us, length us, event | category | flops | bytes accessed | tf_op | source)
XLA Modules:
  0.0 198.3 jit_solution(9338987131111072644)
XLA Ops:
  0.6 2.3 %shard_map.104 = bf16[3648,128]{1,0:T(8,128)(2,1)} custom-call(s32[2,128]{1,0:T(2,128)} %bitcast.24, f32[2,128]{1,0:T(2,128)} %bitcast.25, bf16[128,3584]{1,0:T(8,128)(2,1)} %grad_ref.1), custom_call_target="tpu_custom_call" | custom-call | tf_op jit(solution)/shard_map/pallas_call | solution.py:384
  3.0 0.0 copy-start.7
  3.0 0.0 copy-start.12
  3.0 6.2 %all-to-all-start = ((bf16[8,456,128]{2,1,0:T(8,128)(2,1)}), bf16[8,456,128]{2,1,0:T(8,128)(2,1)S(1)}, u32[]{:S(2)}, u32[]{:S(2)}) async-start(bf16[8,456,128]{2,1,0:T(8,128)(2,1)} %bitcast.3), calls=%async_computation | async-start | bytes 1867776 | tf_op jit(solution)/shard_map/all_to_all | solution.py:422
  9.1 3.9 %shard_map.105 = (bf16[1344,128]{1,0:T(8,128)(2,1)}, bf16[1344,128]{1,0:T(8,128)(2,1)}, bf16[1344,128]{1,0:T(8,128)(2,1)}, bf16[1344,128]{1,0:T(8,128)(2,1)}, bf...) custom-call(s32[1]{0:T(128)} %bitcast.own_ref, ...), custom_call_target="tpu_custom_call" | custom-call | tf_op jit(solution)/shard_map/pallas_call | solution.py:384
  13.0 0.0 copy-done.7
  13.0 0.0 copy-done.12
  13.0 1.0 pad_maximum_fusion.refs_0_.refs_8_
  14.0 11.1 %all-to-all-done = bf16[8,456,128]{2,1,0:T(8,128)(2,1)S(1)} async-done(((bf16[8,456,128]{2,1,0:T(8,128)(2,1)}), bf16[8,456,128]{2,1,0:T(8,128)(2,1)S(1)}, u32[]{:S(2)}, u32[]{:S(2)}) %all-to-all-start) | async-done | bytes 933920 | tf_op jit(solution)/shard_map/all_to_all | solution.py:422
  25.1 6.4 %shard_map.106 = bf16[10752,128]{1,0:T(8,128)(2,1)} custom-call(bf16[3648,128]{1,0:T(8,128)(2,1)S(1)} %bitcast.16), custom_call_target="tpu_custom_call" | custom-call | tf_op jit(solution)/shard_map/pallas_call | solution.py:384
  31.5 0.0 copy-start.6
  31.5 17.3 %all-to-all-start.1 = ((bf16[64,168,128]{2,1,0:T(8,128)(2,1)}), bf16[64,168,128]{2,1,0:T(8,128)(2,1)S(1)}, u32[]{:S(2)}, u32[]{:S(2)}) async-start(bf16[64,168,128]{2,1,0:T(8,128)(2,1)} %bitcast.10), calls=%async_computation.1 | async-start | bytes 5505024 | tf_op jit(solution)/shard_map/all_to_all | solution.py:422
  48.9 2.8 %collective-permute-start = (bf16[416,1024]{1,0:T(8,128)(2,1)}, bf16[416,1024]{1,0:T(8,128)(2,1)}, u32[]{:S(2)}, u32[]{:S(2)}) collective-permute-start(bf16[416,1024]{1,0:T(8,128)(2,1)} %pad_maximum_fusion.refs_0_.refs_8_), channel_id=1, source_target_pairs={{0,1},{1,0},{2,3},{3,2},{4,5},{5,4},{6,7},{7,6},{8,9},{9,8},{10,11... | collective-permute-start | bytes 2555912 | tf_op jit(solution)/shard_map/ppermute | solution.py:395
  51.6 2.5 %collective-permute-start.1 = (bf16[416,1024]{1,0:T(8,128)(2,1)}, bf16[416,1024]{1,0:T(8,128)(2,1)S(1)}, u32[]{:S(2)}, u32[]{:S(2)}) collective-permute-start(bf16[416,1024]{1,0:T(8,128)(2,1)} %pad_maximum_fusion.refs_0_.refs_8_), channel_id=1, source_target_pairs={{0,3},{1,2},{2,1},{3,0},{4,7},{5,6},{6,5},{7,4},{8,11},{9,10},{10,... | collective-permute-start | bytes 2555912 | tf_op jit(solution)/shard_map/ppermute | solution.py:395
  54.1 2.5 %collective-permute-start.2 = (bf16[416,1024]{1,0:T(8,128)(2,1)}, bf16[416,1024]{1,0:T(8,128)(2,1)S(1)}, u32[]{:S(2)}, u32[]{:S(2)}) collective-permute-start(bf16[416,1024]{1,0:T(8,128)(2,1)} %pad_maximum_fusion.refs_0_.refs_8_), channel_id=1, source_target_pairs={{0,4},{1,5},{2,6},{3,7},{4,0},{5,1},{6,2},{7,3},{8,12},{9,13},{10,... | collective-permute-start | bytes 2555912 | tf_op jit(solution)/shard_map/ppermute | solution.py:395
  56.6 3.3 %collective-permute-start.3 = (bf16[1344,128]{1,0:T(8,128)(2,1)}, bf16[1344,128]{1,0:T(8,128)(2,1)S(1)}, u32[]{:S(2)}, u32[]{:S(2)}) collective-permute-start(bf16[1344,128]{1,0:T(8,128)(2,1)} %get-tuple-element.57), channel_id=1, source_target_pairs={{0,1},{1,0},{2,3},{3,2},{4,5},{5,4},{6,7},{7,6},{8,9},{9,8},{10,11... | collective-permute-start | bytes 1032200 | tf_op jit(solution)/shard_map/ppermute | solution.py:395
  60.0 3.7 %collective-permute-start.4 = (bf16[1344,128]{1,0:T(8,128)(2,1)}, bf16[1344,128]{1,0:T(8,128)(2,1)S(1)}, u32[]{:S(2)}, u32[]{:S(2)}) collective-permute-start(bf16[1344,128]{1,0:T(8,128)(2,1)} %get-tuple-element.58), channel_id=1, source_target_pairs={{0,3},{1,2},{2,1},{3,0},{4,7},{5,6},{6,5},{7,4},{8,11},{9,10},{10,... | collective-permute-start | bytes 1032200 | tf_op jit(solution)/shard_map/ppermute | solution.py:395
  63.7 15.7 %collective-permute-done.3.refs_1_ = bf16[1344,128]{1,0:T(8,128)(2,1)S(1)} collective-permute-done((bf16[1344,128]{1,0:T(8,128)(2,1)}, bf16[1344,128]{1,0:T(8,128)(2,1)S(1)}, u32[]{:S(2)}, u32[]{:S(2)}) %collective-permute-start.3) | collective-permute-done | bytes 344096 | tf_op jit(solution)/shard_map/ppermute | solution.py:395
  79.3 0.0 copy-start.8
  79.3 3.7 %collective-permute-done.4.refs_3_ = bf16[1344,128]{1,0:T(8,128)(2,1)S(1)} collective-permute-done((bf16[1344,128]{1,0:T(8,128)(2,1)}, bf16[1344,128]{1,0:T(8,128)(2,1)S(1)}, u32[]{:S(2)}, u32[]{:S(2)}) %collective-permute-start.4) | collective-permute-done | bytes 344096 | tf_op jit(solution)/shard_map/ppermute | solution.py:395
  83.0 0.0 collective-permute-done.refs_1_.refs_9_
  83.0 0.0 collective-permute-done.1.refs_3_.refs_11_
  83.0 0.0 copy-start
  83.1 0.0 collective-permute-done.2.refs_4_.refs_12_
  83.1 0.0 copy-start.1
  83.1 2.2 %collective-permute-start.5 = (bf16[416,1024]{1,0:T(8,128)(2,1)S(1)}, bf16[416,1024]{1,0:T(8,128)(2,1)S(1)}, u32[]{:S(2)}, u32[]{:S(2)}) collective-permute-start(bf16[416,1024]{1,0:T(8,128)(2,1)S(1)} %collective-permute-done.2.refs_4_.refs_12_), channel_id=1, source_target_pairs={{0,1},{1,0},{2,3},{3,2},{4,5},{5,4},{6,7},{7,6},{8,9},{9,8},{10,11... | collective-permute-start | bytes 2555912 | tf_op jit(solution)/shard_map/ppermute | solution.py:395
  85.3 3.9 %collective-permute-start.6 = (bf16[416,1024]{1,0:T(8,128)(2,1)S(1)}, bf16[416,1024]{1,0:T(8,128)(2,1)S(1)}, u32[]{:S(2)}, u32[]{:S(2)}) collective-permute-start(bf16[416,1024]{1,0:T(8,128)(2,1)S(1)} %collective-permute-done.2.refs_4_.refs_12_), channel_id=1, source_target_pairs={{0,3},{1,2},{2,1},{3,0},{4,7},{5,6},{6,5},{7,4},{8,11},{9,10},{10,... | collective-permute-start | bytes 2555912 | tf_op jit(solution)/shard_map/ppermute | solution.py:395
  89.3 2.8 %collective-permute-start.7 = (bf16[1344,128]{1,0:T(8,128)(2,1)}, bf16[1344,128]{1,0:T(8,128)(2,1)S(1)}, u32[]{:S(2)}, u32[]{:S(2)}) collective-permute-start(bf16[1344,128]{1,0:T(8,128)(2,1)} %get-tuple-element.68), channel_id=1, source_target_pairs={{0,4},{1,5},{2,6},{3,7},{4,0},{5,1},{6,2},{7,3},{8,12},{9,13},{10,... | collective-permute-start | bytes 1032200 | tf_op jit(solution)/shard_map/ppermute | solution.py:395
  92.0 11.8 %collective-permute-done.7.refs_4_ = bf16[1344,128]{1,0:T(8,128)(2,1)S(1)} collective-permute-done((bf16[1344,128]{1,0:T(8,128)(2,1)}, bf16[1344,128]{1,0:T(8,128)(2,1)S(1)}, u32[]{:S(2)}, u32[]{:S(2)}) %collective-permute-start.7) | collective-permute-done | bytes 344096 | tf_op jit(solution)/shard_map/ppermute | solution.py:395
  103.8 1.0 collective-permute-done.5.refs_5_.refs_13_
  104.8 0.0 copy-done.10
  104.8 3.5 %collective-permute-done.6.refs_7_.refs_15_ = bf16[416,1024]{1,0:T(8,128)(2,1)S(1)} collective-permute-done((bf16[416,1024]{1,0:T(8,128)(2,1)S(1)}, bf16[416,1024]{1,0:T(8,128)(2,1)S(1)}, u32[]{:S(2)}, u32[]{:S(2)}) %collective-permute-start.6) | collective-permute-done | bytes 852000 | tf_op jit(solution)/shard_map/ppermute | solution.py:395
  108.3 0.0 copy-done
  108.3 2.1 %collective-permute-start.8 = (bf16[416,1024]{1,0:T(8,128)(2,1)S(1)}, bf16[416,1024]{1,0:T(8,128)(2,1)S(1)}, u32[]{:S(2)}, u32[]{:S(2)}) collective-permute-start(bf16[416,1024]{1,0:T(8,128)(2,1)S(1)} %collective-permute-done.1.refs_3_.refs_11_), channel_id=1, source_target_pairs={{0,1},{1,0},{2,3},{3,2},{4,5},{5,4},{6,7},{7,6},{8,9},{9,8},{10,11... | collective-permute-start | bytes 2555912 | tf_op jit(solution)/shard_map/ppermute | solution.py:395
  110.4 4.1 %collective-permute-start.9 = (bf16[416,1024]{1,0:T(8,128)(2,1)S(1)}, bf16[416,1024]{1,0:T(8,128)(2,1)S(1)}, u32[]{:S(2)}, u32[]{:S(2)}) collective-permute-start(bf16[416,1024]{1,0:T(8,128)(2,1)S(1)} %collective-permute-done.5.refs_5_.refs_13_), channel_id=1, source_target_pairs={{0,3},{1,2},{2,1},{3,0},{4,7},{5,6},{6,5},{7,4},{8,11},{9,10},{10,... | collective-permute-start | bytes 2555912 | tf_op jit(solution)/shard_map/ppermute | solution.py:395
  114.6 3.6 %collective-permute-start.10 = (bf16[1344,128]{1,0:T(8,128)(2,1)}, bf16[1344,128]{1,0:T(8,128)(2,1)S(1)}, u32[]{:S(2)}, u32[]{:S(2)}) collective-permute-start(bf16[1344,128]{1,0:T(8,128)(2,1)} %get-tuple-element.76), channel_id=1, source_target_pairs={{0,2},{1,3},{2,0},{3,1},{4,6},{5,7},{6,4},{7,5},{8,10},{9,11},{10,... | collective-permute-start | bytes 1032200 | tf_op jit(solution)/shard_map/ppermute | solution.py:395
  118.1 20.2 %collective-permute-done.10.refs_2_ = bf16[1344,128]{1,0:T(8,128)(2,1)S(1)} collective-permute-done((bf16[1344,128]{1,0:T(8,128)(2,1)}, bf16[1344,128]{1,0:T(8,128)(2,1)S(1)}, u32[]{:S(2)}, u32[]{:S(2)}) %collective-permute-start.10) | collective-permute-done | bytes 344096 | tf_op jit(solution)/shard_map/ppermute | solution.py:395
  138.3 0.0 collective-permute-done.8.refs_2_.refs_10_
  138.3 0.0 copy-done.1
  138.3 0.0 copy-start.4
  138.3 1.4 collective-permute-done.9.refs_6_.refs_14_
  139.6 0.0 copy-done.2
  139.7 2.1 %collective-permute-start.11 = (bf16[1344,128]{1,0:T(8,128)(2,1)}, bf16[1344,128]{1,0:T(8,128)(2,1)}, u32[]{:S(2)}, u32[]{:S(2)}) collective-permute-start(bf16[1344,128]{1,0:T(8,128)(2,1)} %get-tuple-element.89), channel_id=1, source_target_pairs={{0,5},{1,4},{2,7},{3,6},{4,1},{5,0},{6,3},{7,2},{8,13},{9,12},{10,... | collective-permute-start | bytes 1032200 | tf_op jit(solution)/shard_map/ppermute | solution.py:395
  141.7 0.0 copy-done.3
  141.8 7.8 %collective-permute-start.12 = (bf16[1344,128]{1,0:T(8,128)(2,1)}, bf16[1344,128]{1,0:T(8,128)(2,1)}, u32[]{:S(2)}, u32[]{:S(2)}) collective-permute-start(bf16[1344,128]{1,0:T(8,128)(2,1)} %get-tuple-element.90), channel_id=1, source_target_pairs={{0,6},{1,7},{2,4},{3,5},{4,2},{5,3},{6,0},{7,1},{8,14},{9,15},{10,... | collective-permute-start | bytes 1032200 | tf_op jit(solution)/shard_map/ppermute | solution.py:395
  149.6 0.0 copy-done.11
  149.6 0.0 copy-done.4
  149.6 0.0 copy-done.5
  149.6 3.1 %collective-permute-start.13 = (bf16[1344,128]{1,0:T(8,128)(2,1)}, bf16[1344,128]{1,0:T(8,128)(2,1)}, u32[]{:S(2)}, u32[]{:S(2)}) collective-permute-start(bf16[1344,128]{1,0:T(8,128)(2,1)} %get-tuple-element.91), channel_id=1, source_target_pairs={{0,7},{1,6},{2,5},{3,4},{4,3},{5,2},{6,1},{7,0},{8,15},{9,14},{10,... | collective-permute-start | bytes 1032200 | tf_op jit(solution)/shard_map/ppermute | solution.py:395
  152.8 0.0 copy-done.6
  152.8 0.1 reduce_max.14
  152.9 0.2 fusion.1
  153.1 9.6 %shard_map.107.hidden_ref = bf16[4,1024,768]{2,1,0:T(8,128)(2,1)} custom-call(s32[1]{0:T(128)} %bitcast.own_ref, bf16[416,1024]{1,0:T(8,128)(2,1)} %pad_maximum_fusion.refs_0_.refs_8_, bf16[416,1024]{1,0:T(8,128)(2,1)} %collective-permute-done.refs_1_.refs_9_, bf16[416,1024]{1,0:T(8,128)(2,1)} %copy-done.4, bf16[416,1024]{1,0:T(8,128)(2,1)} %copy-done, ...), custom_call_target="tpu_custom_call" | custom-call | tf_op jit(solution)/shard_map/pallas_call | solution.py:384
  162.7 0.1 collective-permute-done.11.refs_5_
  162.8 5.0 %collective-permute-done.12.refs_6_ = bf16[1344,128]{1,0:T(8,128)(2,1)} collective-permute-done((bf16[1344,128]{1,0:T(8,128)(2,1)}, bf16[1344,128]{1,0:T(8,128)(2,1)}, u32[]{:S(2)}, u32[]{:S(2)}) %collective-permute-start.12) | collective-permute-done | bytes 344096 | tf_op jit(solution)/shard_map/ppermute | solution.py:395
  167.9 5.0 %collective-permute-done.13.refs_7_ = bf16[1344,128]{1,0:T(8,128)(2,1)} collective-permute-done((bf16[1344,128]{1,0:T(8,128)(2,1)}, bf16[1344,128]{1,0:T(8,128)(2,1)}, u32[]{:S(2)}, u32[]{:S(2)}) %collective-permute-start.13) | collective-permute-done | bytes 344096 | tf_op jit(solution)/shard_map/ppermute | solution.py:395
  172.8 3.4 %all-to-all-done.1 = bf16[64,168,128]{2,1,0:T(8,128)(2,1)S(1)} async-done(((bf16[64,168,128]{2,1,0:T(8,128)(2,1)}), bf16[64,168,128]{2,1,0:T(8,128)(2,1)S(1)}, u32[]{:S(2)}, u32[]{:S(2)}) %all-to-all-start.1) | async-done | bytes 2752544 | tf_op jit(solution)/shard_map/all_to_all | solution.py:422
  176.2 0.0 copy-done.8
  176.2 0.0 copy-done.9
  176.2 9.1 %shard_map.108 = bf16[256,512]{1,0:T(8,128)(2,1)} custom-call(s32[1]{0:T(128)} %bitcast.own_ref, bf16[10752,128]{1,0:T(8,128)(2,1)S(1)} %bitcast.15, bf16[4,1024,768]{2,1,0:T(8,128)(2,1)} %shard_map.107.hidden_ref, bf16[1344,128]{1,0:T(8,128)(2,1)} %get-tuple-element.84.refs_0_, bf16[1344,128]{1,0:T(8,128)(2,1)} %copy-done.8, bf16[1344,128]{1,0:T(8,128)(2,1)} %copy-done.11, ...), custom_call_target="tpu_custom_call" | custom-call | tf_op jit(solution)/shard_map/pallas_call | solution.py:384
  185.4 3.4 %all-to-all-start.2 = ((bf16[8,32,512]{2,1,0:T(8,128)(2,1)}), bf16[8,32,512]{2,1,0:T(8,128)(2,1)S(1)}, u32[]{:S(2)}, u32[]{:S(2)}) async-start(bf16[8,32,512]{2,1,0:T(8,128)(2,1)} %bitcast.12), calls=%async_computation.2 | async-start | bytes 524288 | tf_op jit(solution)/shard_map/all_to_all | solution.py:422
  188.8 0.7 fusion.4
  189.5 8.0 %all-to-all-done.2 = bf16[8,32,512]{2,1,0:T(8,128)(2,1)S(1)} async-done(((bf16[8,32,512]{2,1,0:T(8,128)(2,1)}), bf16[8,32,512]{2,1,0:T(8,128)(2,1)S(1)}, u32[]{:S(2)}, u32[]{:S(2)}) %all-to-all-start.2) | async-done | bytes 262176 | tf_op jit(solution)/shard_map/all_to_all | solution.py:422
  197.5 0.8 shard_map.109
  (8 shorter events, 0.0 us)
Async XLA Ops:
  3.0 10.0 %copy-start.7 = (bf16[1,384,1024]{2,1,0:T(8,128)(2,1)S(1)}, bf16[1,384,1024]{2,1,0:T(8,128)(2,1)}, u32[]{:S(2)}) copy-start(bf16[1,384,1024]{2,1,0:T(8,128)(2,1)} %param.13) | copy-start | bytes 2359300
  3.0 10.0 %copy-start.12 = (bf16[1,32,1024]{2,1,0:T(8,128)(2,1)S(1)}, bf16[1,32,1024]{2,1,0:T(8,128)(2,1)}, u32[]{:S(2)}) copy-start(bf16[1,32,1024]{2,1,0:T(8,128)(2,1)} %param.17) | copy-start | bytes 196612
  3.0 22.1 %all-to-all-start = ((bf16[8,456,128]{2,1,0:T(8,128)(2,1)}), bf16[8,456,128]{2,1,0:T(8,128)(2,1)S(1)}, u32[]{:S(2)}, u32[]{:S(2)}) async-start(bf16[8,456,128]{2,1,0:T(8,128)(2,1)} %bitcast.3), calls=%async_computation | async-start | bytes 1867776 | tf_op jit(solution)/shard_map/all_to_all | solution.py:422
  31.5 121.3 %copy-start.6 = (bf16[128,384]{1,0:T(8,128)(2,1)S(1)}, bf16[128,384]{1,0:T(8,128)(2,1)}, u32[]{:S(2)}) copy-start(bf16[128,384]{1,0:T(8,128)(2,1)} %param.12) | copy-start | bytes 294916
  31.5 144.7 %all-to-all-start.1 = ((bf16[64,168,128]{2,1,0:T(8,128)(2,1)}), bf16[64,168,128]{2,1,0:T(8,128)(2,1)S(1)}, u32[]{:S(2)}, u32[]{:S(2)}) async-start(bf16[64,168,128]{2,1,0:T(8,128)(2,1)} %bitcast.10), calls=%async_computation.1 | async-start | bytes 5505024 | tf_op jit(solution)/shard_map/all_to_all | solution.py:422
  48.9 34.2 %collective-permute-start = (bf16[416,1024]{1,0:T(8,128)(2,1)}, bf16[416,1024]{1,0:T(8,128)(2,1)}, u32[]{:S(2)}, u32[]{:S(2)}) collective-permute-start(bf16[416,1024]{1,0:T(8,128)(2,1)} %pad_maximum_fusion.refs_0_.refs_8_), channel_id=1, source_target_pairs={{0,1},{1,0},{2,3},{3,2},{4,5},{5,4},{6,7},{7,6},{8,9},{9,8},{10,11... | collective-permute-start | bytes 2555912 | tf_op jit(solution)/shard_map/ppermute | solution.py:395
  51.6 31.4 %collective-permute-start.1 = (bf16[416,1024]{1,0:T(8,128)(2,1)}, bf16[416,1024]{1,0:T(8,128)(2,1)S(1)}, u32[]{:S(2)}, u32[]{:S(2)}) collective-permute-start(bf16[416,1024]{1,0:T(8,128)(2,1)} %pad_maximum_fusion.refs_0_.refs_8_), channel_id=1, source_target_pairs={{0,3},{1,2},{2,1},{3,0},{4,7},{5,6},{6,5},{7,4},{8,11},{9,10},{10,... | collective-permute-start | bytes 2555912 | tf_op jit(solution)/shard_map/ppermute | solution.py:395
  54.1 29.0 %collective-permute-start.2 = (bf16[416,1024]{1,0:T(8,128)(2,1)}, bf16[416,1024]{1,0:T(8,128)(2,1)S(1)}, u32[]{:S(2)}, u32[]{:S(2)}) collective-permute-start(bf16[416,1024]{1,0:T(8,128)(2,1)} %pad_maximum_fusion.refs_0_.refs_8_), channel_id=1, source_target_pairs={{0,4},{1,5},{2,6},{3,7},{4,0},{5,1},{6,2},{7,3},{8,12},{9,13},{10,... | collective-permute-start | bytes 2555912 | tf_op jit(solution)/shard_map/ppermute | solution.py:395
  56.6 22.7 %collective-permute-start.3 = (bf16[1344,128]{1,0:T(8,128)(2,1)}, bf16[1344,128]{1,0:T(8,128)(2,1)S(1)}, u32[]{:S(2)}, u32[]{:S(2)}) collective-permute-start(bf16[1344,128]{1,0:T(8,128)(2,1)} %get-tuple-element.57), channel_id=1, source_target_pairs={{0,1},{1,0},{2,3},{3,2},{4,5},{5,4},{6,7},{7,6},{8,9},{9,8},{10,11... | collective-permute-start | bytes 1032200 | tf_op jit(solution)/shard_map/ppermute | solution.py:395
  60.0 23.1 %collective-permute-start.4 = (bf16[1344,128]{1,0:T(8,128)(2,1)}, bf16[1344,128]{1,0:T(8,128)(2,1)S(1)}, u32[]{:S(2)}, u32[]{:S(2)}) collective-permute-start(bf16[1344,128]{1,0:T(8,128)(2,1)} %get-tuple-element.58), channel_id=1, source_target_pairs={{0,3},{1,2},{2,1},{3,0},{4,7},{5,6},{6,5},{7,4},{8,11},{9,10},{10,... | collective-permute-start | bytes 1032200 | tf_op jit(solution)/shard_map/ppermute | solution.py:395
  79.3 96.9 %copy-start.8 = (bf16[1344,128]{1,0:T(8,128)(2,1)}, bf16[1344,128]{1,0:T(8,128)(2,1)S(1)}, u32[]{:S(2)}) copy-start(bf16[1344,128]{1,0:T(8,128)(2,1)S(1)} %collective-permute-done.3.refs_1_) | copy-start | bytes 1032196
  83.0 93.2 %copy-start.9 = (bf16[1344,128]{1,0:T(8,128)(2,1)}, bf16[1344,128]{1,0:T(8,128)(2,1)S(1)}, u32[]{:S(2)}) copy-start(bf16[1344,128]{1,0:T(8,128)(2,1)S(1)} %collective-permute-done.4.refs_3_) | copy-start | bytes 1032196
  83.0 25.2 %copy-start = (bf16[416,1024]{1,0:T(8,128)(2,1)}, bf16[416,1024]{1,0:T(8,128)(2,1)S(1)}, u32[]{:S(2)}) copy-start(bf16[416,1024]{1,0:T(8,128)(2,1)S(1)} %collective-permute-done.1.refs_3_.refs_11_) | copy-start | bytes 2555908
  83.1 55.2 %copy-start.1 = (bf16[416,1024]{1,0:T(8,128)(2,1)}, bf16[416,1024]{1,0:T(8,128)(2,1)S(1)}, u32[]{:S(2)}) copy-start(bf16[416,1024]{1,0:T(8,128)(2,1)S(1)} %collective-permute-done.2.refs_4_.refs_12_) | copy-start | bytes 2555908
  83.1 21.7 %collective-permute-start.5 = (bf16[416,1024]{1,0:T(8,128)(2,1)S(1)}, bf16[416,1024]{1,0:T(8,128)(2,1)S(1)}, u32[]{:S(2)}, u32[]{:S(2)}) collective-permute-start(bf16[416,1024]{1,0:T(8,128)(2,1)S(1)} %collective-permute-done.2.refs_4_.refs_12_), channel_id=1, source_target_pairs={{0,1},{1,0},{2,3},{3,2},{4,5},{5,4},{6,7},{7,6},{8,9},{9,8},{10,11... | collective-permute-start | bytes 2555912 | tf_op jit(solution)/shard_map/ppermute | solution.py:395
  85.3 23.0 %collective-permute-start.6 = (bf16[416,1024]{1,0:T(8,128)(2,1)S(1)}, bf16[416,1024]{1,0:T(8,128)(2,1)S(1)}, u32[]{:S(2)}, u32[]{:S(2)}) collective-permute-start(bf16[416,1024]{1,0:T(8,128)(2,1)S(1)} %collective-permute-done.2.refs_4_.refs_12_), channel_id=1, source_target_pairs={{0,3},{1,2},{2,1},{3,0},{4,7},{5,6},{6,5},{7,4},{8,11},{9,10},{10,... | collective-permute-start | bytes 2555912 | tf_op jit(solution)/shard_map/ppermute | solution.py:395
  89.3 14.5 %collective-permute-start.7 = (bf16[1344,128]{1,0:T(8,128)(2,1)}, bf16[1344,128]{1,0:T(8,128)(2,1)S(1)}, u32[]{:S(2)}, u32[]{:S(2)}) collective-permute-start(bf16[1344,128]{1,0:T(8,128)(2,1)} %get-tuple-element.68), channel_id=1, source_target_pairs={{0,4},{1,5},{2,6},{3,7},{4,0},{5,1},{6,2},{7,3},{8,12},{9,13},{10,... | collective-permute-start | bytes 1032200 | tf_op jit(solution)/shard_map/ppermute | solution.py:395
  103.8 1.0 copy-start.10
  104.8 34.8 %copy-start.2 = (bf16[416,1024]{1,0:T(8,128)(2,1)}, bf16[416,1024]{1,0:T(8,128)(2,1)S(1)}, u32[]{:S(2)}) copy-start(bf16[416,1024]{1,0:T(8,128)(2,1)S(1)} %collective-permute-done.5.refs_5_.refs_13_) | copy-start | bytes 2555908
  108.3 33.5 %copy-start.3 = (bf16[416,1024]{1,0:T(8,128)(2,1)}, bf16[416,1024]{1,0:T(8,128)(2,1)S(1)}, u32[]{:S(2)}) copy-start(bf16[416,1024]{1,0:T(8,128)(2,1)S(1)} %collective-permute-done.6.refs_7_.refs_15_) | copy-start | bytes 2555908
  108.3 30.0 %collective-permute-start.8 = (bf16[416,1024]{1,0:T(8,128)(2,1)S(1)}, bf16[416,1024]{1,0:T(8,128)(2,1)S(1)}, u32[]{:S(2)}, u32[]{:S(2)}) collective-permute-start(bf16[416,1024]{1,0:T(8,128)(2,1)S(1)} %collective-permute-done.1.refs_3_.refs_11_), channel_id=1, source_target_pairs={{0,1},{1,0},{2,3},{3,2},{4,5},{5,4},{6,7},{7,6},{8,9},{9,8},{10,11... | collective-permute-start | bytes 2555912 | tf_op jit(solution)/shard_map/ppermute | solution.py:395
  110.4 29.2 %collective-permute-start.9 = (bf16[416,1024]{1,0:T(8,128)(2,1)S(1)}, bf16[416,1024]{1,0:T(8,128)(2,1)S(1)}, u32[]{:S(2)}, u32[]{:S(2)}) collective-permute-start(bf16[416,1024]{1,0:T(8,128)(2,1)S(1)} %collective-permute-done.5.refs_5_.refs_13_), channel_id=1, source_target_pairs={{0,3},{1,2},{2,1},{3,0},{4,7},{5,6},{6,5},{7,4},{8,11},{9,10},{10,... | collective-permute-start | bytes 2555912 | tf_op jit(solution)/shard_map/ppermute | solution.py:395
  114.6 23.7 %collective-permute-start.10 = (bf16[1344,128]{1,0:T(8,128)(2,1)}, bf16[1344,128]{1,0:T(8,128)(2,1)S(1)}, u32[]{:S(2)}, u32[]{:S(2)}) collective-permute-start(bf16[1344,128]{1,0:T(8,128)(2,1)} %get-tuple-element.76), channel_id=1, source_target_pairs={{0,2},{1,3},{2,0},{3,1},{4,6},{5,7},{6,4},{7,5},{8,10},{9,11},{10,... | collective-permute-start | bytes 1032200 | tf_op jit(solution)/shard_map/ppermute | solution.py:395
  138.3 11.3 %copy-start.11 = (bf16[1344,128]{1,0:T(8,128)(2,1)}, bf16[1344,128]{1,0:T(8,128)(2,1)S(1)}, u32[]{:S(2)}) copy-start(bf16[1344,128]{1,0:T(8,128)(2,1)S(1)} %collective-permute-done.10.refs_2_) | copy-start | bytes 1032196
  138.3 11.3 %copy-start.4 = (bf16[416,1024]{1,0:T(8,128)(2,1)}, bf16[416,1024]{1,0:T(8,128)(2,1)S(1)}, u32[]{:S(2)}) copy-start(bf16[416,1024]{1,0:T(8,128)(2,1)S(1)} %collective-permute-done.8.refs_2_.refs_10_) | copy-start | bytes 2555908
  139.6 9.9 %copy-start.5 = (bf16[416,1024]{1,0:T(8,128)(2,1)}, bf16[416,1024]{1,0:T(8,128)(2,1)S(1)}, u32[]{:S(2)}) copy-start(bf16[416,1024]{1,0:T(8,128)(2,1)S(1)} %collective-permute-done.9.refs_6_.refs_14_) | copy-start | bytes 2555908
  139.7 23.2 %collective-permute-start.11 = (bf16[1344,128]{1,0:T(8,128)(2,1)}, bf16[1344,128]{1,0:T(8,128)(2,1)}, u32[]{:S(2)}, u32[]{:S(2)}) collective-permute-start(bf16[1344,128]{1,0:T(8,128)(2,1)} %get-tuple-element.89), channel_id=1, source_target_pairs={{0,5},{1,4},{2,7},{3,6},{4,1},{5,0},{6,3},{7,2},{8,13},{9,12},{10,... | collective-permute-start | bytes 1032200 | tf_op jit(solution)/shard_map/ppermute | solution.py:395
  141.8 26.1 %collective-permute-start.12 = (bf16[1344,128]{1,0:T(8,128)(2,1)}, bf16[1344,128]{1,0:T(8,128)(2,1)}, u32[]{:S(2)}, u32[]{:S(2)}) collective-permute-start(bf16[1344,128]{1,0:T(8,128)(2,1)} %get-tuple-element.90), channel_id=1, source_target_pairs={{0,6},{1,7},{2,4},{3,5},{4,2},{5,3},{6,0},{7,1},{8,14},{9,15},{10,... | collective-permute-start | bytes 1032200 | tf_op jit(solution)/shard_map/ppermute | solution.py:395
  149.6 23.2 %collective-permute-start.13 = (bf16[1344,128]{1,0:T(8,128)(2,1)}, bf16[1344,128]{1,0:T(8,128)(2,1)}, u32[]{:S(2)}, u32[]{:S(2)}) collective-permute-start(bf16[1344,128]{1,0:T(8,128)(2,1)} %get-tuple-element.91), channel_id=1, source_target_pairs={{0,7},{1,6},{2,5},{3,4},{4,3},{5,2},{6,1},{7,0},{8,15},{9,14},{10,... | collective-permute-start | bytes 1032200 | tf_op jit(solution)/shard_map/ppermute | solution.py:395
  185.4 12.2 %all-to-all-start.2 = ((bf16[8,32,512]{2,1,0:T(8,128)(2,1)}), bf16[8,32,512]{2,1,0:T(8,128)(2,1)S(1)}, u32[]{:S(2)}, u32[]{:S(2)}) async-start(bf16[8,32,512]{2,1,0:T(8,128)(2,1)} %bitcast.12), calls=%async_computation.2 | async-start | bytes 524288 | tf_op jit(solution)/shard_map/all_to_all | solution.py:422

commit v3 on v2

--- a/solution.py
+++ b/solution.py
@@ -174,7 +174,10 @@
 
 def split_state(replicas):
     def body(own_ref, *refs):
-        inputs, outputs = refs[:3], refs[3:]
+        inputs, outputs = refs[:3], list(refs[3:])
+        part = replicas // 2
+        size = outputs[0].shape[0]
+        outputs += [outputs[part].at[pl.ds(r * size, size)] for r in range(1, part)]
         for a in range(3):
             rows = inputs[a].shape[0]
             height = WIDE * rows + rows // 2
@@ -397,24 +400,23 @@
     def tie(*values):
         return lax.optimization_barrier(values)
 
-    def spread(value, pieces):
+    def spread(value, pieces, across):
         if part != 4:
-            return (
-                [value] + [send(value, r) for r in range(1, replicas)],
-                pieces[:1] + [send(pieces[r], r) for r in range(1, replicas)],
-            )
+            return [value, send(value, part)], [pieces[0], send(across, part)]
+        first = (send(value, part), send(value, 1), send(value, 3))
         moved = {r: send(pieces[r], r) for r in (1, 3)}
-        first = (send(value, 1), send(value, 3), send(value, part), moved[1], moved[3])
-        near1, near3, far0, moved[1], moved[3], *pieces = tie(*first, *pieces)
-        moved[4] = send(pieces[4], 4)
-        far1, far3, near3, moved[4], *pieces = tie(
-            send(far0, 1), send(far0, 3), near3, moved[4], *pieces
+        far0, near1, near3, moved[1], moved[3], across, last = tie(
+            *first, moved[1], moved[3], across, pieces[2]
         )
-        moved[2] = send(pieces[2], 2)
-        near2, far2, moved[2], *pieces = tie(send(near3, 1), send(far1, 3), moved[2], *pieces)
-        moved.update({r: send(pieces[r], r) for r in (6, 5, 7)})
+        far1, far3, across = send(far0, 1), send(far0, 3), send(across, part)
+        far1, far3, near3, last = tie(far1, far3, near3, last)
+        far2, near2 = send(far1, 3), send(near3, 1)
+        far2, near2, across, last = tie(far2, near2, across, last)
+        across = [across[q * state_rows : (q + 1) * state_rows] for q in range(part)]
+        moved.update({0: pieces[0], 2: send(last, 2), 4: across[0]})
+        moved.update({part + q: send(across[q], q) for q in (1, 3, 2)})
         gathered = [value, near1, near2, near3, far0, far1, far2, far3]
-        return gathered, pieces[:1] + [moved[r] for r in range(1, replicas)]
+        return gathered, [moved[r] for r in range(replicas)]
 
     def swap(value, axis):
         parts = lax.axis_size(axis)
@@ -434,7 +436,7 @@
     state = call(
         split_state(replicas),
         [weight[0], moment_one[0], moment_two[0]],
-        [((state_rows, LANE), half16)] * replicas,
+        [((state_rows, LANE), half16)] * part + [((part * state_rows, LANE), half16)],
         scalar=True,
     )
     message, hidden, *state = tie(message, hidden, *state)
@@ -450,7 +452,7 @@
         local=True,
     )
     wide = swap(wide, "ep")
-    hidden, state = spread(hidden, state)
+    hidden, state = spread(hidden, state[:part], state[part])
 
     runs = 2
     ordered = call(

time: 199 us -> 197 us (0.990)
  local copies, waits for them, and re-layouts: 0.05 us -> 3.59 us
  starting transfers between devices: 73.5 us -> 70.2 us
  waiting for transfers between devices: 89.8 us -> 87.2 us
    ppermute x14, waiting for transfers between devices: 67.2 us -> 54.5 us  [send(): return lax.ppermute(value, 'dp', [(i, i ^ r) for i in range(replicas)])]
    all_to_all x3, waiting for transfers between devices: 22.5 us -> 32.7 us  [swap(): value = lax.all_to_all(value, axis, split_axis=0, concat_axis=0, tiled=True)]
    ppermute x14, starting transfers between devices: 46.5 us -> 43.4 us  [send(): return lax.ppermute(value, 'dp', [(i, i ^ r) for i in range(replicas)])]
    unnamed x26 -> x28, local copies, waits for them, and re-layouts: 0.05 us -> 2.64 us
  transfers between devices with their start and end apart: 17 -> 17, of which waited for: 13 -> 8; matrix products, arithmetic and copies ran while one was open for 1% -> 2% of each run, Pallas kernels for 7% -> 7%
where the time goes in v3:
time: 197 us; the launch traced here: 196 us
  waiting for transfers between devices  87.2 us (44%)
  starting transfers between devices  70.2 us (36%)
  Pallas kernels  32.2 us (16%)
  local copies, waits for them, and re-layouts  3.59 us (2%)
  other arithmetic  2.01 us (1%)
    ppermute x14, waiting for transfers between devices, send(): return lax.ppermute(value, 'dp', [(i, i ^ r) for i in range(replicas)])  54.5 us
    ppermute x14, starting transfers between devices, send(): return lax.ppermute(value, 'dp', [(i, i ^ r) for i in range(replicas)])  43.4 us
    all_to_all x3, waiting for transfers between devices, swap(): value = lax.all_to_all(value, axis, split_axis=0, concat_axis=0, tiled=True)  32.7 us
    pallas_call x6, Pallas kernels, call(): pl.pallas_call(body, out_shape=shapes[0] if single else tuple(shapes), in...  32.2 us
    all_to_all x3, starting transfers between devices, swap(): value = lax.all_to_all(value, axis, split_axis=0, concat_axis=0, tiled=True)  26.8 us
  transfers between devices with their start and end apart: 17, of which 8 were waited for; matrix products, arithmetic and copies ran while one was open for 2% of the time, Pallas kernels for 7%

profile of v3, /device:TPU:8, one launch (start us, length us, event | category | flops | bytes accessed | tf_op | source)
XLA Modules:
  0.0 196.2 jit_solution(2151169295968734346)
XLA Ops:
  0.6 2.3 %shard_map.104 = bf16[3648,128]{1,0:T(8,128)(2,1)} custom-call(s32[2,128]{1,0:T(2,128)} %bitcast.24, f32[2,128]{1,0:T(2,128)} %bitcast.25, bf16[128,3584]{1,0:T(8,128)(2,1)} %grad_ref.1), custom_call_target="tpu_custom_call" | custom-call | tf_op jit(solution)/shard_map/pallas_call | solution.py:387
  3.0 6.0 %all-to-all-start = ((bf16[8,456,128]{2,1,0:T(8,128)(2,1)}), bf16[8,456,128]{2,1,0:T(8,128)(2,1)S(1)}, u32[]{:S(2)}, u32[]{:S(2)}) async-start(bf16[8,456,128]{2,1,0:T(8,128)(2,1)} %bitcast.3), calls=%async_computation | async-start | bytes 1867776 | tf_op jit(solution)/shard_map/all_to_all | solution.py:424
  9.0 0.0 copy-start.11
  9.0 4.0 %shard_map.105 = (bf16[1344,128]{1,0:T(8,128)(2,1)}, bf16[1344,128]{1,0:T(8,128)(2,1)}, bf16[1344,128]{1,0:T(8,128)(2,1)}, bf16[1344,128]{1,0:T(8,128)(2,1)}, bf16[5376,128]{1,0:T(8,128)(2,1)}) custom-call(s32[1]{0:T(128)} %bitcast.own_ref, bf16[128,3584]{1,0:T(8,128)(2,1)} %bitcast.18, bf16[128,3584]{1,0:T(8,128)(2,1)} %bitcast.19, bf16[128,3584]{1,0:T(8,128)(2,1)} %bitcast.20), custom_call_target="tpu_custom_call" | custom-call | tf_op jit(solution)/shard_map/pallas_call | solution.py:387
  13.0 0.0 copy-done.8
  13.0 0.0 copy-done.11
  13.0 1.0 pad_maximum_fusion.refs_0_.refs_8_
  14.0 11.0 %all-to-all-done = bf16[8,456,128]{2,1,0:T(8,128)(2,1)S(1)} async-done(((bf16[8,456,128]{2,1,0:T(8,128)(2,1)}), bf16[8,456,128]{2,1,0:T(8,128)(2,1)S(1)}, u32[]{:S(2)}, u32[]{:S(2)}) %all-to-all-start) | async-done | bytes 933920 | tf_op jit(solution)/shard_map/all_to_all | solution.py:424
  25.0 6.4 %shard_map.106 = bf16[10752,128]{1,0:T(8,128)(2,1)} custom-call(bf16[3648,128]{1,0:T(8,128)(2,1)S(1)} %bitcast.16), custom_call_target="tpu_custom_call" | custom-call | tf_op jit(solution)/shard_map/pallas_call | solution.py:387
  31.4 0.0 copy-start.13
  31.4 0.0 copy-start.12
  31.4 17.3 %all-to-all-start.1 = ((bf16[64,168,128]{2,1,0:T(8,128)(2,1)}), bf16[64,168,128]{2,1,0:T(8,128)(2,1)S(1)}, u32[]{:S(2)}, u32[]{:S(2)}) async-start(bf16[64,168,128]{2,1,0:T(8,128)(2,1)} %bitcast.10), calls=%async_computation.1 | async-start | bytes 5505024 | tf_op jit(solution)/shard_map/all_to_all | solution.py:424
  48.7 0.0 copy-start.7
  48.7 2.6 %collective-permute-start.2 = (bf16[416,1024]{1,0:T(8,128)(2,1)}, bf16[416,1024]{1,0:T(8,128)(2,1)S(1)}, u32[]{:S(2)}, u32[]{:S(2)}) collective-permute-start(bf16[416,1024]{1,0:T(8,128)(2,1)} %pad_maximum_fusion.refs_0_.refs_8_), channel_id=1, source_target_pairs={{0,3},{1,2},{2,1},{3,0},{4,7},{5,6},{6,5},{7,4},{8,11},{9,10},{10,... | collective-permute-start | bytes 2555912 | tf_op jit(solution)/shard_map/ppermute | solution.py:398
  51.3 2.2 %collective-permute-start.1 = (bf16[416,1024]{1,0:T(8,128)(2,1)}, bf16[416,1024]{1,0:T(8,128)(2,1)S(1)}, u32[]{:S(2)}, u32[]{:S(2)}) collective-permute-start(bf16[416,1024]{1,0:T(8,128)(2,1)} %pad_maximum_fusion.refs_0_.refs_8_), channel_id=1, source_target_pairs={{0,1},{1,0},{2,3},{3,2},{4,5},{5,4},{6,7},{7,6},{8,9},{9,8},{10,11... | collective-permute-start | bytes 2555912 | tf_op jit(solution)/shard_map/ppermute | solution.py:398
  53.6 3.1 %collective-permute-start = (bf16[416,1024]{1,0:T(8,128)(2,1)}, bf16[416,1024]{1,0:T(8,128)(2,1)S(1)}, u32[]{:S(2)}, u32[]{:S(2)}) collective-permute-start(bf16[416,1024]{1,0:T(8,128)(2,1)} %pad_maximum_fusion.refs_0_.refs_8_), channel_id=1, source_target_pairs={{0,4},{1,5},{2,6},{3,7},{4,0},{5,1},{6,2},{7,3},{8,12},{9,13},{10,... | collective-permute-start | bytes 2555912 | tf_op jit(solution)/shard_map/ppermute | solution.py:398
  56.7 0.0 copy-done.13
  56.7 3.9 %collective-permute-start.3 = (bf16[1344,128]{1,0:T(8,128)(2,1)S(1)}, bf16[1344,128]{1,0:T(8,128)(2,1)S(1)}, u32[]{:S(2)}, u32[]{:S(2)}) collective-permute-start(bf16[1344,128]{1,0:T(8,128)(2,1)S(1)} %copy-done.13), channel_id=1, source_target_pairs={{0,1},{1,0},{2,3},{3,2},{4,5},{5,4},{6,7},{7,6},{8,9},{9,8},{10,11... | collective-permute-start | bytes 1032200 | tf_op jit(solution)/shard_map/ppermute | solution.py:398
  60.6 0.0 copy-done.12
  60.6 3.7 %collective-permute-start.4 = (bf16[1344,128]{1,0:T(8,128)(2,1)S(1)}, bf16[1344,128]{1,0:T(8,128)(2,1)S(1)}, u32[]{:S(2)}, u32[]{:S(2)}) collective-permute-start(bf16[1344,128]{1,0:T(8,128)(2,1)S(1)} %copy-done.12), channel_id=1, source_target_pairs={{0,3},{1,2},{2,1},{3,0},{4,7},{5,6},{6,5},{7,4},{8,11},{9,10},{10,... | collective-permute-start | bytes 1032200 | tf_op jit(solution)/shard_map/ppermute | solution.py:398
  64.3 17.2 %collective-permute-done.3.refs_1_ = bf16[1344,128]{1,0:T(8,128)(2,1)S(1)} collective-permute-done((bf16[1344,128]{1,0:T(8,128)(2,1)S(1)}, bf16[1344,128]{1,0:T(8,128)(2,1)S(1)}, u32[]{:S(2)}, u32[]{:S(2)}) %collective-permute-start.3) | collective-permute-done | bytes 344096 | tf_op jit(solution)/shard_map/ppermute | solution.py:398
  81.5 0.0 collective-permute-done.4.refs_3_
  81.5 0.0 collective-permute-done.2.refs_3_.refs_11_
  81.6 0.0 copy-start
  81.6 0.0 collective-permute-done.1.refs_1_.refs_9_
  81.6 0.7 copy-done.9
  82.3 0.1 copy-done.10
  82.4 0.0 collective-permute-done.refs_4_.refs_12_
  82.4 4.6 %collective-permute-start.6 = (bf16[416,1024]{1,0:T(8,128)(2,1)S(1)}, bf16[416,1024]{1,0:T(8,128)(2,1)S(1)}, u32[]{:S(2)}, u32[]{:S(2)}) collective-permute-start(bf16[416,1024]{1,0:T(8,128)(2,1)S(1)} %collective-permute-done.refs_4_.refs_12_), channel_id=1, source_target_pairs={{0,3},{1,2},{2,1},{3,0},{4,7},{5,6},{6,5},{7,4},{8,11},{9,10},{10,... | collective-permute-start | bytes 2555912 | tf_op jit(solution)/shard_map/ppermute | solution.py:398
  87.0 1.9 collective-permute-start.5
  88.9 3.1 %collective-permute-start.9 = (bf16[5376,128]{1,0:T(8,128)(2,1)}, bf16[5376,128]{1,0:T(8,128)(2,1)S(1)}, u32[]{:S(2)}, u32[]{:S(2)}) collective-permute-start(bf16[5376,128]{1,0:T(8,128)(2,1)} %get-tuple-element.46), channel_id=1, source_target_pairs={{0,4},{1,5},{2,6},{3,7},{4,0},{5,1},{6,2},{7,3},{8,12},{9,13},{10,... | collective-permute-start | bytes 4128776 | tf_op jit(solution)/shard_map/ppermute | solution.py:398
  92.1 13.4 %collective-permute-done.6.refs_7_.refs_15_ = bf16[416,1024]{1,0:T(8,128)(2,1)S(1)} collective-permute-done((bf16[416,1024]{1,0:T(8,128)(2,1)S(1)}, bf16[416,1024]{1,0:T(8,128)(2,1)S(1)}, u32[]{:S(2)}, u32[]{:S(2)}) %collective-permute-start.6) | collective-permute-done | bytes 852000 | tf_op jit(solution)/shard_map/ppermute | solution.py:398
  105.5 3.0 %collective-permute-done.5.refs_5_.refs_13_ = bf16[416,1024]{1,0:T(8,128)(2,1)S(1)} collective-permute-done((bf16[416,1024]{1,0:T(8,128)(2,1)S(1)}, bf16[416,1024]{1,0:T(8,128)(2,1)S(1)}, u32[]{:S(2)}, u32[]{:S(2)}) %collective-permute-start.5) | collective-permute-done | bytes 852000 | tf_op jit(solution)/shard_map/ppermute | solution.py:398
  108.5 2.6 %collective-permute-start.7 = (bf16[416,1024]{1,0:T(8,128)(2,1)S(1)}, bf16[416,1024]{1,0:T(8,128)(2,1)S(1)}, u32[]{:S(2)}, u32[]{:S(2)}) collective-permute-start(bf16[416,1024]{1,0:T(8,128)(2,1)S(1)} %collective-permute-done.5.refs_5_.refs_13_), channel_id=1, source_target_pairs={{0,3},{1,2},{2,1},{3,0},{4,7},{5,6},{6,5},{7,4},{8,11},{9,10},{10,... | collective-permute-start | bytes 2555912 | tf_op jit(solution)/shard_map/ppermute | solution.py:398
  111.0 0.0 copy-done
  111.1 2.0 %collective-permute-start.8 = (bf16[416,1024]{1,0:T(8,128)(2,1)S(1)}, bf16[416,1024]{1,0:T(8,128)(2,1)S(1)}, u32[]{:S(2)}, u32[]{:S(2)}) collective-permute-start(bf16[416,1024]{1,0:T(8,128)(2,1)S(1)} %collective-permute-done.2.refs_3_.refs_11_), channel_id=1, source_target_pairs={{0,1},{1,0},{2,3},{3,2},{4,5},{5,4},{6,7},{7,6},{8,9},{9,8},{10,11... | collective-permute-start | bytes 2555912 | tf_op jit(solution)/shard_map/ppermute | solution.py:398
  113.1 19.2 %collective-permute-done.9 = bf16[5376,128]{1,0:T(8,128)(2,1)S(1)} collective-permute-done((bf16[5376,128]{1,0:T(8,128)(2,1)}, bf16[5376,128]{1,0:T(8,128)(2,1)S(1)}, u32[]{:S(2)}, u32[]{:S(2)}) %collective-permute-start.9) | collective-permute-done | bytes 1376288 | tf_op jit(solution)/shard_map/ppermute | solution.py:398
  132.3 0.0 collective-permute-done.7.refs_6_.refs_14_
  132.3 0.0 collective-permute-done.8.refs_2_.refs_10_
  132.3 0.0 copy-done.1
  132.3 0.0 copy-done.2
  132.3 0.0 copy-done.3
  132.3 0.0 copy-done.4
  132.3 0.9 copy-done.5
  133.2 0.9 copy-done.6
  134.1 3.7 %collective-permute-start.10 = (bf16[1344,128]{1,0:T(8,128)(2,1)}, bf16[1344,128]{1,0:T(8,128)(2,1)}, u32[]{:S(2)}, u32[]{:S(2)}) collective-permute-start(bf16[1344,128]{1,0:T(8,128)(2,1)} %get-tuple-element.53), channel_id=1, source_target_pairs={{0,2},{1,3},{2,0},{3,1},{4,6},{5,7},{6,4},{7,5},{8,10},{9,11},{10,... | collective-permute-start | bytes 1032200 | tf_op jit(solution)/shard_map/ppermute | solution.py:398
  137.8 1.0 fusion.5
  138.8 4.5 %collective-permute-start.13 = (bf16[1344,128]{1,0:T(8,128)(2,1)}, bf16[1344,128]{1,0:T(8,128)(2,1)}, u32[]{:S(2)}, u32[]{:S(2)}) collective-permute-start(bf16[1344,128]{1,0:T(8,128)(2,1)} %get-tuple-element.58), channel_id=1, source_target_pairs={{0,3},{1,2},{2,1},{3,0},{4,7},{5,6},{6,5},{7,4},{8,11},{9,10},{10,... | collective-permute-start | bytes 1032200 | tf_op jit(solution)/shard_map/ppermute | solution.py:398
  143.2 1.9 collective-permute-start.12
  145.2 3.6 %collective-permute-start.11 = (bf16[1344,128]{1,0:T(8,128)(2,1)S(1)}, bf16[1344,128]{1,0:T(8,128)(2,1)}, u32[]{:S(2)}, u32[]{:S(2)}) collective-permute-start(bf16[1344,128]{1,0:T(8,128)(2,1)S(1)} %get-tuple-element.60), channel_id=1, source_target_pairs={{0,1},{1,0},{2,3},{3,2},{4,5},{5,4},{6,7},{7,6},{8,9},{9,8},{10,11... | collective-permute-start | bytes 1032200 | tf_op jit(solution)/shard_map/ppermute | solution.py:398
  148.8 0.0 copy-done.7
  148.8 0.1 reduce_max.14
  148.9 0.2 fusion.1
  149.1 9.6 %shard_map.107.hidden_ref = bf16[4,1024,768]{2,1,0:T(8,128)(2,1)} custom-call(s32[1]{0:T(128)} %bitcast.own_ref, bf16[416,1024]{1,0:T(8,128)(2,1)} %pad_maximum_fusion.refs_0_.refs_8_, bf16[416,1024]{1,0:T(8,128)(2,1)} %copy-done.1, bf16[416,1024]{1,0:T(8,128)(2,1)} %copy-done.6, bf16[416,1024]{1,0:T(8,128)(2,1)} %copy-done, bf16[416,1024]{1,0:T(8,128)(2,1)} %copy-done.2, ...), custom_call_target="tpu_custom_call" | custom-call | tf_op jit(solution)/shard_map/pallas_call | solution.py:387
  158.7 0.0 collective-permute-done.10.refs_2_
  158.7 1.6 collective-permute-done.13.refs_7_
  160.3 0.0 collective-permute-done.12.refs_6_
  160.3 0.0 collective-permute-done.11.refs_5_
  160.3 13.8 %all-to-all-done.1 = bf16[64,168,128]{2,1,0:T(8,128)(2,1)S(1)} async-done(((bf16[64,168,128]{2,1,0:T(8,128)(2,1)}), bf16[64,168,128]{2,1,0:T(8,128)(2,1)S(1)}, u32[]{:S(2)}, u32[]{:S(2)}) %all-to-all-start.1) | async-done | bytes 2752544 | tf_op jit(solution)/shard_map/all_to_all | solution.py:424
  174.1 9.1 %shard_map.108 = bf16[256,512]{1,0:T(8,128)(2,1)} custom-call(s32[1]{0:T(128)} %bitcast.own_ref, bf16[10752,128]{1,0:T(8,128)(2,1)S(1)} %bitcast.15, bf16[4,1024,768]{2,1,0:T(8,128)(2,1)} %shard_map.107.hidden_ref, bf16[1344,128]{1,0:T(8,128)(2,1)} %get-tuple-element.51.refs_0_, bf16[1344,128]{1,0:T(8,128)(2,1)} %copy-done.9, ...), custom_call_target="tpu_custom_call" | custom-call | tf_op jit(solution)/shard_map/pallas_call | solution.py:387
  183.2 3.4 %all-to-all-start.2 = ((bf16[8,32,512]{2,1,0:T(8,128)(2,1)}), bf16[8,32,512]{2,1,0:T(8,128)(2,1)S(1)}, u32[]{:S(2)}, u32[]{:S(2)}) async-start(bf16[8,32,512]{2,1,0:T(8,128)(2,1)} %bitcast.12), calls=%async_computation.2 | async-start | bytes 524288 | tf_op jit(solution)/shard_map/all_to_all | solution.py:424
  186.7 0.7 fusion.4
  187.4 8.0 %all-to-all-done.2 = bf16[8,32,512]{2,1,0:T(8,128)(2,1)S(1)} async-done(((bf16[8,32,512]{2,1,0:T(8,128)(2,1)}), bf16[8,32,512]{2,1,0:T(8,128)(2,1)S(1)}, u32[]{:S(2)}, u32[]{:S(2)}) %all-to-all-start.2) | async-done | bytes 262176 | tf_op jit(solution)/shard_map/all_to_all | solution.py:424
  195.4 0.8 shard_map.109
  (11 shorter events, 0.0 us)
Async XLA Ops:
  3.0 22.0 %all-to-all-start = ((bf16[8,456,128]{2,1,0:T(8,128)(2,1)}), bf16[8,456,128]{2,1,0:T(8,128)(2,1)S(1)}, u32[]{:S(2)}, u32[]{:S(2)}) async-start(bf16[8,456,128]{2,1,0:T(8,128)(2,1)} %bitcast.3), calls=%async_computation | async-start | bytes 1867776 | tf_op jit(solution)/shard_map/all_to_all | solution.py:424
  9.0 4.0 %copy-start.8 = (bf16[1,384,1024]{2,1,0:T(8,128)(2,1)S(1)}, bf16[1,384,1024]{2,1,0:T(8,128)(2,1)}, u32[]{:S(2)}) copy-start(bf16[1,384,1024]{2,1,0:T(8,128)(2,1)} %param.13) | copy-start | bytes 2359300
  9.0 4.0 %copy-start.11 = (bf16[1,32,1024]{2,1,0:T(8,128)(2,1)S(1)}, bf16[1,32,1024]{2,1,0:T(8,128)(2,1)}, u32[]{:S(2)}) copy-start(bf16[1,32,1024]{2,1,0:T(8,128)(2,1)} %param.17) | copy-start | bytes 196612
  31.4 25.3 %copy-start.13 = (bf16[1344,128]{1,0:T(8,128)(2,1)S(1)}, bf16[1344,128]{1,0:T(8,128)(2,1)}, u32[]{:S(2)}) copy-start(bf16[1344,128]{1,0:T(8,128)(2,1)} %get-tuple-element.36) | copy-start | bytes 1032196
  31.4 29.2 %copy-start.12 = (bf16[1344,128]{1,0:T(8,128)(2,1)S(1)}, bf16[1344,128]{1,0:T(8,128)(2,1)}, u32[]{:S(2)}) copy-start(bf16[1344,128]{1,0:T(8,128)(2,1)} %get-tuple-element.37) | copy-start | bytes 1032196
  31.4 142.7 %all-to-all-start.1 = ((bf16[64,168,128]{2,1,0:T(8,128)(2,1)}), bf16[64,168,128]{2,1,0:T(8,128)(2,1)S(1)}, u32[]{:S(2)}, u32[]{:S(2)}) async-start(bf16[64,168,128]{2,1,0:T(8,128)(2,1)} %bitcast.10), calls=%async_computation.1 | async-start | bytes 5505024 | tf_op jit(solution)/shard_map/all_to_all | solution.py:424
  48.7 100.1 %copy-start.7 = (bf16[128,384]{1,0:T(8,128)(2,1)S(1)}, bf16[128,384]{1,0:T(8,128)(2,1)}, u32[]{:S(2)}) copy-start(bf16[128,384]{1,0:T(8,128)(2,1)} %param.12) | copy-start | bytes 294916
  48.7 32.8 %collective-permute-start.2 = (bf16[416,1024]{1,0:T(8,128)(2,1)}, bf16[416,1024]{1,0:T(8,128)(2,1)S(1)}, u32[]{:S(2)}, u32[]{:S(2)}) collective-permute-start(bf16[416,1024]{1,0:T(8,128)(2,1)} %pad_maximum_fusion.refs_0_.refs_8_), channel_id=1, source_target_pairs={{0,3},{1,2},{2,1},{3,0},{4,7},{5,6},{6,5},{7,4},{8,11},{9,10},{10,... | collective-permute-start | bytes 2555912 | tf_op jit(solution)/shard_map/ppermute | solution.py:398
  51.3 30.2 %collective-permute-start.1 = (bf16[416,1024]{1,0:T(8,128)(2,1)}, bf16[416,1024]{1,0:T(8,128)(2,1)S(1)}, u32[]{:S(2)}, u32[]{:S(2)}) collective-permute-start(bf16[416,1024]{1,0:T(8,128)(2,1)} %pad_maximum_fusion.refs_0_.refs_8_), channel_id=1, source_target_pairs={{0,1},{1,0},{2,3},{3,2},{4,5},{5,4},{6,7},{7,6},{8,9},{9,8},{10,11... | collective-permute-start | bytes 2555912 | tf_op jit(solution)/shard_map/ppermute | solution.py:398
  53.6 28.8 %collective-permute-start = (bf16[416,1024]{1,0:T(8,128)(2,1)}, bf16[416,1024]{1,0:T(8,128)(2,1)S(1)}, u32[]{:S(2)}, u32[]{:S(2)}) collective-permute-start(bf16[416,1024]{1,0:T(8,128)(2,1)} %pad_maximum_fusion.refs_0_.refs_8_), channel_id=1, source_target_pairs={{0,4},{1,5},{2,6},{3,7},{4,0},{5,1},{6,2},{7,3},{8,12},{9,13},{10,... | collective-permute-start | bytes 2555912 | tf_op jit(solution)/shard_map/ppermute | solution.py:398
  56.7 24.9 %collective-permute-start.3 = (bf16[1344,128]{1,0:T(8,128)(2,1)S(1)}, bf16[1344,128]{1,0:T(8,128)(2,1)S(1)}, u32[]{:S(2)}, u32[]{:S(2)}) collective-permute-start(bf16[1344,128]{1,0:T(8,128)(2,1)S(1)} %copy-done.13), channel_id=1, source_target_pairs={{0,1},{1,0},{2,3},{3,2},{4,5},{5,4},{6,7},{7,6},{8,9},{9,8},{10,11... | collective-permute-start | bytes 1032200 | tf_op jit(solution)/shard_map/ppermute | solution.py:398
  60.6 20.9 %collective-permute-start.4 = (bf16[1344,128]{1,0:T(8,128)(2,1)S(1)}, bf16[1344,128]{1,0:T(8,128)(2,1)S(1)}, u32[]{:S(2)}, u32[]{:S(2)}) collective-permute-start(bf16[1344,128]{1,0:T(8,128)(2,1)S(1)} %copy-done.12), channel_id=1, source_target_pairs={{0,3},{1,2},{2,1},{3,0},{4,7},{5,6},{6,5},{7,4},{8,11},{9,10},{10,... | collective-permute-start | bytes 1032200 | tf_op jit(solution)/shard_map/ppermute | solution.py:398
  81.5 0.7 copy-start.9
  81.5 0.9 copy-start.10
  81.6 29.5 %copy-start = (bf16[416,1024]{1,0:T(8,128)(2,1)}, bf16[416,1024]{1,0:T(8,128)(2,1)S(1)}, u32[]{:S(2)}) copy-start(bf16[416,1024]{1,0:T(8,128)(2,1)S(1)} %collective-permute-done.2.refs_3_.refs_11_) | copy-start | bytes 2555908
  82.4 49.9 %copy-start.1 = (bf16[416,1024]{1,0:T(8,128)(2,1)}, bf16[416,1024]{1,0:T(8,128)(2,1)S(1)}, u32[]{:S(2)}) copy-start(bf16[416,1024]{1,0:T(8,128)(2,1)S(1)} %collective-permute-done.1.refs_1_.refs_9_) | copy-start | bytes 2555908
  82.4 49.9 %copy-start.2 = (bf16[416,1024]{1,0:T(8,128)(2,1)}, bf16[416,1024]{1,0:T(8,128)(2,1)S(1)}, u32[]{:S(2)}) copy-start(bf16[416,1024]{1,0:T(8,128)(2,1)S(1)} %collective-permute-done.refs_4_.refs_12_) | copy-start | bytes 2555908
  82.4 23.1 %collective-permute-start.6 = (bf16[416,1024]{1,0:T(8,128)(2,1)S(1)}, bf16[416,1024]{1,0:T(8,128)(2,1)S(1)}, u32[]{:S(2)}, u32[]{:S(2)}) collective-permute-start(bf16[416,1024]{1,0:T(8,128)(2,1)S(1)} %collective-permute-done.refs_4_.refs_12_), channel_id=1, source_target_pairs={{0,3},{1,2},{2,1},{3,0},{4,7},{5,6},{6,5},{7,4},{8,11},{9,10},{10,... | collective-permute-start | bytes 2555912 | tf_op jit(solution)/shard_map/ppermute | solution.py:398
  87.0 21.5 %collective-permute-start.5 = (bf16[416,1024]{1,0:T(8,128)(2,1)S(1)}, bf16[416,1024]{1,0:T(8,128)(2,1)S(1)}, u32[]{:S(2)}, u32[]{:S(2)}) collective-permute-start(bf16[416,1024]{1,0:T(8,128)(2,1)S(1)} %collective-permute-done.refs_4_.refs_12_), channel_id=1, source_target_pairs={{0,1},{1,0},{2,3},{3,2},{4,5},{5,4},{6,7},{7,6},{8,9},{9,8},{10,11... | collective-permute-start | bytes 2555912 | tf_op jit(solution)/shard_map/ppermute | solution.py:398
  88.9 43.4 %collective-permute-start.9 = (bf16[5376,128]{1,0:T(8,128)(2,1)}, bf16[5376,128]{1,0:T(8,128)(2,1)S(1)}, u32[]{:S(2)}, u32[]{:S(2)}) collective-permute-start(bf16[5376,128]{1,0:T(8,128)(2,1)} %get-tuple-element.46), channel_id=1, source_target_pairs={{0,4},{1,5},{2,6},{3,7},{4,0},{5,1},{6,2},{7,3},{8,12},{9,13},{10,... | collective-permute-start | bytes 4128776 | tf_op jit(solution)/shard_map/ppermute | solution.py:398
  105.5 26.8 %copy-start.3 = (bf16[416,1024]{1,0:T(8,128)(2,1)}, bf16[416,1024]{1,0:T(8,128)(2,1)S(1)}, u32[]{:S(2)}) copy-start(bf16[416,1024]{1,0:T(8,128)(2,1)S(1)} %collective-permute-done.6.refs_7_.refs_15_) | copy-start | bytes 2555908
  108.5 23.9 %copy-start.4 = (bf16[416,1024]{1,0:T(8,128)(2,1)}, bf16[416,1024]{1,0:T(8,128)(2,1)S(1)}, u32[]{:S(2)}) copy-start(bf16[416,1024]{1,0:T(8,128)(2,1)S(1)} %collective-permute-done.5.refs_5_.refs_13_) | copy-start | bytes 2555908
  108.5 23.8 %collective-permute-start.7 = (bf16[416,1024]{1,0:T(8,128)(2,1)S(1)}, bf16[416,1024]{1,0:T(8,128)(2,1)S(1)}, u32[]{:S(2)}, u32[]{:S(2)}) collective-permute-start(bf16[416,1024]{1,0:T(8,128)(2,1)S(1)} %collective-permute-done.5.refs_5_.refs_13_), channel_id=1, source_target_pairs={{0,3},{1,2},{2,1},{3,0},{4,7},{5,6},{6,5},{7,4},{8,11},{9,10},{10,... | collective-permute-start | bytes 2555912 | tf_op jit(solution)/shard_map/ppermute | solution.py:398
  111.1 21.2 %collective-permute-start.8 = (bf16[416,1024]{1,0:T(8,128)(2,1)S(1)}, bf16[416,1024]{1,0:T(8,128)(2,1)S(1)}, u32[]{:S(2)}, u32[]{:S(2)}) collective-permute-start(bf16[416,1024]{1,0:T(8,128)(2,1)S(1)} %collective-permute-done.2.refs_3_.refs_11_), channel_id=1, source_target_pairs={{0,1},{1,0},{2,3},{3,2},{4,5},{5,4},{6,7},{7,6},{8,9},{9,8},{10,11... | collective-permute-start | bytes 2555912 | tf_op jit(solution)/shard_map/ppermute | solution.py:398
  132.3 0.9 copy-start.5
  133.2 0.9 copy-start.6
  134.1 24.6 %collective-permute-start.10 = (bf16[1344,128]{1,0:T(8,128)(2,1)}, bf16[1344,128]{1,0:T(8,128)(2,1)}, u32[]{:S(2)}, u32[]{:S(2)}) collective-permute-start(bf16[1344,128]{1,0:T(8,128)(2,1)} %get-tuple-element.53), channel_id=1, source_target_pairs={{0,2},{1,3},{2,0},{3,1},{4,6},{5,7},{6,4},{7,5},{8,10},{9,11},{10,... | collective-permute-start | bytes 1032200 | tf_op jit(solution)/shard_map/ppermute | solution.py:398
  138.8 21.6 %collective-permute-start.13 = (bf16[1344,128]{1,0:T(8,128)(2,1)}, bf16[1344,128]{1,0:T(8,128)(2,1)}, u32[]{:S(2)}, u32[]{:S(2)}) collective-permute-start(bf16[1344,128]{1,0:T(8,128)(2,1)} %get-tuple-element.58), channel_id=1, source_target_pairs={{0,3},{1,2},{2,1},{3,0},{4,7},{5,6},{6,5},{7,4},{8,11},{9,10},{10,... | collective-permute-start | bytes 1032200 | tf_op jit(solution)/shard_map/ppermute | solution.py:398
  143.2 17.1 %collective-permute-start.12 = (bf16[1344,128]{1,0:T(8,128)(2,1)S(1)}, bf16[1344,128]{1,0:T(8,128)(2,1)}, u32[]{:S(2)}, u32[]{:S(2)}) collective-permute-start(bf16[1344,128]{1,0:T(8,128)(2,1)S(1)} %get-tuple-element.59), channel_id=1, source_target_pairs={{0,2},{1,3},{2,0},{3,1},{4,6},{5,7},{6,4},{7,5},{8,10},{9,11},{10,... | collective-permute-start | bytes 1032200 | tf_op jit(solution)/shard_map/ppermute | solution.py:398
  145.2 15.2 %collective-permute-start.11 = (bf16[1344,128]{1,0:T(8,128)(2,1)S(1)}, bf16[1344,128]{1,0:T(8,128)(2,1)}, u32[]{:S(2)}, u32[]{:S(2)}) collective-permute-start(bf16[1344,128]{1,0:T(8,128)(2,1)S(1)} %get-tuple-element.60), channel_id=1, source_target_pairs={{0,1},{1,0},{2,3},{3,2},{4,5},{5,4},{6,7},{7,6},{8,9},{9,8},{10,11... | collective-permute-start | bytes 1032200 | tf_op jit(solution)/shard_map/ppermute | solution.py:398
  183.2 12.2 %all-to-all-start.2 = ((bf16[8,32,512]{2,1,0:T(8,128)(2,1)}), bf16[8,32,512]{2,1,0:T(8,128)(2,1)S(1)}, u32[]{:S(2)}, u32[]{:S(2)}) async-start(bf16[8,32,512]{2,1,0:T(8,128)(2,1)} %bitcast.12), calls=%async_computation.2 | async-start | bytes 524288 | tf_op jit(solution)/shard_map/all_to_all | solution.py:424

commit v4 on v3

--- a/solution.py
+++ b/solution.py
@@ -167,7 +167,7 @@
                 ).astype(jnp.bfloat16)
             return carry
 
-        lax.fori_loop(0, experts // group, step, 0)
+        lax.fori_loop(0, experts // group, step, 0, unroll=4 if experts // group % 4 == 0 else 1)
 
     return body
 
@@ -268,6 +268,7 @@
             )
         for copy in copies:
             copy.start()
+        blocks = []
         for run in range(runs):
             received = wide_ref[run * run_rows : (run + 1) * run_rows, :]
             received = received.reshape(experts // runs, total, LANE)
@@ -279,39 +280,44 @@
                     )
                     for t in range(WIDE)
                 ]
-                copies[2 * run + h].wait()
+                blocks.append(jnp.concatenate(tiles + [last], axis=1))
+        slab = state_rows * 2 // (3 * (2 * WIDE + 1))
+        piece = WIDE * slab + slab // 2
+        per = replicas // 2
+        for m in range(2):
+            units = slice(m * per * slab, (m + 1) * per * slab)
+            for i, block in enumerate(blocks):
+                if m == 0:
+                    copies[i].wait()
                 product = jnp.dot(
-                    units_ref[2 * run + h],
-                    jnp.concatenate(tiles + [last], axis=1),
-                    preferred_element_type=jnp.float32,
+                    units_ref[i, units, :], block, preferred_element_type=jnp.float32
                 )
-                if h == 1:
+                if i % 2 == 1:
                     turned = pltpu.roll(product[:, SPAN : SPAN + LANE], HALF, 1)
                     product = jnp.concatenate([product[:, :SPAN], turned], axis=1)
-                if run == 0 and h == 0:
-                    gradient_ref[...] = product
+                if i == 0:
+                    gradient_ref[units, :] = product
                 else:
-                    gradient_ref[...] += product
-        slab = state_rows * 2 // (3 * (2 * WIDE + 1))
-        piece = WIDE * slab + slab // 2
-        for r in range(replicas):
-            copies[2 * runs + r].wait()
-            start = pl.multiple_of((own_ref[0] ^ r) * slab, slab)
-            for t in range(WIDE + 1):
-                state = []
-                for a in range(3):
-                    base = r * state_rows + a * piece + t * slab
-                    if t < WIDE:
-                        state.append(state_ref[base : base + slab, :])
-                    else:
-                        folded = state_ref[base : base + slab // 2, :].astype(jnp.float32)
-                        state.append(
-                            jnp.concatenate([folded, pltpu.roll(folded, HALF, 1)], axis=0)
-                        )
-                gradient = gradient_ref[pl.ds(start, slab), t * LANE : (t + 1) * LANE]
-                updated_ref[pl.ds(start, slab), t * LANE : (t + 1) * LANE] = adamw(
-                    *state, gradient
-                )
+                    gradient_ref[units, :] += product
+            if m == 0:
+                for copy in copies[2 * runs : 2 * runs + replicas]:
+                    copy.wait()
+            for s in range(m * per, (m + 1) * per):
+                first = (own_ref[0] ^ s) * state_rows
+                place = slice(s * slab, (s + 1) * slab)
+                for t in range(WIDE + 1):
+                    state = []
+                    for a in range(3):
+                        base = pl.multiple_of(first + a * piece + t * slab, 16)
+                        if t < WIDE:
+                            state.append(state_ref[pl.ds(base, slab), :])
+                        else:
+                            folded = state_ref[pl.ds(base, slab // 2), :].astype(jnp.float32)
+                            state.append(
+                                jnp.concatenate([folded, pltpu.roll(folded, HALF, 1)], axis=0)
+                            )
+                    columns = slice(t * LANE, (t + 1) * LANE)
+                    updated_ref[place, columns] = adamw(*state, gradient_ref[place, columns])
         for copy in copies[2 * runs + replicas :]:
             copy.wait()
         result = jnp.dot(next_ref[...], updated_ref[...], preferred_element_type=jnp.float32)

time: 197 us -> 196 us (level)
  no operation moved by 1% of the time
where the time goes in v4:
time: 196 us; the launch traced here: 195 us
  waiting for transfers between devices  87.2 us (44%)
  starting transfers between devices  70.2 us (36%)
  Pallas kernels  30.8 us (16%)
  local copies, waits for them, and re-layouts  3.59 us (2%)
  other arithmetic  2.01 us (1%)
    ppermute x14, waiting for transfers between devices, send(): return lax.ppermute(value, 'dp', [(i, i ^ r) for i in range(replicas)])  54.5 us
    ppermute x14, starting transfers between devices, send(): return lax.ppermute(value, 'dp', [(i, i ^ r) for i in range(replicas)])  43.4 us
    all_to_all x3, waiting for transfers between devices, swap(): value = lax.all_to_all(value, axis, split_axis=0, concat_axis=0, tiled=True)  32.7 us
    pallas_call x6, Pallas kernels, call(): pl.pallas_call(body, out_shape=shapes[0] if single else tuple(shapes), in...  30.8 us
    all_to_all x3, starting transfers between devices, swap(): value = lax.all_to_all(value, axis, split_axis=0, concat_axis=0, tiled=True)  26.8 us
  transfers between devices with their start and end apart: 17, of which 8 were waited for; matrix products, arithmetic and copies ran while one was open for 2% of the time, Pallas kernels for 7%

profile of v4, /device:TPU:8, one launch (start us, length us, event | category | flops | bytes accessed | tf_op | source)
XLA Modules:
  0.0 194.7 jit_solution(16006369287472262674)
XLA Ops:
  0.6 2.3 %shard_map.104 = bf16[3648,128]{1,0:T(8,128)(2,1)} custom-call(s32[2,128]{1,0:T(2,128)} %bitcast.24, f32[2,128]{1,0:T(2,128)} %bitcast.25, bf16[128,3584]{1,0:T(8,128)(2,1)} %grad_ref.1), custom_call_target="tpu_custom_call" | custom-call | tf_op jit(solution)/shard_map/pallas_call | solution.py:393
  3.0 6.0 %all-to-all-start = ((bf16[8,456,128]{2,1,0:T(8,128)(2,1)}), bf16[8,456,128]{2,1,0:T(8,128)(2,1)S(1)}, u32[]{:S(2)}, u32[]{:S(2)}) async-start(bf16[8,456,128]{2,1,0:T(8,128)(2,1)} %bitcast.3), calls=%async_computation | async-start | bytes 1867776 | tf_op jit(solution)/shard_map/all_to_all | solution.py:430
  9.0 0.0 copy-start.11
  9.0 4.0 %shard_map.105 = (bf16[1344,128]{1,0:T(8,128)(2,1)}, bf16[1344,128]{1,0:T(8,128)(2,1)}, bf16[1344,128]{1,0:T(8,128)(2,1)}, bf16[1344,128]{1,0:T(8,128)(2,1)}, bf16[5376,128]{1,0:T(8,128)(2,1)}) custom-call(s32[1]{0:T(128)} %bitcast.own_ref, bf16[128,3584]{1,0:T(8,128)(2,1)} %bitcast.18, bf16[128,3584]{1,0:T(8,128)(2,1)} %bitcast.19, bf16[128,3584]{1,0:T(8,128)(2,1)} %bitcast.20), custom_call_target="tpu_custom_call" | custom-call | tf_op jit(solution)/shard_map/pallas_call | solution.py:393
  13.0 0.0 copy-done.8
  13.0 0.0 copy-done.11
  13.0 1.0 pad_maximum_fusion.refs_0_.refs_8_
  14.0 11.0 %all-to-all-done = bf16[8,456,128]{2,1,0:T(8,128)(2,1)S(1)} async-done(((bf16[8,456,128]{2,1,0:T(8,128)(2,1)}), bf16[8,456,128]{2,1,0:T(8,128)(2,1)S(1)}, u32[]{:S(2)}, u32[]{:S(2)}) %all-to-all-start) | async-done | bytes 933920 | tf_op jit(solution)/shard_map/all_to_all | solution.py:430
  25.0 5.4 %shard_map.106 = bf16[10752,128]{1,0:T(8,128)(2,1)} custom-call(bf16[3648,128]{1,0:T(8,128)(2,1)S(1)} %bitcast.16), custom_call_target="tpu_custom_call" | custom-call | tf_op jit(solution)/shard_map/pallas_call | solution.py:393
  30.3 0.0 copy-start.13
  30.3 0.0 copy-start.12
  30.3 17.3 %all-to-all-start.1 = ((bf16[64,168,128]{2,1,0:T(8,128)(2,1)}), bf16[64,168,128]{2,1,0:T(8,128)(2,1)S(1)}, u32[]{:S(2)}, u32[]{:S(2)}) async-start(bf16[64,168,128]{2,1,0:T(8,128)(2,1)} %bitcast.10), calls=%async_computation.1 | async-start | bytes 5505024 | tf_op jit(solution)/shard_map/all_to_all | solution.py:430
  47.7 0.0 copy-start.7
  47.7 2.6 %collective-permute-start.2 = (bf16[416,1024]{1,0:T(8,128)(2,1)}, bf16[416,1024]{1,0:T(8,128)(2,1)S(1)}, u32[]{:S(2)}, u32[]{:S(2)}) collective-permute-start(bf16[416,1024]{1,0:T(8,128)(2,1)} %pad_maximum_fusion.refs_0_.refs_8_), channel_id=1, source_target_pairs={{0,3},{1,2},{2,1},{3,0},{4,7},{5,6},{6,5},{7,4},{8,11},{9,10},{10,... | collective-permute-start | bytes 2555912 | tf_op jit(solution)/shard_map/ppermute | solution.py:404
  50.3 2.2 %collective-permute-start.1 = (bf16[416,1024]{1,0:T(8,128)(2,1)}, bf16[416,1024]{1,0:T(8,128)(2,1)S(1)}, u32[]{:S(2)}, u32[]{:S(2)}) collective-permute-start(bf16[416,1024]{1,0:T(8,128)(2,1)} %pad_maximum_fusion.refs_0_.refs_8_), channel_id=1, source_target_pairs={{0,1},{1,0},{2,3},{3,2},{4,5},{5,4},{6,7},{7,6},{8,9},{9,8},{10,11... | collective-permute-start | bytes 2555912 | tf_op jit(solution)/shard_map/ppermute | solution.py:404
  52.5 3.1 %collective-permute-start = (bf16[416,1024]{1,0:T(8,128)(2,1)}, bf16[416,1024]{1,0:T(8,128)(2,1)S(1)}, u32[]{:S(2)}, u32[]{:S(2)}) collective-permute-start(bf16[416,1024]{1,0:T(8,128)(2,1)} %pad_maximum_fusion.refs_0_.refs_8_), channel_id=1, source_target_pairs={{0,4},{1,5},{2,6},{3,7},{4,0},{5,1},{6,2},{7,3},{8,12},{9,13},{10,... | collective-permute-start | bytes 2555912 | tf_op jit(solution)/shard_map/ppermute | solution.py:404
  55.6 0.0 copy-done.13
  55.6 3.9 %collective-permute-start.3 = (bf16[1344,128]{1,0:T(8,128)(2,1)S(1)}, bf16[1344,128]{1,0:T(8,128)(2,1)S(1)}, u32[]{:S(2)}, u32[]{:S(2)}) collective-permute-start(bf16[1344,128]{1,0:T(8,128)(2,1)S(1)} %copy-done.13), channel_id=1, source_target_pairs={{0,1},{1,0},{2,3},{3,2},{4,5},{5,4},{6,7},{7,6},{8,9},{9,8},{10,11... | collective-permute-start | bytes 1032200 | tf_op jit(solution)/shard_map/ppermute | solution.py:404
  59.6 0.0 copy-done.12
  59.6 3.7 %collective-permute-start.4 = (bf16[1344,128]{1,0:T(8,128)(2,1)S(1)}, bf16[1344,128]{1,0:T(8,128)(2,1)S(1)}, u32[]{:S(2)}, u32[]{:S(2)}) collective-permute-start(bf16[1344,128]{1,0:T(8,128)(2,1)S(1)} %copy-done.12), channel_id=1, source_target_pairs={{0,3},{1,2},{2,1},{3,0},{4,7},{5,6},{6,5},{7,4},{8,11},{9,10},{10,... | collective-permute-start | bytes 1032200 | tf_op jit(solution)/shard_map/ppermute | solution.py:404
  63.3 17.2 %collective-permute-done.3.refs_1_ = bf16[1344,128]{1,0:T(8,128)(2,1)S(1)} collective-permute-done((bf16[1344,128]{1,0:T(8,128)(2,1)S(1)}, bf16[1344,128]{1,0:T(8,128)(2,1)S(1)}, u32[]{:S(2)}, u32[]{:S(2)}) %collective-permute-start.3) | collective-permute-done | bytes 344096 | tf_op jit(solution)/shard_map/ppermute | solution.py:404
  80.5 0.0 collective-permute-done.4.refs_3_
  80.5 0.0 collective-permute-done.2.refs_3_.refs_11_
  80.5 0.0 copy-start
  80.5 0.0 collective-permute-done.1.refs_1_.refs_9_
  80.5 0.7 copy-done.9
  81.2 0.1 copy-done.10
  81.4 0.0 collective-permute-done.refs_4_.refs_12_
  81.4 4.6 %collective-permute-start.6 = (bf16[416,1024]{1,0:T(8,128)(2,1)S(1)}, bf16[416,1024]{1,0:T(8,128)(2,1)S(1)}, u32[]{:S(2)}, u32[]{:S(2)}) collective-permute-start(bf16[416,1024]{1,0:T(8,128)(2,1)S(1)} %collective-permute-done.refs_4_.refs_12_), channel_id=1, source_target_pairs={{0,3},{1,2},{2,1},{3,0},{4,7},{5,6},{6,5},{7,4},{8,11},{9,10},{10,... | collective-permute-start | bytes 2555912 | tf_op jit(solution)/shard_map/ppermute | solution.py:404
  86.0 1.9 collective-permute-start.5
  87.9 3.1 %collective-permute-start.9 = (bf16[5376,128]{1,0:T(8,128)(2,1)}, bf16[5376,128]{1,0:T(8,128)(2,1)S(1)}, u32[]{:S(2)}, u32[]{:S(2)}) collective-permute-start(bf16[5376,128]{1,0:T(8,128)(2,1)} %get-tuple-element.46), channel_id=1, source_target_pairs={{0,4},{1,5},{2,6},{3,7},{4,0},{5,1},{6,2},{7,3},{8,12},{9,13},{10,... | collective-permute-start | bytes 4128776 | tf_op jit(solution)/shard_map/ppermute | solution.py:404
  91.0 13.4 %collective-permute-done.6.refs_7_.refs_15_ = bf16[416,1024]{1,0:T(8,128)(2,1)S(1)} collective-permute-done((bf16[416,1024]{1,0:T(8,128)(2,1)S(1)}, bf16[416,1024]{1,0:T(8,128)(2,1)S(1)}, u32[]{:S(2)}, u32[]{:S(2)}) %collective-permute-start.6) | collective-permute-done | bytes 852000 | tf_op jit(solution)/shard_map/ppermute | solution.py:404
  104.4 3.0 %collective-permute-done.5.refs_5_.refs_13_ = bf16[416,1024]{1,0:T(8,128)(2,1)S(1)} collective-permute-done((bf16[416,1024]{1,0:T(8,128)(2,1)S(1)}, bf16[416,1024]{1,0:T(8,128)(2,1)S(1)}, u32[]{:S(2)}, u32[]{:S(2)}) %collective-permute-start.5) | collective-permute-done | bytes 852000 | tf_op jit(solution)/shard_map/ppermute | solution.py:404
  107.4 2.6 %collective-permute-start.7 = (bf16[416,1024]{1,0:T(8,128)(2,1)S(1)}, bf16[416,1024]{1,0:T(8,128)(2,1)S(1)}, u32[]{:S(2)}, u32[]{:S(2)}) collective-permute-start(bf16[416,1024]{1,0:T(8,128)(2,1)S(1)} %collective-permute-done.5.refs_5_.refs_13_), channel_id=1, source_target_pairs={{0,3},{1,2},{2,1},{3,0},{4,7},{5,6},{6,5},{7,4},{8,11},{9,10},{10,... | collective-permute-start | bytes 2555912 | tf_op jit(solution)/shard_map/ppermute | solution.py:404
  110.0 0.0 copy-done
  110.0 2.0 %collective-permute-start.8 = (bf16[416,1024]{1,0:T(8,128)(2,1)S(1)}, bf16[416,1024]{1,0:T(8,128)(2,1)S(1)}, u32[]{:S(2)}, u32[]{:S(2)}) collective-permute-start(bf16[416,1024]{1,0:T(8,128)(2,1)S(1)} %collective-permute-done.2.refs_3_.refs_11_), channel_id=1, source_target_pairs={{0,1},{1,0},{2,3},{3,2},{4,5},{5,4},{6,7},{7,6},{8,9},{9,8},{10,11... | collective-permute-start | bytes 2555912 | tf_op jit(solution)/shard_map/ppermute | solution.py:404
  112.0 19.2 %collective-permute-done.9 = bf16[5376,128]{1,0:T(8,128)(2,1)S(1)} collective-permute-done((bf16[5376,128]{1,0:T(8,128)(2,1)}, bf16[5376,128]{1,0:T(8,128)(2,1)S(1)}, u32[]{:S(2)}, u32[]{:S(2)}) %collective-permute-start.9) | collective-permute-done | bytes 1376288 | tf_op jit(solution)/shard_map/ppermute | solution.py:404
  131.3 0.0 collective-permute-done.7.refs_6_.refs_14_
  131.3 0.0 collective-permute-done.8.refs_2_.refs_10_
  131.3 0.0 copy-done.1
  131.3 0.0 copy-done.2
  131.3 0.0 copy-done.3
  131.3 0.0 copy-done.4
  131.3 0.9 copy-done.5
  132.2 0.9 copy-done.6
  133.1 3.7 %collective-permute-start.10 = (bf16[1344,128]{1,0:T(8,128)(2,1)}, bf16[1344,128]{1,0:T(8,128)(2,1)}, u32[]{:S(2)}, u32[]{:S(2)}) collective-permute-start(bf16[1344,128]{1,0:T(8,128)(2,1)} %get-tuple-element.53), channel_id=1, source_target_pairs={{0,2},{1,3},{2,0},{3,1},{4,6},{5,7},{6,4},{7,5},{8,10},{9,11},{10,... | collective-permute-start | bytes 1032200 | tf_op jit(solution)/shard_map/ppermute | solution.py:404
  136.8 1.0 fusion.5
  137.7 4.5 %collective-permute-start.13 = (bf16[1344,128]{1,0:T(8,128)(2,1)}, bf16[1344,128]{1,0:T(8,128)(2,1)}, u32[]{:S(2)}, u32[]{:S(2)}) collective-permute-start(bf16[1344,128]{1,0:T(8,128)(2,1)} %get-tuple-element.58), channel_id=1, source_target_pairs={{0,3},{1,2},{2,1},{3,0},{4,7},{5,6},{6,5},{7,4},{8,11},{9,10},{10,... | collective-permute-start | bytes 1032200 | tf_op jit(solution)/shard_map/ppermute | solution.py:404
  142.2 1.9 collective-permute-start.12
  144.1 3.6 %collective-permute-start.11 = (bf16[1344,128]{1,0:T(8,128)(2,1)S(1)}, bf16[1344,128]{1,0:T(8,128)(2,1)}, u32[]{:S(2)}, u32[]{:S(2)}) collective-permute-start(bf16[1344,128]{1,0:T(8,128)(2,1)S(1)} %get-tuple-element.60), channel_id=1, source_target_pairs={{0,1},{1,0},{2,3},{3,2},{4,5},{5,4},{6,7},{7,6},{8,9},{9,8},{10,11... | collective-permute-start | bytes 1032200 | tf_op jit(solution)/shard_map/ppermute | solution.py:404
  147.7 0.0 copy-done.7
  147.8 0.1 reduce_max.14
  147.9 0.2 fusion.1
  148.1 9.6 %shard_map.107.hidden_ref = bf16[4,1024,768]{2,1,0:T(8,128)(2,1)} custom-call(s32[1]{0:T(128)} %bitcast.own_ref, bf16[416,1024]{1,0:T(8,128)(2,1)} %pad_maximum_fusion.refs_0_.refs_8_, bf16[416,1024]{1,0:T(8,128)(2,1)} %copy-done.1, bf16[416,1024]{1,0:T(8,128)(2,1)} %copy-done.6, bf16[416,1024]{1,0:T(8,128)(2,1)} %copy-done, bf16[416,1024]{1,0:T(8,128)(2,1)} %copy-done.2, ...), custom_call_target="tpu_custom_call" | custom-call | tf_op jit(solution)/shard_map/pallas_call | solution.py:393
  157.7 0.0 collective-permute-done.10.refs_2_
  157.7 1.6 collective-permute-done.13.refs_7_
  159.3 0.0 collective-permute-done.12.refs_6_
  159.3 0.0 collective-permute-done.11.refs_5_
  159.3 13.8 %all-to-all-done.1 = bf16[64,168,128]{2,1,0:T(8,128)(2,1)S(1)} async-done(((bf16[64,168,128]{2,1,0:T(8,128)(2,1)}), bf16[64,168,128]{2,1,0:T(8,128)(2,1)S(1)}, u32[]{:S(2)}, u32[]{:S(2)}) %all-to-all-start.1) | async-done | bytes 2752544 | tf_op jit(solution)/shard_map/all_to_all | solution.py:430
  173.1 8.7 %shard_map.108 = bf16[256,512]{1,0:T(8,128)(2,1)} custom-call(s32[1]{0:T(128)} %bitcast.own_ref, bf16[10752,128]{1,0:T(8,128)(2,1)S(1)} %bitcast.15, bf16[4,1024,768]{2,1,0:T(8,128)(2,1)} %shard_map.107.hidden_ref, bf16[1344,128]{1,0:T(8,128)(2,1)} %get-tuple-element.51.refs_0_, bf16[1344,128]{1,0:T(8,128)(2,1)} %copy-done.9, ...), custom_call_target="tpu_custom_call" | custom-call | tf_op jit(solution)/shard_map/pallas_call | solution.py:393
  181.8 3.4 %all-to-all-start.2 = ((bf16[8,32,512]{2,1,0:T(8,128)(2,1)}), bf16[8,32,512]{2,1,0:T(8,128)(2,1)S(1)}, u32[]{:S(2)}, u32[]{:S(2)}) async-start(bf16[8,32,512]{2,1,0:T(8,128)(2,1)} %bitcast.12), calls=%async_computation.2 | async-start | bytes 524288 | tf_op jit(solution)/shard_map/all_to_all | solution.py:430
  185.2 0.7 fusion.4
  186.0 8.0 %all-to-all-done.2 = bf16[8,32,512]{2,1,0:T(8,128)(2,1)S(1)} async-done(((bf16[8,32,512]{2,1,0:T(8,128)(2,1)}), bf16[8,32,512]{2,1,0:T(8,128)(2,1)S(1)}, u32[]{:S(2)}, u32[]{:S(2)}) %all-to-all-start.2) | async-done | bytes 262176 | tf_op jit(solution)/shard_map/all_to_all | solution.py:430
  193.9 0.8 shard_map.109
  (11 shorter events, 0.0 us)
Async XLA Ops:
  3.0 22.0 %all-to-all-start = ((bf16[8,456,128]{2,1,0:T(8,128)(2,1)}), bf16[8,456,128]{2,1,0:T(8,128)(2,1)S(1)}, u32[]{:S(2)}, u32[]{:S(2)}) async-start(bf16[8,456,128]{2,1,0:T(8,128)(2,1)} %bitcast.3), calls=%async_computation | async-start | bytes 1867776 | tf_op jit(solution)/shard_map/all_to_all | solution.py:430
  9.0 4.0 %copy-start.8 = (bf16[1,384,1024]{2,1,0:T(8,128)(2,1)S(1)}, bf16[1,384,1024]{2,1,0:T(8,128)(2,1)}, u32[]{:S(2)}) copy-start(bf16[1,384,1024]{2,1,0:T(8,128)(2,1)} %param.13) | copy-start | bytes 2359300
  9.0 4.0 %copy-start.11 = (bf16[1,32,1024]{2,1,0:T(8,128)(2,1)S(1)}, bf16[1,32,1024]{2,1,0:T(8,128)(2,1)}, u32[]{:S(2)}) copy-start(bf16[1,32,1024]{2,1,0:T(8,128)(2,1)} %param.17) | copy-start | bytes 196612
  30.3 25.3 %copy-start.13 = (bf16[1344,128]{1,0:T(8,128)(2,1)S(1)}, bf16[1344,128]{1,0:T(8,128)(2,1)}, u32[]{:S(2)}) copy-start(bf16[1344,128]{1,0:T(8,128)(2,1)} %get-tuple-element.36) | copy-start | bytes 1032196
  30.3 29.2 %copy-start.12 = (bf16[1344,128]{1,0:T(8,128)(2,1)S(1)}, bf16[1344,128]{1,0:T(8,128)(2,1)}, u32[]{:S(2)}) copy-start(bf16[1344,128]{1,0:T(8,128)(2,1)} %get-tuple-element.37) | copy-start | bytes 1032196
  30.3 142.7 %all-to-all-start.1 = ((bf16[64,168,128]{2,1,0:T(8,128)(2,1)}), bf16[64,168,128]{2,1,0:T(8,128)(2,1)S(1)}, u32[]{:S(2)}, u32[]{:S(2)}) async-start(bf16[64,168,128]{2,1,0:T(8,128)(2,1)} %bitcast.10), calls=%async_computation.1 | async-start | bytes 5505024 | tf_op jit(solution)/shard_map/all_to_all | solution.py:430
  47.7 100.1 %copy-start.7 = (bf16[128,384]{1,0:T(8,128)(2,1)S(1)}, bf16[128,384]{1,0:T(8,128)(2,1)}, u32[]{:S(2)}) copy-start(bf16[128,384]{1,0:T(8,128)(2,1)} %param.12) | copy-start | bytes 294916
  47.7 32.8 %collective-permute-start.2 = (bf16[416,1024]{1,0:T(8,128)(2,1)}, bf16[416,1024]{1,0:T(8,128)(2,1)S(1)}, u32[]{:S(2)}, u32[]{:S(2)}) collective-permute-start(bf16[416,1024]{1,0:T(8,128)(2,1)} %pad_maximum_fusion.refs_0_.refs_8_), channel_id=1, source_target_pairs={{0,3},{1,2},{2,1},{3,0},{4,7},{5,6},{6,5},{7,4},{8,11},{9,10},{10,... | collective-permute-start | bytes 2555912 | tf_op jit(solution)/shard_map/ppermute | solution.py:404
  50.3 30.2 %collective-permute-start.1 = (bf16[416,1024]{1,0:T(8,128)(2,1)}, bf16[416,1024]{1,0:T(8,128)(2,1)S(1)}, u32[]{:S(2)}, u32[]{:S(2)}) collective-permute-start(bf16[416,1024]{1,0:T(8,128)(2,1)} %pad_maximum_fusion.refs_0_.refs_8_), channel_id=1, source_target_pairs={{0,1},{1,0},{2,3},{3,2},{4,5},{5,4},{6,7},{7,6},{8,9},{9,8},{10,11... | collective-permute-start | bytes 2555912 | tf_op jit(solution)/shard_map/ppermute | solution.py:404
  52.5 28.8 %collective-permute-start = (bf16[416,1024]{1,0:T(8,128)(2,1)}, bf16[416,1024]{1,0:T(8,128)(2,1)S(1)}, u32[]{:S(2)}, u32[]{:S(2)}) collective-permute-start(bf16[416,1024]{1,0:T(8,128)(2,1)} %pad_maximum_fusion.refs_0_.refs_8_), channel_id=1, source_target_pairs={{0,4},{1,5},{2,6},{3,7},{4,0},{5,1},{6,2},{7,3},{8,12},{9,13},{10,... | collective-permute-start | bytes 2555912 | tf_op jit(solution)/shard_map/ppermute | solution.py:404
  55.6 24.9 %collective-permute-start.3 = (bf16[1344,128]{1,0:T(8,128)(2,1)S(1)}, bf16[1344,128]{1,0:T(8,128)(2,1)S(1)}, u32[]{:S(2)}, u32[]{:S(2)}) collective-permute-start(bf16[1344,128]{1,0:T(8,128)(2,1)S(1)} %copy-done.13), channel_id=1, source_target_pairs={{0,1},{1,0},{2,3},{3,2},{4,5},{5,4},{6,7},{7,6},{8,9},{9,8},{10,11... | collective-permute-start | bytes 1032200 | tf_op jit(solution)/shard_map/ppermute | solution.py:404
  59.6 20.9 %collective-permute-start.4 = (bf16[1344,128]{1,0:T(8,128)(2,1)S(1)}, bf16[1344,128]{1,0:T(8,128)(2,1)S(1)}, u32[]{:S(2)}, u32[]{:S(2)}) collective-permute-start(bf16[1344,128]{1,0:T(8,128)(2,1)S(1)} %copy-done.12), channel_id=1, source_target_pairs={{0,3},{1,2},{2,1},{3,0},{4,7},{5,6},{6,5},{7,4},{8,11},{9,10},{10,... | collective-permute-start | bytes 1032200 | tf_op jit(solution)/shard_map/ppermute | solution.py:404
  80.5 0.7 copy-start.9
  80.5 0.9 copy-start.10
  80.5 29.5 %copy-start = (bf16[416,1024]{1,0:T(8,128)(2,1)}, bf16[416,1024]{1,0:T(8,128)(2,1)S(1)}, u32[]{:S(2)}) copy-start(bf16[416,1024]{1,0:T(8,128)(2,1)S(1)} %collective-permute-done.2.refs_3_.refs_11_) | copy-start | bytes 2555908
  81.4 49.9 %copy-start.1 = (bf16[416,1024]{1,0:T(8,128)(2,1)}, bf16[416,1024]{1,0:T(8,128)(2,1)S(1)}, u32[]{:S(2)}) copy-start(bf16[416,1024]{1,0:T(8,128)(2,1)S(1)} %collective-permute-done.1.refs_1_.refs_9_) | copy-start | bytes 2555908
  81.4 49.9 %copy-start.2 = (bf16[416,1024]{1,0:T(8,128)(2,1)}, bf16[416,1024]{1,0:T(8,128)(2,1)S(1)}, u32[]{:S(2)}) copy-start(bf16[416,1024]{1,0:T(8,128)(2,1)S(1)} %collective-permute-done.refs_4_.refs_12_) | copy-start | bytes 2555908
  81.4 23.1 %collective-permute-start.6 = (bf16[416,1024]{1,0:T(8,128)(2,1)S(1)}, bf16[416,1024]{1,0:T(8,128)(2,1)S(1)}, u32[]{:S(2)}, u32[]{:S(2)}) collective-permute-start(bf16[416,1024]{1,0:T(8,128)(2,1)S(1)} %collective-permute-done.refs_4_.refs_12_), channel_id=1, source_target_pairs={{0,3},{1,2},{2,1},{3,0},{4,7},{5,6},{6,5},{7,4},{8,11},{9,10},{10,... | collective-permute-start | bytes 2555912 | tf_op jit(solution)/shard_map/ppermute | solution.py:404
  86.0 21.5 %collective-permute-start.5 = (bf16[416,1024]{1,0:T(8,128)(2,1)S(1)}, bf16[416,1024]{1,0:T(8,128)(2,1)S(1)}, u32[]{:S(2)}, u32[]{:S(2)}) collective-permute-start(bf16[416,1024]{1,0:T(8,128)(2,1)S(1)} %collective-permute-done.refs_4_.refs_12_), channel_id=1, source_target_pairs={{0,1},{1,0},{2,3},{3,2},{4,5},{5,4},{6,7},{7,6},{8,9},{9,8},{10,11... | collective-permute-start | bytes 2555912 | tf_op jit(solution)/shard_map/ppermute | solution.py:404
  87.9 43.4 %collective-permute-start.9 = (bf16[5376,128]{1,0:T(8,128)(2,1)}, bf16[5376,128]{1,0:T(8,128)(2,1)S(1)}, u32[]{:S(2)}, u32[]{:S(2)}) collective-permute-start(bf16[5376,128]{1,0:T(8,128)(2,1)} %get-tuple-element.46), channel_id=1, source_target_pairs={{0,4},{1,5},{2,6},{3,7},{4,0},{5,1},{6,2},{7,3},{8,12},{9,13},{10,... | collective-permute-start | bytes 4128776 | tf_op jit(solution)/shard_map/ppermute | solution.py:404
  104.4 26.9 %copy-start.3 = (bf16[416,1024]{1,0:T(8,128)(2,1)}, bf16[416,1024]{1,0:T(8,128)(2,1)S(1)}, u32[]{:S(2)}) copy-start(bf16[416,1024]{1,0:T(8,128)(2,1)S(1)} %collective-permute-done.6.refs_7_.refs_15_) | copy-start | bytes 2555908
  107.4 23.9 %copy-start.4 = (bf16[416,1024]{1,0:T(8,128)(2,1)}, bf16[416,1024]{1,0:T(8,128)(2,1)S(1)}, u32[]{:S(2)}) copy-start(bf16[416,1024]{1,0:T(8,128)(2,1)S(1)} %collective-permute-done.5.refs_5_.refs_13_) | copy-start | bytes 2555908
  107.4 23.8 %collective-permute-start.7 = (bf16[416,1024]{1,0:T(8,128)(2,1)S(1)}, bf16[416,1024]{1,0:T(8,128)(2,1)S(1)}, u32[]{:S(2)}, u32[]{:S(2)}) collective-permute-start(bf16[416,1024]{1,0:T(8,128)(2,1)S(1)} %collective-permute-done.5.refs_5_.refs_13_), channel_id=1, source_target_pairs={{0,3},{1,2},{2,1},{3,0},{4,7},{5,6},{6,5},{7,4},{8,11},{9,10},{10,... | collective-permute-start | bytes 2555912 | tf_op jit(solution)/shard_map/ppermute | solution.py:404
  110.0 21.2 %collective-permute-start.8 = (bf16[416,1024]{1,0:T(8,128)(2,1)S(1)}, bf16[416,1024]{1,0:T(8,128)(2,1)S(1)}, u32[]{:S(2)}, u32[]{:S(2)}) collective-permute-start(bf16[416,1024]{1,0:T(8,128)(2,1)S(1)} %collective-permute-done.2.refs_3_.refs_11_), channel_id=1, source_target_pairs={{0,1},{1,0},{2,3},{3,2},{4,5},{5,4},{6,7},{7,6},{8,9},{9,8},{10,11... | collective-permute-start | bytes 2555912 | tf_op jit(solution)/shard_map/ppermute | solution.py:404
  131.3 0.9 copy-start.5
  132.2 0.9 copy-start.6
  133.1 24.6 %collective-permute-start.10 = (bf16[1344,128]{1,0:T(8,128)(2,1)}, bf16[1344,128]{1,0:T(8,128)(2,1)}, u32[]{:S(2)}, u32[]{:S(2)}) collective-permute-start(bf16[1344,128]{1,0:T(8,128)(2,1)} %get-tuple-element.53), channel_id=1, source_target_pairs={{0,2},{1,3},{2,0},{3,1},{4,6},{5,7},{6,4},{7,5},{8,10},{9,11},{10,... | collective-permute-start | bytes 1032200 | tf_op jit(solution)/shard_map/ppermute | solution.py:404
  137.7 21.6 %collective-permute-start.13 = (bf16[1344,128]{1,0:T(8,128)(2,1)}, bf16[1344,128]{1,0:T(8,128)(2,1)}, u32[]{:S(2)}, u32[]{:S(2)}) collective-permute-start(bf16[1344,128]{1,0:T(8,128)(2,1)} %get-tuple-element.58), channel_id=1, source_target_pairs={{0,3},{1,2},{2,1},{3,0},{4,7},{5,6},{6,5},{7,4},{8,11},{9,10},{10,... | collective-permute-start | bytes 1032200 | tf_op jit(solution)/shard_map/ppermute | solution.py:404
  142.2 17.1 %collective-permute-start.12 = (bf16[1344,128]{1,0:T(8,128)(2,1)S(1)}, bf16[1344,128]{1,0:T(8,128)(2,1)}, u32[]{:S(2)}, u32[]{:S(2)}) collective-permute-start(bf16[1344,128]{1,0:T(8,128)(2,1)S(1)} %get-tuple-element.59), channel_id=1, source_target_pairs={{0,2},{1,3},{2,0},{3,1},{4,6},{5,7},{6,4},{7,5},{8,10},{9,11},{10,... | collective-permute-start | bytes 1032200 | tf_op jit(solution)/shard_map/ppermute | solution.py:404
  144.1 15.2 %collective-permute-start.11 = (bf16[1344,128]{1,0:T(8,128)(2,1)S(1)}, bf16[1344,128]{1,0:T(8,128)(2,1)}, u32[]{:S(2)}, u32[]{:S(2)}) collective-permute-start(bf16[1344,128]{1,0:T(8,128)(2,1)S(1)} %get-tuple-element.60), channel_id=1, source_target_pairs={{0,1},{1,0},{2,3},{3,2},{4,5},{5,4},{6,7},{7,6},{8,9},{9,8},{10,11... | collective-permute-start | bytes 1032200 | tf_op jit(solution)/shard_map/ppermute | solution.py:404
  181.8 12.2 %all-to-all-start.2 = ((bf16[8,32,512]{2,1,0:T(8,128)(2,1)}), bf16[8,32,512]{2,1,0:T(8,128)(2,1)S(1)}, u32[]{:S(2)}, u32[]{:S(2)}) async-start(bf16[8,32,512]{2,1,0:T(8,128)(2,1)} %bitcast.12), calls=%async_computation.2 | async-start | bytes 524288 | tf_op jit(solution)/shard_map/all_to_all | solution.py:430

commit v5 on v4

--- a/solution.py
+++ b/solution.py
@@ -167,7 +167,7 @@
                 ).astype(jnp.bfloat16)
             return carry
 
-        lax.fori_loop(0, experts // group, step, 0, unroll=4 if experts // group % 4 == 0 else 1)
+        lax.fori_loop(0, experts // group, step, 0, unroll=True)
 
     return body
 

time: 196 us -> 195 us (level)
  no operation moved by 1% of the time
where the time goes in v5:
time: 195 us; the launch traced here: 194 us
  waiting for transfers between devices  87.2 us (45%)
  starting transfers between devices  70.2 us (36%)
  Pallas kernels  30.4 us (16%)
  local copies, waits for them, and re-layouts  3.59 us (2%)
  other arithmetic  2.01 us (1%)
    ppermute x14, waiting for transfers between devices, send(): return lax.ppermute(value, 'dp', [(i, i ^ r) for i in range(replicas)])  54.5 us
    ppermute x14, starting transfers between devices, send(): return lax.ppermute(value, 'dp', [(i, i ^ r) for i in range(replicas)])  43.4 us
    all_to_all x3, waiting for transfers between devices, swap(): value = lax.all_to_all(value, axis, split_axis=0, concat_axis=0, tiled=True)  32.7 us
    pallas_call x6, Pallas kernels, call(): pl.pallas_call(body, out_shape=shapes[0] if single else tuple(shapes), in...  30.4 us
    all_to_all x3, starting transfers between devices, swap(): value = lax.all_to_all(value, axis, split_axis=0, concat_axis=0, tiled=True)  26.8 us
  transfers between devices with their start and end apart: 17, of which 8 were waited for; matrix products, arithmetic and copies ran while one was open for 2% of the time, Pallas kernels for 7%

profile of v5, /device:TPU:8, one launch (start us, length us, event | category | flops | bytes accessed | tf_op | source)
XLA Modules:
  0.0 194.4 jit_solution(17267266793396309752)
XLA Ops:
  0.6 2.3 %shard_map.104 = bf16[3648,128]{1,0:T(8,128)(2,1)} custom-call(s32[2,128]{1,0:T(2,128)} %bitcast.24, f32[2,128]{1,0:T(2,128)} %bitcast.25, bf16[128,3584]{1,0:T(8,128)(2,1)} %grad_ref.1), custom_call_target="tpu_custom_call" | custom-call | tf_op jit(solution)/shard_map/pallas_call | solution.py:393
  3.0 6.0 %all-to-all-start = ((bf16[8,456,128]{2,1,0:T(8,128)(2,1)}), bf16[8,456,128]{2,1,0:T(8,128)(2,1)S(1)}, u32[]{:S(2)}, u32[]{:S(2)}) async-start(bf16[8,456,128]{2,1,0:T(8,128)(2,1)} %bitcast.3), calls=%async_computation | async-start | bytes 1867776 | tf_op jit(solution)/shard_map/all_to_all | solution.py:430
  9.0 0.0 copy-start.8
  9.0 0.0 copy-start.11
  9.0 4.0 %shard_map.105 = (bf16[1344,128]{1,0:T(8,128)(2,1)}, bf16[1344,128]{1,0:T(8,128)(2,1)}, bf16[1344,128]{1,0:T(8,128)(2,1)}, bf16[1344,128]{1,0:T(8,128)(2,1)}, bf16[5376,128]{1,0:T(8,128)(2,1)}) custom-call(s32[1]{0:T(128)} %bitcast.own_ref, bf16[128,3584]{1,0:T(8,128)(2,1)} %bitcast.18, bf16[128,3584]{1,0:T(8,128)(2,1)} %bitcast.19, bf16[128,3584]{1,0:T(8,128)(2,1)} %bitcast.20), custom_call_target="tpu_custom_call" | custom-call | tf_op jit(solution)/shard_map/pallas_call | solution.py:393
  13.0 0.0 copy-done.8
  13.0 0.0 copy-done.11
  13.0 1.0 pad_maximum_fusion.refs_0_.refs_8_
  14.0 11.0 %all-to-all-done = bf16[8,456,128]{2,1,0:T(8,128)(2,1)S(1)} async-done(((bf16[8,456,128]{2,1,0:T(8,128)(2,1)}), bf16[8,456,128]{2,1,0:T(8,128)(2,1)S(1)}, u32[]{:S(2)}, u32[]{:S(2)}) %all-to-all-start) | async-done | bytes 933920 | tf_op jit(solution)/shard_map/all_to_all | solution.py:430
  25.0 5.0 %shard_map.106 = bf16[10752,128]{1,0:T(8,128)(2,1)} custom-call(bf16[3648,128]{1,0:T(8,128)(2,1)S(1)} %bitcast.16), custom_call_target="tpu_custom_call" | custom-call | tf_op jit(solution)/shard_map/pallas_call | solution.py:393
  30.0 0.0 copy-start.13
  30.0 17.3 %all-to-all-start.1 = ((bf16[64,168,128]{2,1,0:T(8,128)(2,1)}), bf16[64,168,128]{2,1,0:T(8,128)(2,1)S(1)}, u32[]{:S(2)}, u32[]{:S(2)}) async-start(bf16[64,168,128]{2,1,0:T(8,128)(2,1)} %bitcast.10), calls=%async_computation.1 | async-start | bytes 5505024 | tf_op jit(solution)/shard_map/all_to_all | solution.py:430
  47.4 0.0 copy-start.7
  47.4 2.6 %collective-permute-start.2 = (bf16[416,1024]{1,0:T(8,128)(2,1)}, bf16[416,1024]{1,0:T(8,128)(2,1)S(1)}, u32[]{:S(2)}, u32[]{:S(2)}) collective-permute-start(bf16[416,1024]{1,0:T(8,128)(2,1)} %pad_maximum_fusion.refs_0_.refs_8_), channel_id=1, source_target_pairs={{0,3},{1,2},{2,1},{3,0},{4,7},{5,6},{6,5},{7,4},{8,11},{9,10},{10,... | collective-permute-start | bytes 2555912 | tf_op jit(solution)/shard_map/ppermute | solution.py:404
  50.0 2.2 %collective-permute-start.1 = (bf16[416,1024]{1,0:T(8,128)(2,1)}, bf16[416,1024]{1,0:T(8,128)(2,1)S(1)}, u32[]{:S(2)}, u32[]{:S(2)}) collective-permute-start(bf16[416,1024]{1,0:T(8,128)(2,1)} %pad_maximum_fusion.refs_0_.refs_8_), channel_id=1, source_target_pairs={{0,1},{1,0},{2,3},{3,2},{4,5},{5,4},{6,7},{7,6},{8,9},{9,8},{10,11... | collective-permute-start | bytes 2555912 | tf_op jit(solution)/shard_map/ppermute | solution.py:404
  52.2 3.1 %collective-permute-start = (bf16[416,1024]{1,0:T(8,128)(2,1)}, bf16[416,1024]{1,0:T(8,128)(2,1)S(1)}, u32[]{:S(2)}, u32[]{:S(2)}) collective-permute-start(bf16[416,1024]{1,0:T(8,128)(2,1)} %pad_maximum_fusion.refs_0_.refs_8_), channel_id=1, source_target_pairs={{0,4},{1,5},{2,6},{3,7},{4,0},{5,1},{6,2},{7,3},{8,12},{9,13},{10,... | collective-permute-start | bytes 2555912 | tf_op jit(solution)/shard_map/ppermute | solution.py:404
  55.3 0.0 copy-done.13
  55.3 3.9 %collective-permute-start.3 = (bf16[1344,128]{1,0:T(8,128)(2,1)S(1)}, bf16[1344,128]{1,0:T(8,128)(2,1)S(1)}, u32[]{:S(2)}, u32[]{:S(2)}) collective-permute-start(bf16[1344,128]{1,0:T(8,128)(2,1)S(1)} %copy-done.13), channel_id=1, source_target_pairs={{0,1},{1,0},{2,3},{3,2},{4,5},{5,4},{6,7},{7,6},{8,9},{9,8},{10,11... | collective-permute-start | bytes 1032200 | tf_op jit(solution)/shard_map/ppermute | solution.py:404
  59.2 0.0 copy-done.12
  59.2 3.7 %collective-permute-start.4 = (bf16[1344,128]{1,0:T(8,128)(2,1)S(1)}, bf16[1344,128]{1,0:T(8,128)(2,1)S(1)}, u32[]{:S(2)}, u32[]{:S(2)}) collective-permute-start(bf16[1344,128]{1,0:T(8,128)(2,1)S(1)} %copy-done.12), channel_id=1, source_target_pairs={{0,3},{1,2},{2,1},{3,0},{4,7},{5,6},{6,5},{7,4},{8,11},{9,10},{10,... | collective-permute-start | bytes 1032200 | tf_op jit(solution)/shard_map/ppermute | solution.py:404
  62.9 17.3 %collective-permute-done.3.refs_1_ = bf16[1344,128]{1,0:T(8,128)(2,1)S(1)} collective-permute-done((bf16[1344,128]{1,0:T(8,128)(2,1)S(1)}, bf16[1344,128]{1,0:T(8,128)(2,1)S(1)}, u32[]{:S(2)}, u32[]{:S(2)}) %collective-permute-start.3) | collective-permute-done | bytes 344096 | tf_op jit(solution)/shard_map/ppermute | solution.py:404
  80.2 0.0 collective-permute-done.4.refs_3_
  80.2 0.0 collective-permute-done.2.refs_3_.refs_11_
  80.2 0.0 copy-start
  80.2 0.0 collective-permute-done.1.refs_1_.refs_9_
  80.2 0.7 copy-done.9
  80.9 0.1 copy-done.10
  81.0 0.0 collective-permute-done.refs_4_.refs_12_
  81.0 4.6 %collective-permute-start.6 = (bf16[416,1024]{1,0:T(8,128)(2,1)S(1)}, bf16[416,1024]{1,0:T(8,128)(2,1)S(1)}, u32[]{:S(2)}, u32[]{:S(2)}) collective-permute-start(bf16[416,1024]{1,0:T(8,128)(2,1)S(1)} %collective-permute-done.refs_4_.refs_12_), channel_id=1, source_target_pairs={{0,3},{1,2},{2,1},{3,0},{4,7},{5,6},{6,5},{7,4},{8,11},{9,10},{10,... | collective-permute-start | bytes 2555912 | tf_op jit(solution)/shard_map/ppermute | solution.py:404
  85.6 1.9 collective-permute-start.5
  87.6 3.1 %collective-permute-start.9 = (bf16[5376,128]{1,0:T(8,128)(2,1)}, bf16[5376,128]{1,0:T(8,128)(2,1)S(1)}, u32[]{:S(2)}, u32[]{:S(2)}) collective-permute-start(bf16[5376,128]{1,0:T(8,128)(2,1)} %get-tuple-element.46), channel_id=1, source_target_pairs={{0,4},{1,5},{2,6},{3,7},{4,0},{5,1},{6,2},{7,3},{8,12},{9,13},{10,... | collective-permute-start | bytes 4128776 | tf_op jit(solution)/shard_map/ppermute | solution.py:404
  90.7 13.4 %collective-permute-done.6.refs_7_.refs_15_ = bf16[416,1024]{1,0:T(8,128)(2,1)S(1)} collective-permute-done((bf16[416,1024]{1,0:T(8,128)(2,1)S(1)}, bf16[416,1024]{1,0:T(8,128)(2,1)S(1)}, u32[]{:S(2)}, u32[]{:S(2)}) %collective-permute-start.6) | collective-permute-done | bytes 852000 | tf_op jit(solution)/shard_map/ppermute | solution.py:404
  104.1 3.0 %collective-permute-done.5.refs_5_.refs_13_ = bf16[416,1024]{1,0:T(8,128)(2,1)S(1)} collective-permute-done((bf16[416,1024]{1,0:T(8,128)(2,1)S(1)}, bf16[416,1024]{1,0:T(8,128)(2,1)S(1)}, u32[]{:S(2)}, u32[]{:S(2)}) %collective-permute-start.5) | collective-permute-done | bytes 852000 | tf_op jit(solution)/shard_map/ppermute | solution.py:404
  107.1 2.6 %collective-permute-start.7 = (bf16[416,1024]{1,0:T(8,128)(2,1)S(1)}, bf16[416,1024]{1,0:T(8,128)(2,1)S(1)}, u32[]{:S(2)}, u32[]{:S(2)}) collective-permute-start(bf16[416,1024]{1,0:T(8,128)(2,1)S(1)} %collective-permute-done.5.refs_5_.refs_13_), channel_id=1, source_target_pairs={{0,3},{1,2},{2,1},{3,0},{4,7},{5,6},{6,5},{7,4},{8,11},{9,10},{10,... | collective-permute-start | bytes 2555912 | tf_op jit(solution)/shard_map/ppermute | solution.py:404
  109.7 0.0 copy-done
  109.7 2.0 %collective-permute-start.8 = (bf16[416,1024]{1,0:T(8,128)(2,1)S(1)}, bf16[416,1024]{1,0:T(8,128)(2,1)S(1)}, u32[]{:S(2)}, u32[]{:S(2)}) collective-permute-start(bf16[416,1024]{1,0:T(8,128)(2,1)S(1)} %collective-permute-done.2.refs_3_.refs_11_), channel_id=1, source_target_pairs={{0,1},{1,0},{2,3},{3,2},{4,5},{5,4},{6,7},{7,6},{8,9},{9,8},{10,11... | collective-permute-start | bytes 2555912 | tf_op jit(solution)/shard_map/ppermute | solution.py:404
  111.7 19.2 %collective-permute-done.9 = bf16[5376,128]{1,0:T(8,128)(2,1)S(1)} collective-permute-done((bf16[5376,128]{1,0:T(8,128)(2,1)}, bf16[5376,128]{1,0:T(8,128)(2,1)S(1)}, u32[]{:S(2)}, u32[]{:S(2)}) %collective-permute-start.9) | collective-permute-done | bytes 1376288 | tf_op jit(solution)/shard_map/ppermute | solution.py:404
  130.9 0.0 collective-permute-done.7.refs_6_.refs_14_
  130.9 0.0 collective-permute-done.8.refs_2_.refs_10_
  130.9 0.0 copy-done.1
  130.9 0.0 copy-done.2
  131.0 0.0 copy-done.3
  131.0 0.0 copy-done.4
  131.0 0.9 copy-done.5
  131.8 0.9 copy-done.6
  132.7 3.7 %collective-permute-start.10 = (bf16[1344,128]{1,0:T(8,128)(2,1)}, bf16[1344,128]{1,0:T(8,128)(2,1)}, u32[]{:S(2)}, u32[]{:S(2)}) collective-permute-start(bf16[1344,128]{1,0:T(8,128)(2,1)} %get-tuple-element.53), channel_id=1, source_target_pairs={{0,2},{1,3},{2,0},{3,1},{4,6},{5,7},{6,4},{7,5},{8,10},{9,11},{10,... | collective-permute-start | bytes 1032200 | tf_op jit(solution)/shard_map/ppermute | solution.py:404
  136.4 1.0 fusion.5
  137.4 4.5 %collective-permute-start.13 = (bf16[1344,128]{1,0:T(8,128)(2,1)}, bf16[1344,128]{1,0:T(8,128)(2,1)}, u32[]{:S(2)}, u32[]{:S(2)}) collective-permute-start(bf16[1344,128]{1,0:T(8,128)(2,1)} %get-tuple-element.58), channel_id=1, source_target_pairs={{0,3},{1,2},{2,1},{3,0},{4,7},{5,6},{6,5},{7,4},{8,11},{9,10},{10,... | collective-permute-start | bytes 1032200 | tf_op jit(solution)/shard_map/ppermute | solution.py:404
  141.9 1.9 collective-permute-start.12
  143.8 3.6 %collective-permute-start.11 = (bf16[1344,128]{1,0:T(8,128)(2,1)S(1)}, bf16[1344,128]{1,0:T(8,128)(2,1)}, u32[]{:S(2)}, u32[]{:S(2)}) collective-permute-start(bf16[1344,128]{1,0:T(8,128)(2,1)S(1)} %get-tuple-element.60), channel_id=1, source_target_pairs={{0,1},{1,0},{2,3},{3,2},{4,5},{5,4},{6,7},{7,6},{8,9},{9,8},{10,11... | collective-permute-start | bytes 1032200 | tf_op jit(solution)/shard_map/ppermute | solution.py:404
  147.4 0.0 copy-done.7
  147.4 0.1 reduce_max.14
  147.6 0.2 fusion.1
  147.7 9.6 %shard_map.107.hidden_ref = bf16[4,1024,768]{2,1,0:T(8,128)(2,1)} custom-call(s32[1]{0:T(128)} %bitcast.own_ref, bf16[416,1024]{1,0:T(8,128)(2,1)} %pad_maximum_fusion.refs_0_.refs_8_, bf16[416,1024]{1,0:T(8,128)(2,1)} %copy-done.1, bf16[416,1024]{1,0:T(8,128)(2,1)} %copy-done.6, bf16[416,1024]{1,0:T(8,128)(2,1)} %copy-done, bf16[416,1024]{1,0:T(8,128)(2,1)} %copy-done.2, ...), custom_call_target="tpu_custom_call" | custom-call | tf_op jit(solution)/shard_map/pallas_call | solution.py:393
  157.4 0.0 collective-permute-done.10.refs_2_
  157.4 1.6 collective-permute-done.13.refs_7_
  159.0 0.0 collective-permute-done.12.refs_6_
  159.0 0.0 collective-permute-done.11.refs_5_
  159.0 13.8 %all-to-all-done.1 = bf16[64,168,128]{2,1,0:T(8,128)(2,1)S(1)} async-done(((bf16[64,168,128]{2,1,0:T(8,128)(2,1)}), bf16[64,168,128]{2,1,0:T(8,128)(2,1)S(1)}, u32[]{:S(2)}, u32[]{:S(2)}) %all-to-all-start.1) | async-done | bytes 2752544 | tf_op jit(solution)/shard_map/all_to_all | solution.py:430
  172.7 8.7 %shard_map.108 = bf16[256,512]{1,0:T(8,128)(2,1)} custom-call(s32[1]{0:T(128)} %bitcast.own_ref, bf16[10752,128]{1,0:T(8,128)(2,1)S(1)} %bitcast.15, bf16[4,1024,768]{2,1,0:T(8,128)(2,1)} %shard_map.107.hidden_ref, bf16[1344,128]{1,0:T(8,128)(2,1)} %get-tuple-element.51.refs_0_, bf16[1344,128]{1,0:T(8,128)(2,1)} %copy-done.9, ...), custom_call_target="tpu_custom_call" | custom-call | tf_op jit(solution)/shard_map/pallas_call | solution.py:393
  181.4 3.4 %all-to-all-start.2 = ((bf16[8,32,512]{2,1,0:T(8,128)(2,1)}), bf16[8,32,512]{2,1,0:T(8,128)(2,1)S(1)}, u32[]{:S(2)}, u32[]{:S(2)}) async-start(bf16[8,32,512]{2,1,0:T(8,128)(2,1)} %bitcast.12), calls=%async_computation.2 | async-start | bytes 524288 | tf_op jit(solution)/shard_map/all_to_all | solution.py:430
  184.9 0.7 fusion.4
  185.6 8.0 %all-to-all-done.2 = bf16[8,32,512]{2,1,0:T(8,128)(2,1)S(1)} async-done(((bf16[8,32,512]{2,1,0:T(8,128)(2,1)}), bf16[8,32,512]{2,1,0:T(8,128)(2,1)S(1)}, u32[]{:S(2)}, u32[]{:S(2)}) %all-to-all-start.2) | async-done | bytes 262176 | tf_op jit(solution)/shard_map/all_to_all | solution.py:430
  193.6 0.8 shard_map.109
  (11 shorter events, 0.0 us)
Async XLA Ops:
  3.0 22.0 %all-to-all-start = ((bf16[8,456,128]{2,1,0:T(8,128)(2,1)}), bf16[8,456,128]{2,1,0:T(8,128)(2,1)S(1)}, u32[]{:S(2)}, u32[]{:S(2)}) async-start(bf16[8,456,128]{2,1,0:T(8,128)(2,1)} %bitcast.3), calls=%async_computation | async-start | bytes 1867776 | tf_op jit(solution)/shard_map/all_to_all | solution.py:430
  9.0 4.0 %copy-start.8 = (bf16[1,384,1024]{2,1,0:T(8,128)(2,1)S(1)}, bf16[1,384,1024]{2,1,0:T(8,128)(2,1)}, u32[]{:S(2)}) copy-start(bf16[1,384,1024]{2,1,0:T(8,128)(2,1)} %param.13) | copy-start | bytes 2359300
  9.0 4.0 %copy-start.11 = (bf16[1,32,1024]{2,1,0:T(8,128)(2,1)S(1)}, bf16[1,32,1024]{2,1,0:T(8,128)(2,1)}, u32[]{:S(2)}) copy-start(bf16[1,32,1024]{2,1,0:T(8,128)(2,1)} %param.17) | copy-start | bytes 196612
  30.0 25.3 %copy-start.13 = (bf16[1344,128]{1,0:T(8,128)(2,1)S(1)}, bf16[1344,128]{1,0:T(8,128)(2,1)}, u32[]{:S(2)}) copy-start(bf16[1344,128]{1,0:T(8,128)(2,1)} %get-tuple-element.36) | copy-start | bytes 1032196
  30.0 29.2 %copy-start.12 = (bf16[1344,128]{1,0:T(8,128)(2,1)S(1)}, bf16[1344,128]{1,0:T(8,128)(2,1)}, u32[]{:S(2)}) copy-start(bf16[1344,128]{1,0:T(8,128)(2,1)} %get-tuple-element.37) | copy-start | bytes 1032196
  30.0 142.7 %all-to-all-start.1 = ((bf16[64,168,128]{2,1,0:T(8,128)(2,1)}), bf16[64,168,128]{2,1,0:T(8,128)(2,1)S(1)}, u32[]{:S(2)}, u32[]{:S(2)}) async-start(bf16[64,168,128]{2,1,0:T(8,128)(2,1)} %bitcast.10), calls=%async_computation.1 | async-start | bytes 5505024 | tf_op jit(solution)/shard_map/all_to_all | solution.py:430
  47.4 100.1 %copy-start.7 = (bf16[128,384]{1,0:T(8,128)(2,1)S(1)}, bf16[128,384]{1,0:T(8,128)(2,1)}, u32[]{:S(2)}) copy-start(bf16[128,384]{1,0:T(8,128)(2,1)} %param.12) | copy-start | bytes 294916
  47.4 32.8 %collective-permute-start.2 = (bf16[416,1024]{1,0:T(8,128)(2,1)}, bf16[416,1024]{1,0:T(8,128)(2,1)S(1)}, u32[]{:S(2)}, u32[]{:S(2)}) collective-permute-start(bf16[416,1024]{1,0:T(8,128)(2,1)} %pad_maximum_fusion.refs_0_.refs_8_), channel_id=1, source_target_pairs={{0,3},{1,2},{2,1},{3,0},{4,7},{5,6},{6,5},{7,4},{8,11},{9,10},{10,... | collective-permute-start | bytes 2555912 | tf_op jit(solution)/shard_map/ppermute | solution.py:404
  50.0 30.2 %collective-permute-start.1 = (bf16[416,1024]{1,0:T(8,128)(2,1)}, bf16[416,1024]{1,0:T(8,128)(2,1)S(1)}, u32[]{:S(2)}, u32[]{:S(2)}) collective-permute-start(bf16[416,1024]{1,0:T(8,128)(2,1)} %pad_maximum_fusion.refs_0_.refs_8_), channel_id=1, source_target_pairs={{0,1},{1,0},{2,3},{3,2},{4,5},{5,4},{6,7},{7,6},{8,9},{9,8},{10,11... | collective-permute-start | bytes 2555912 | tf_op jit(solution)/shard_map/ppermute | solution.py:404
  52.2 28.8 %collective-permute-start = (bf16[416,1024]{1,0:T(8,128)(2,1)}, bf16[416,1024]{1,0:T(8,128)(2,1)S(1)}, u32[]{:S(2)}, u32[]{:S(2)}) collective-permute-start(bf16[416,1024]{1,0:T(8,128)(2,1)} %pad_maximum_fusion.refs_0_.refs_8_), channel_id=1, source_target_pairs={{0,4},{1,5},{2,6},{3,7},{4,0},{5,1},{6,2},{7,3},{8,12},{9,13},{10,... | collective-permute-start | bytes 2555912 | tf_op jit(solution)/shard_map/ppermute | solution.py:404
  55.3 24.9 %collective-permute-start.3 = (bf16[1344,128]{1,0:T(8,128)(2,1)S(1)}, bf16[1344,128]{1,0:T(8,128)(2,1)S(1)}, u32[]{:S(2)}, u32[]{:S(2)}) collective-permute-start(bf16[1344,128]{1,0:T(8,128)(2,1)S(1)} %copy-done.13), channel_id=1, source_target_pairs={{0,1},{1,0},{2,3},{3,2},{4,5},{5,4},{6,7},{7,6},{8,9},{9,8},{10,11... | collective-permute-start | bytes 1032200 | tf_op jit(solution)/shard_map/ppermute | solution.py:404
  59.2 20.9 %collective-permute-start.4 = (bf16[1344,128]{1,0:T(8,128)(2,1)S(1)}, bf16[1344,128]{1,0:T(8,128)(2,1)S(1)}, u32[]{:S(2)}, u32[]{:S(2)}) collective-permute-start(bf16[1344,128]{1,0:T(8,128)(2,1)S(1)} %copy-done.12), channel_id=1, source_target_pairs={{0,3},{1,2},{2,1},{3,0},{4,7},{5,6},{6,5},{7,4},{8,11},{9,10},{10,... | collective-permute-start | bytes 1032200 | tf_op jit(solution)/shard_map/ppermute | solution.py:404
  80.2 0.7 copy-start.9
  80.2 0.9 copy-start.10
  80.2 29.5 %copy-start = (bf16[416,1024]{1,0:T(8,128)(2,1)}, bf16[416,1024]{1,0:T(8,128)(2,1)S(1)}, u32[]{:S(2)}) copy-start(bf16[416,1024]{1,0:T(8,128)(2,1)S(1)} %collective-permute-done.2.refs_3_.refs_11_) | copy-start | bytes 2555908
  81.0 49.9 %copy-start.1 = (bf16[416,1024]{1,0:T(8,128)(2,1)}, bf16[416,1024]{1,0:T(8,128)(2,1)S(1)}, u32[]{:S(2)}) copy-start(bf16[416,1024]{1,0:T(8,128)(2,1)S(1)} %collective-permute-done.1.refs_1_.refs_9_) | copy-start | bytes 2555908
  81.0 49.9 %copy-start.2 = (bf16[416,1024]{1,0:T(8,128)(2,1)}, bf16[416,1024]{1,0:T(8,128)(2,1)S(1)}, u32[]{:S(2)}) copy-start(bf16[416,1024]{1,0:T(8,128)(2,1)S(1)} %collective-permute-done.refs_4_.refs_12_) | copy-start | bytes 2555908
  81.0 23.1 %collective-permute-start.6 = (bf16[416,1024]{1,0:T(8,128)(2,1)S(1)}, bf16[416,1024]{1,0:T(8,128)(2,1)S(1)}, u32[]{:S(2)}, u32[]{:S(2)}) collective-permute-start(bf16[416,1024]{1,0:T(8,128)(2,1)S(1)} %collective-permute-done.refs_4_.refs_12_), channel_id=1, source_target_pairs={{0,3},{1,2},{2,1},{3,0},{4,7},{5,6},{6,5},{7,4},{8,11},{9,10},{10,... | collective-permute-start | bytes 2555912 | tf_op jit(solution)/shard_map/ppermute | solution.py:404
  85.6 21.5 %collective-permute-start.5 = (bf16[416,1024]{1,0:T(8,128)(2,1)S(1)}, bf16[416,1024]{1,0:T(8,128)(2,1)S(1)}, u32[]{:S(2)}, u32[]{:S(2)}) collective-permute-start(bf16[416,1024]{1,0:T(8,128)(2,1)S(1)} %collective-permute-done.refs_4_.refs_12_), channel_id=1, source_target_pairs={{0,1},{1,0},{2,3},{3,2},{4,5},{5,4},{6,7},{7,6},{8,9},{9,8},{10,11... | collective-permute-start | bytes 2555912 | tf_op jit(solution)/shard_map/ppermute | solution.py:404
  87.6 43.4 %collective-permute-start.9 = (bf16[5376,128]{1,0:T(8,128)(2,1)}, bf16[5376,128]{1,0:T(8,128)(2,1)S(1)}, u32[]{:S(2)}, u32[]{:S(2)}) collective-permute-start(bf16[5376,128]{1,0:T(8,128)(2,1)} %get-tuple-element.46), channel_id=1, source_target_pairs={{0,4},{1,5},{2,6},{3,7},{4,0},{5,1},{6,2},{7,3},{8,12},{9,13},{10,... | collective-permute-start | bytes 4128776 | tf_op jit(solution)/shard_map/ppermute | solution.py:404
  104.1 26.8 %copy-start.3 = (bf16[416,1024]{1,0:T(8,128)(2,1)}, bf16[416,1024]{1,0:T(8,128)(2,1)S(1)}, u32[]{:S(2)}) copy-start(bf16[416,1024]{1,0:T(8,128)(2,1)S(1)} %collective-permute-done.6.refs_7_.refs_15_) | copy-start | bytes 2555908
  107.1 23.9 %copy-start.4 = (bf16[416,1024]{1,0:T(8,128)(2,1)}, bf16[416,1024]{1,0:T(8,128)(2,1)S(1)}, u32[]{:S(2)}) copy-start(bf16[416,1024]{1,0:T(8,128)(2,1)S(1)} %collective-permute-done.5.refs_5_.refs_13_) | copy-start | bytes 2555908
  107.1 23.8 %collective-permute-start.7 = (bf16[416,1024]{1,0:T(8,128)(2,1)S(1)}, bf16[416,1024]{1,0:T(8,128)(2,1)S(1)}, u32[]{:S(2)}, u32[]{:S(2)}) collective-permute-start(bf16[416,1024]{1,0:T(8,128)(2,1)S(1)} %collective-permute-done.5.refs_5_.refs_13_), channel_id=1, source_target_pairs={{0,3},{1,2},{2,1},{3,0},{4,7},{5,6},{6,5},{7,4},{8,11},{9,10},{10,... | collective-permute-start | bytes 2555912 | tf_op jit(solution)/shard_map/ppermute | solution.py:404
  109.7 21.2 %collective-permute-start.8 = (bf16[416,1024]{1,0:T(8,128)(2,1)S(1)}, bf16[416,1024]{1,0:T(8,128)(2,1)S(1)}, u32[]{:S(2)}, u32[]{:S(2)}) collective-permute-start(bf16[416,1024]{1,0:T(8,128)(2,1)S(1)} %collective-permute-done.2.refs_3_.refs_11_), channel_id=1, source_target_pairs={{0,1},{1,0},{2,3},{3,2},{4,5},{5,4},{6,7},{7,6},{8,9},{9,8},{10,11... | collective-permute-start | bytes 2555912 | tf_op jit(solution)/shard_map/ppermute | solution.py:404
  130.9 0.9 copy-start.5
  131.8 0.9 copy-start.6
  132.7 24.6 %collective-permute-start.10 = (bf16[1344,128]{1,0:T(8,128)(2,1)}, bf16[1344,128]{1,0:T(8,128)(2,1)}, u32[]{:S(2)}, u32[]{:S(2)}) collective-permute-start(bf16[1344,128]{1,0:T(8,128)(2,1)} %get-tuple-element.53), channel_id=1, source_target_pairs={{0,2},{1,3},{2,0},{3,1},{4,6},{5,7},{6,4},{7,5},{8,10},{9,11},{10,... | collective-permute-start | bytes 1032200 | tf_op jit(solution)/shard_map/ppermute | solution.py:404
  137.4 21.6 %collective-permute-start.13 = (bf16[1344,128]{1,0:T(8,128)(2,1)}, bf16[1344,128]{1,0:T(8,128)(2,1)}, u32[]{:S(2)}, u32[]{:S(2)}) collective-permute-start(bf16[1344,128]{1,0:T(8,128)(2,1)} %get-tuple-element.58), channel_id=1, source_target_pairs={{0,3},{1,2},{2,1},{3,0},{4,7},{5,6},{6,5},{7,4},{8,11},{9,10},{10,... | collective-permute-start | bytes 1032200 | tf_op jit(solution)/shard_map/ppermute | solution.py:404
  141.9 17.1 %collective-permute-start.12 = (bf16[1344,128]{1,0:T(8,128)(2,1)S(1)}, bf16[1344,128]{1,0:T(8,128)(2,1)}, u32[]{:S(2)}, u32[]{:S(2)}) collective-permute-start(bf16[1344,128]{1,0:T(8,128)(2,1)S(1)} %get-tuple-element.59), channel_id=1, source_target_pairs={{0,2},{1,3},{2,0},{3,1},{4,6},{5,7},{6,4},{7,5},{8,10},{9,11},{10,... | collective-permute-start | bytes 1032200 | tf_op jit(solution)/shard_map/ppermute | solution.py:404
  143.8 15.2 %collective-permute-start.11 = (bf16[1344,128]{1,0:T(8,128)(2,1)S(1)}, bf16[1344,128]{1,0:T(8,128)(2,1)}, u32[]{:S(2)}, u32[]{:S(2)}) collective-permute-start(bf16[1344,128]{1,0:T(8,128)(2,1)S(1)} %get-tuple-element.60), channel_id=1, source_target_pairs={{0,1},{1,0},{2,3},{3,2},{4,5},{5,4},{6,7},{7,6},{8,9},{9,8},{10,11... | collective-permute-start | bytes 1032200 | tf_op jit(solution)/shard_map/ppermute | solution.py:404
  181.4 12.2 %all-to-all-start.2 = ((bf16[8,32,512]{2,1,0:T(8,128)(2,1)}), bf16[8,32,512]{2,1,0:T(8,128)(2,1)S(1)}, u32[]{:S(2)}, u32[]{:S(2)}) async-start(bf16[8,32,512]{2,1,0:T(8,128)(2,1)} %bitcast.12), calls=%async_computation.2 | async-start | bytes 524288 | tf_op jit(solution)/shard_map/all_to_all | solution.py:430
